TPU v7x, 256 devices: a whole 4x4x8 slice. The times are simulated.
256 devices in a mesh: grid: 16 (over y, x), day: 16 (over z, core).
Axes of the slice: x: 4, y: 4, z: 8, core: 2. Of those that a mesh axis runs over, the one named last changes fastest.
Arguments:
- anomalies: bfloat16 [16384, 65536], P('day', 'grid'), may hold values from -6 to 6
- eofs: bfloat16 [64, 65536], P(None, ('grid', 'day')), may hold values from -0.0234375 to 0.0234375
- means_init: float32 [8, 64], replicated, may hold values from -4 to 4
- variances: float32 [8, 64], replicated, may hold values from 0.05 to 2
- mixing: float32 [8], replicated, may hold values from 0.5 to 2
Outputs:
- regime_means: float32 [8, 64], replicated
- regime_covs: float32 [8, 64, 64], replicated
- regime_weights: float32 [8], replicated
- membership: float32 [8, 16384], P(None, 'day')
- composites: bfloat16 [8, 65536], P(None, ('grid', 'day'))
All inputs are finite; a program needn't handle non-finite values.
Results may differ from a plain program's by a relative error of at most 0.0034.
Values may be sent and summed in bfloat16 or wider, within the bound.
No kernel may reach another device: no remote copies, remote signals or barrier semaphores. Data moves between devices by JAX's collectives and lax.ppermute only.
A program may use at most 64 MiB of HBM per device.

v0:
```python
import jax
import jax.numpy as jnp
from jax import lax
from jax.sharding import PartitionSpec as P

ITERS = 2


PRECISE = lax.Precision.HIGHEST
REG = 0.01


def log_density(pcs_t, means, covs, weights):
    regimes = means.shape[0]
    width = means.shape[1]
    eye = jnp.broadcast_to(jnp.eye(width, dtype=jnp.float32), (regimes, width, width))
    factor = jnp.linalg.cholesky(covs)
    inverse = lax.linalg.triangular_solve(factor, eye, left_side=True, lower=True)
    centred = pcs_t[None, :, :] - means[:, :, None]
    shifted = jnp.einsum("rkj,rjd->rkd", inverse, centred, precision=PRECISE)
    logdet = jnp.sum(jnp.log(jnp.diagonal(factor, axis1=1, axis2=2)), axis=1)
    return jnp.log(weights)[:, None] - logdet[:, None] - 0.5 * jnp.sum(shifted * shifted, axis=1)


def responsibilities(pcs_t, means, covs, weights):
    logp = log_density(pcs_t, means, covs, weights)
    top = jnp.max(logp, axis=0, keepdims=True)
    expo = jnp.exp(logp - top)
    return expo / jnp.sum(expo, axis=0, keepdims=True)


def second_moments(pcs_t, resp, means):
    diff = pcs_t[None, :, :] - means[:, :, None]
    return jnp.einsum("rkd,rjd->rkj", diff * resp[:, None, :], diff, precision=PRECISE)


def total_days(values):
    return lax.psum(values, "day")


def first_moments(pcs_t, resp):
    return lax.dot_general(resp, pcs_t, (((1,), (1,)), ((), ())), precision=PRECISE)


def update(pcs_t, resp, eye):
    counts, sums = total_days((jnp.sum(resp, axis=1), first_moments(pcs_t, resp)))
    counted = jnp.maximum(counts, 1.0)
    means = sums / counted[:, None]
    second = total_days(second_moments(pcs_t, resp, means))
    covs = second / counted[:, None, None] + REG * eye[None]
    weights = counted / jnp.sum(counted)
    return (means, covs, weights)


def body(anomalies, eofs, means_init, variances, mixing):
    width = eofs.shape[0]
    partial_pcs = lax.dot_general(
        anomalies,
        lax.all_gather(eofs, "day", axis=1, tiled=True),
        (((1,), (1,)), ((), ())),
        preferred_element_type=jnp.float32,
    )
    pcs = lax.psum(partial_pcs, "grid")
    pcs_t = pcs.T
    eye = jnp.eye(width, dtype=jnp.float32)
    means = means_init
    covs = variances[:, :, None] * eye[None]
    weights = mixing / jnp.sum(mixing)
    for step in range(ITERS):
        resp = responsibilities(pcs_t, means, covs, weights)
        means, covs, weights = update(pcs_t, resp, eye)
    member = responsibilities(pcs_t, means, covs, weights)
    counts = lax.psum(jnp.sum(member, axis=1), "day")
    counted = jnp.maximum(counts, 1.0)
    terms = jnp.dot(member.astype(jnp.bfloat16), anomalies, preferred_element_type=jnp.float32)
    sums = lax.psum_scatter(terms, "day", scatter_dimension=1, tiled=True)
    composites = (sums / counted[:, None]).astype(jnp.bfloat16)
    return (means, covs, weights, member, composites)


def solution(mesh):
    in_specs = (P("day", "grid"), P(None, ("grid", "day")), P(), P(), P())
    out_specs = (P(), P(), P(), P(None, "day"), P(None, ("grid", "day")))
    return jax.shard_map(body, mesh=mesh, in_specs=in_specs, out_specs=out_specs, check_vma=False)
```

profile of v0, /device:TPU:1, one launch (start us, length us, event | category | flops | bytes accessed | tf_op | source)
XLA Modules:
  0.0 665.7 jit_solution(10305190547740485479)
XLA Ops:
  7.2 23.0 %all_gather.3 = bf16[64,4096]{1,0:T(8,128)(2,1)S(1)} all-gather(bf16[64,256]{1,0:T(8,128)(2,1)} %param.9), channel_id=1, replica_groups=mesh['grid'=16,'day'=16] {'day'}, dimensions={1}, use_global_device_ids=true | all-gather | bytes 557056 | tf_op jit(solution)/shard_map/all_gather | solution.py:59
  30.2 6.8 %fusion.61 = f32[1024,64]{0,1:T(8,128)} fusion(bf16[1024,4096]{1,0:T(8,128)(2,1)} %param.8, bf16[64,4096]{1,0:T(8,128)(2,1)S(1)} %all_gather.3), kind=kOutput, calls=%fused_computation.101 | convolution fusion | flops 536870912 | bytes 9175040 | tf_op jit(solution)/shard_map/dot_general | solution.py:57
  37.3 46.9 %custom-call.16 = f32[8,64,64]{2,1,0:T(8,128)S(1)} custom-call(f32[8,64,64]{2,1,0:T(8,128)S(1)} %fusion.36), custom_call_target="Cholesky" | custom-call | tf_op jit(solution)/shard_map/jit(cholesky)/cholesky | solution.py:17
  85.2 0.9 gather_fusion
  87.3 39.3 %custom-call.17 = f32[8,1,64,64]{2,3,1,0:T(8,128)S(1)} custom-call(f32[8,1,64,64]{3,2,1,0:T(8,128)S(1)} %get-tuple-element.33), custom_call_target="InvertDiagBlocksLowerTriangular" | custom-call | tf_op jit(solution)/shard_map/triangular_solve/custom-call.0 | solution.py:18
  127.3 1.5 all-reduce.6.cloned.1.call-done
  128.8 3.0 multiply_reduce_fusion.2
  132.1 1.2 fusion.62
  133.3 26.5 %all-reduce.1 = (f32[8,64]{1,0:T(8,128)S(1)}, f32[8]{0:T(128)S(1)}) all-reduce(f32[8,64]{1,0:T(8,128)S(1)} %fusion.62, f32[8]{0:T(128)S(1)} %get-tuple-element.31), channel_id=1, replica_groups=mesh['grid'=16,'day'=16] {'day'}, use_global_device_ids=true, to_apply=%region_11.0 | all-reduce | flops 520 | bytes 4160 | tf_op jit(solution)/shard_map/psum | solution.py:38
  160.5 4.2 fusion.6
  164.9 107.4 %all-reduce.8.cloned.1.call-done = f32[8,64,64]{1,2,0:T(8,128)} async-done(((f32[8,64,64]{1,2,0:T(8,128)}), f32[8,64,64]{1,2,0:T(8,128)}) %all-reduce.8.cloned.1.call-update) | async-done | bytes 131088 | tf_op jit(solution)/shard_map/psum | solution.py:38
  272.3 1.0 divide_add_fusion.1
  273.5 1.1 fusion.33
  274.5 46.9 %custom-call.18 = f32[8,64,64]{2,1,0:T(8,128)S(1)} custom-call(f32[8,64,64]{2,1,0:T(8,128)S(1)} %fusion.33), custom_call_target="Cholesky" | custom-call | tf_op jit(solution)/shard_map/jit(cholesky)/cholesky | solution.py:17
  321.7 39.3 %custom-call.19 = f32[8,1,64,64]{2,3,1,0:T(8,128)S(1)} custom-call(f32[8,1,64,64]{3,2,1,0:T(8,128)S(1)} %get-tuple-element.29), custom_call_target="InvertDiagBlocksLowerTriangular" | custom-call | tf_op jit(solution)/shard_map/triangular_solve/custom-call.0 | solution.py:18
  361.7 2.0 multiply_reduce_fusion.1
  364.3 0.9 gather_fusion.1
  365.2 0.7 log_subtract_fusion.1
  366.6 24.0 %all-reduce = (f32[8,64]{1,0:T(8,128)S(1)}, f32[8]{0:T(128)S(1)}) all-reduce(f32[8,64]{1,0:T(8,128)S(1)} %fusion.63, f32[8]{0:T(128)S(1)} %get-tuple-element.27), channel_id=1, replica_groups=mesh['grid'=16,'day'=16] {'day'}, use_global_device_ids=true, to_apply=%region_17.0 | all-reduce | flops 520 | bytes 4160 | tf_op jit(solution)/shard_map/psum | solution.py:38
  391.3 3.1 fusion.2
  394.7 109.7 %all-reduce.10.cloned.1.call-done = f32[8,64,64]{1,2,0:T(8,128)} async-done(((f32[8,64,64]{1,2,0:T(8,128)}), f32[8,64,64]{1,2,0:T(8,128)}) %all-reduce.10.cloned.1.call-update) | async-done | bytes 131088 | tf_op jit(solution)/shard_map/psum | solution.py:38
  504.4 1.0 divide_add_fusion
  505.6 1.2 fusion.30
  506.8 46.9 %custom-call.20 = f32[8,64,64]{2,1,0:T(8,128)S(1)} custom-call(f32[8,64,64]{2,1,0:T(8,128)S(1)} %fusion.30), custom_call_target="Cholesky" | custom-call | tf_op jit(solution)/shard_map/jit(cholesky)/cholesky | solution.py:17
  553.9 39.3 %custom-call.21 = f32[8,1,64,64]{2,3,1,0:T(8,128)S(1)} custom-call(f32[8,1,64,64]{3,2,1,0:T(8,128)S(1)} %get-tuple-element.25), custom_call_target="InvertDiagBlocksLowerTriangular" | custom-call | tf_op jit(solution)/shard_map/triangular_solve/custom-call.0 | solution.py:18
  593.9 2.0 multiply_reduce_fusion
  596.6 0.9 gather_fusion.2
  597.5 1.2 log_subtract_fusion
  599.0 5.2 fusion.51
  604.3 23.5 %psum.63 = f32[8]{0:T(128)S(1)} all-reduce(f32[8]{0:T(128)S(1)} %get-tuple-element.21), channel_id=1, replica_groups=mesh['grid'=16,'day'=16] {'day'}, use_global_device_ids=true, to_apply=%region_28.31 | all-reduce | flops 8 | bytes 64 | tf_op jit(solution)/shard_map/psum | solution.py:73
  627.8 30.0 %reduce-scatter.2.cloned.1.call-done = f32[8,256]{1,0:T(8,128)} async-done(((f32[8,4096]{1,0:T(8,128)}), f32[8,256]{1,0:T(8,128)}) %reduce-scatter.2.cloned.1.call-update) | async-done | bytes 8208 | tf_op jit(solution)/shard_map/reduce_scatter | solution.py:76
  657.8 1.4 divide_convert_fusion
  (67 shorter events, 9.8 us)
Async XLA Ops:
  7.2 121.6 %all-reduce.6.cloned.1.call-start = ((), (), s32[]{:S(2)}) async-start(), calls=%async_computation.1 | async-start | bytes 524288 | tf_op jit(solution)/shard_map/psum | solution.py:63
  30.2 6.9 %copy-start.3 = (f32[8,64]{1,0:T(8,128)S(1)}, f32[8,64]{1,0:T(8,128)}, u32[]{:S(2)}) copy-start(f32[8,64]{1,0:T(8,128)} %param.11) | copy-start | bytes 6148
  37.0 235.3 %all-reduce.8.cloned.1.call-start = ((), (), s32[]{:S(2)}) async-start(), calls=%async_computation.2 | async-start | bytes 524288 | tf_op jit(solution)/shard_map/psum | solution.py:38
  37.3 48.8 %copy-start.5 = (f32[8]{0:T(128)S(1)}, f32[8]{0:T(128)}, u32[]{:S(2)}) copy-start(f32[8]{0:T(128)} %param.12) | copy-start | bytes 100
  37.3 91.4 %copy-start.6 = (f32[8,64]{1,0:T(8,128)S(1)}, f32[8,64]{1,0:T(8,128)}, u32[]{:S(2)}) copy-start(f32[8,64]{1,0:T(8,128)} %param.10) | copy-start | bytes 6148
  164.6 197.0 %copy-start = (f32[1024,64]{0,1:T(8,128)S(1)}, f32[1024,64]{0,1:T(8,128)}, u32[]{:S(2)}) copy-start(f32[1024,64]{0,1:T(8,128)} %all-reduce.6.cloned.1.call-done) | copy-start | bytes 786436
  164.7 339.7 %all-reduce.10.cloned.1.call-start = ((), (), s32[]{:S(2)}) async-start(), calls=%async_computation.3 | async-start | bytes 524288 | tf_op jit(solution)/shard_map/psum | solution.py:38
  391.3 202.6 %copy-start.4 = (f32[8,64]{1,0:T(8,128)}, f32[8,64]{1,0:T(8,128)S(1)}, u32[]{:S(2)}) copy-start(f32[8,64]{1,0:T(8,128)S(1)} %broadcast_divide_fusion) | copy-start | bytes 6148
  394.4 263.4 %reduce-scatter.2.cloned.1.call-start = ((), (), s32[]{:S(2)}) async-start(), calls=%async_computation.4 | async-start | bytes 139264 | tf_op jit(solution)/shard_map/reduce_scatter | solution.py:76
  505.6 91.0 %copy-start.1 = (f32[8,64,64]{2,1,0:T(8,128)}, f32[8,64,64]{2,1,0:T(8,128)S(1)}, u32[]{:S(2)}) copy-start(f32[8,64,64]{2,1,0:T(8,128)S(1)} %copy.27) | copy-start | bytes 393220
  599.0 5.3 copy-start.2
Sparse Core Ops, SparseCore 0:
  37.1 91.5 all-reduce.5
  164.8 107.4 all-reduce.7
  394.5 109.7 all-reduce.9
  604.4 53.3 reduce-scatter.1
where the time goes:
time: 668 us; the launch traced here: 666 us
  other arithmetic  271 us (41%)
  waiting for transfers between devices  249 us (37%)
  blocking collectives  97 us (15%)
  matrix products  29.6 us (4%)
  between operations  14.1 us (2%)
    psum x2, waiting for transfers between devices, total_days(): return lax.psum(values, 'day')  217 us
    another operation x10, other arithmetic, log_density(): factor = jnp.linalg.cholesky(covs)  141 us
    another operation x6, other arithmetic, log_density(): lax.linalg.triangular_solve(factor, eye, left_side=True, lower=True)  118 us
    psum x2, blocking collectives, total_days(): return lax.psum(values, 'day')  50.5 us
    reduce_scatter x1, waiting for transfers between devices, body(): sums = lax.psum_scatter(terms, 'day', scatter_dimension=1, tiled=True)  30 us
    psum x1, blocking collectives, body(): counts = lax.psum(jnp.sum(member, axis=1), 'day')  23.5 us
    all_gather x1, blocking collectives, body(): lax.all_gather(eofs, 'day', axis=1, tiled=True)  23 us
  transfers between devices with their start and end apart: 4, of which 4 were waited for; matrix products, arithmetic and copies ran while one was open for 14% of the time, Pallas kernels for 0%

commit v1 on v0

v1 whole, which is shorter than its diff:
```python
import jax
import jax.numpy as jnp
from jax import lax
from jax.experimental import pallas as pl
from jax.experimental.pallas import tpu as pltpu
from jax.sharding import Mesh, PartitionSpec as P

ITERS = 2
K = 64
PRECISE = lax.Precision.HIGHEST
REG = 0.01
SWAP = [(0, 1), (1, 0)]


def lanes_of(x, index):
    return jnp.take_along_axis(x, index, axis=1)


def eliminate(groups):
    lane = lax.broadcasted_iota(jnp.int32, (8, 128), 1)
    sub = lax.broadcasted_iota(jnp.int32, (8, 128), 0)
    half = (lane >= K).astype(jnp.int32) * K
    col = lane - half
    for k in range(K):
        g, s = divmod(k, 8)
        row = jnp.broadcast_to(groups[g][s:s + 1, :], (8, 128))
        at = half + k
        pivot = lanes_of(row, at)
        scaled = jnp.where(col == k, 1.0, row) / pivot
        for i in range(g, 8):
            if i == g and s == 7:
                continue
            factor = lanes_of(groups[i], at)
            new = jnp.where(col == k, 0.0, groups[i]) - factor * scaled
            groups[i] = jnp.where(sub > s, new, groups[i]) if i == g else new
    outs = []
    logs = jnp.zeros((8, 128), jnp.float32)
    for i in range(8):
        row_id = sub + 8 * i
        diag = lanes_of(groups[i], half + row_id)
        unit = jnp.where(col < row_id, groups[i], jnp.where(col == row_id, 1.0, 0.0))
        outs.append(unit * lax.rsqrt(diag))
        logs = logs + jnp.log(diag)
    return outs, 0.5 * jnp.sum(logs, axis=0, keepdims=True)


def factor_kernel(covs_ref, inv_ref, logdet_ref):
    regimes = covs_ref.shape[0]
    for p in range(regimes // 2):
        both = jnp.concatenate([covs_ref[2 * p], covs_ref[2 * p + 1]], axis=1)
        groups = [both[8 * i:8 * i + 8] for i in range(8)]
        outs, logs = eliminate(groups)
        both = jnp.concatenate(outs, axis=0)
        inv_ref[2 * p] = both[:, :K]
        inv_ref[2 * p + 1] = both[:, K:]
        logdet_ref[2 * p:2 * p + 1, :] = jnp.broadcast_to(logs[:, 0:1], (1, 128))
        logdet_ref[2 * p + 1:2 * p + 2, :] = jnp.broadcast_to(logs[:, K:K + 1], (1, 128))


def factor(covs):
    regimes = covs.shape[0]
    vmem = pl.BlockSpec(memory_space=pltpu.VMEM)
    inverse, logdet = pl.pallas_call(
        factor_kernel,
        out_shape=(
            jax.ShapeDtypeStruct(covs.shape, jnp.float32),
            jax.ShapeDtypeStruct((regimes, 128), jnp.float32),
        ),
        in_specs=[vmem],
        out_specs=(vmem, vmem),
    )(covs)
    return inverse, logdet[:, 0]


def softmax_of(logp):
    top = jnp.max(logp, axis=0, keepdims=True)
    expo = jnp.exp(logp - top)
    return expo / jnp.sum(expo, axis=0, keepdims=True)


def first_step(centred, variances, weights):
    maha = jnp.sum(centred * centred / variances[:, :, None], axis=1)
    logdet = 0.5 * jnp.sum(jnp.log(variances), axis=1)
    return softmax_of(jnp.log(weights)[:, None] - logdet[:, None] - 0.5 * maha)


def later_step(centred, inverse, logdet, weights):
    shifted = jnp.einsum("rkj,rjd->rkd", inverse, centred, precision=PRECISE)
    return softmax_of(jnp.log(weights)[:, None] - logdet[:, None] - 0.5 * jnp.sum(shifted * shifted, axis=1))


def total(values):
    flat = values.reshape(-1, 128)
    flat = flat + lax.ppermute(flat, "core", SWAP)
    spread = jnp.broadcast_to(flat[None], (8,) + flat.shape)
    return jnp.sum(lax.all_to_all(spread, "z", 0, 0), axis=0).reshape(values.shape)


def update(centred, resp, means):
    regimes = means.shape[0]
    count = jnp.sum(resp, axis=1)
    first = jnp.einsum("rd,rkd->rk", resp, centred, precision=PRECISE)
    second = jnp.einsum("rkd,rjd->rkj", centred * resp[:, None, :], centred, precision=PRECISE)
    packed = jnp.concatenate(
        [second, first[:, None, :], jnp.broadcast_to(count[:, None, None], (regimes, 1, K))], axis=1)
    packed = total(packed)
    second, first, count = packed[:, :K], packed[:, K], packed[:, K + 1, 0]
    counted = jnp.maximum(count, 1.0)
    moved = (first + count[:, None] * means) / counted[:, None]
    delta = moved - means
    cross = first[:, :, None] * delta[:, None, :]
    second = second - cross - jnp.swapaxes(cross, 1, 2) + count[:, None, None] * delta[:, :, None] * delta[:, None, :]
    covs = second / counted[:, None, None] + REG * jnp.eye(K, dtype=jnp.float32)[None]
    return moved, covs, counted / jnp.sum(counted)


def body(anomalies, eofs, means_init, variances, mixing):
    core = lax.axis_index("core")
    own = lax.all_to_all(jnp.broadcast_to(eofs[None], (8,) + eofs.shape), "z", 0, 0)
    other = lax.ppermute(own, "core", SWAP)
    first = jnp.where(core == 0, own, other)
    second = jnp.where(core == 0, other, own)
    patterns = jnp.stack([first, second], axis=1)
    patterns = jnp.transpose(patterns, (2, 0, 1, 3)).reshape(K, -1)
    partial = lax.dot_general(
        patterns, anomalies, (((1,), (1,)), ((), ())), preferred_element_type=jnp.float32)
    days = anomalies.shape[0]
    blocks = lax.all_to_all(partial.reshape(16, K // 16, days), "grid", 0, 0)
    mine = jnp.sum(blocks, axis=0)
    pcs_t = lax.all_to_all(jnp.broadcast_to(mine[None], (16,) + mine.shape), "grid", 0, 0).reshape(K, days)

    means = means_init
    weights = mixing / jnp.sum(mixing)
    centred = pcs_t[None] - means[:, :, None]
    resp = first_step(centred, variances, weights)
    for step in range(ITERS):
        means, covs, weights = update(centred, resp, means)
        inverse, logdet = factor(covs)
        centred = pcs_t[None] - means[:, :, None]
        resp = later_step(centred, inverse, logdet, weights)
    member = resp
    terms = jnp.dot(member.astype(jnp.bfloat16), anomalies, preferred_element_type=jnp.float32)
    pixels = terms.shape[1] // 16
    terms = jnp.swapaxes(terms.reshape(8, 16, pixels), 0, 1)
    count = jnp.broadcast_to(jnp.sum(member, axis=1)[None, :, None], (16, 8, 128))
    got = jnp.sum(lax.all_to_all(jnp.concatenate([terms, count], axis=2), ("z", "core"), 0, 0), axis=0)
    counted = jnp.maximum(got[:, pixels:pixels + 1], 1.0)
    composites = (got[:, :pixels] / counted).astype(jnp.bfloat16)
    return (means, covs, weights, member, composites)


def solution(mesh):
    split = Mesh(mesh.devices.reshape(16, 8, 2), ("grid", "z", "core"))
    day = ("z", "core")
    in_specs = (P(day, "grid"), P(None, ("grid",) + day), P(), P(), P())
    out_specs = (P(), P(), P(), P(None, day), P(None, ("grid",) + day))
    return jax.shard_map(body, mesh=split, in_specs=in_specs, out_specs=out_specs, check_vma=False)
```

time: 668 us -> 189 us (0.28)
  other arithmetic: 271 us -> 12.2 us
  waiting for transfers between devices: 249 us -> 36.7 us
  blocking collectives: 97 us -> 80.6 us
  Pallas kernels: 0 us -> 14.9 us
  between operations: 14.1 us -> 0.96 us
  starting transfers between devices: 0.57 us -> 13.1 us
    another operation x16 -> x1, other arithmetic: 259 us -> 0.04 us  [body(): patterns = jnp.stack([first, second], axis=1)]
    psum x3 -> x0, waiting for transfers between devices: 219 us -> none  [the longest x2 217 us: total_days(): return lax.psum(values, 'day')]
    all_to_all x0 -> x4, blocking collectives: none -> 80.6 us  [the longest x1 32.5 us: total(): lax.all_to_all(spread, 'z', 0, 0)]
    psum x3 -> x0, blocking collectives: 74 us -> none  [the longest x2 50.5 us: total_days(): return lax.psum(values, 'day')]
    all_to_all x0 -> x2, waiting for transfers between devices: none -> 33.6 us  [the longest x1 27.5 us: total(): lax.all_to_all(spread, 'z', 0, 0)]
    reduce_scatter x1 -> x0, waiting for transfers between devices: 30 us -> none  [body(): sums = lax.psum_scatter(terms, 'day', scatter_dimension=1, tiled=True)]
    all_gather x1 -> x0, blocking collectives: 23 us -> none  [body(): lax.all_gather(eofs, 'day', axis=1, tiled=True)]
    pallas_call x0 -> x2, Pallas kernels: none -> 14.9 us  [factor(): pl.pallas_call(factor_kernel, out_shape=(jax.ShapeDtypeStruct(covs.shape,...]
  transfers between devices with their start and end apart: 4 -> 5, of which waited for: 4 -> 5; matrix products, arithmetic and copies ran while one was open for 14% -> 1% of each run, Pallas kernels for 0% -> 0%
where the time goes in v1:
time: 189 us; the launch traced here: 188 us
  blocking collectives  80.6 us (43%)
  waiting for transfers between devices  36.7 us (19%)
  matrix products  25.1 us (13%)
  Pallas kernels  14.9 us (8%)
  starting transfers between devices  13.1 us (7%)
  other arithmetic  12.2 us (6%)
  local copies, waits for them, and re-layouts  4.84 us (3%)
    all_to_all x1, blocking collectives, total(): lax.all_to_all(spread, 'z', 0, 0)  32.5 us
    all_to_all x1, waiting for transfers between devices, total(): lax.all_to_all(spread, 'z', 0, 0)  27.5 us
    all_to_all x1, blocking collectives, body(): lax.all_to_all(jnp.broadcast_to(eofs[None], (8,) + eofs.shape), 'z', 0, 0)  19.2 us
    pallas_call x2, Pallas kernels, factor(): pl.pallas_call(factor_kernel, out_shape=(jax.ShapeDtypeStruct(covs.shape,...  14.9 us
    all_to_all x1, blocking collectives, body(): blocks = lax.all_to_all(partial.reshape(16, K // 16, days), 'grid', 0, 0)  14.7 us
    all_to_all x1, blocking collectives, body(): lax.all_to_all(jnp.concatenate([terms, count], axis=2), ('z', 'core'), 0, 0)  14.2 us
    all_to_all x1, waiting for transfers between devices, body(): lax.all_to_all(jnp.broadcast_to(mine[None], (16,) + mine.shape), 'grid',...  6.11 us
    dot_general x1, matrix products, body(): lax.dot_general(patterns, anomalies, (((1,), (1,)), ((), ())), preferred_...  6.04 us
  transfers between devices with their start and end apart: 5, of which 5 were waited for; matrix products, arithmetic and copies ran while one was open for 1% of the time, Pallas kernels for 0%

profile of v1, /device:TPU:1, one launch (start us, length us, event | category | flops | bytes accessed | tf_op | source)
XLA Modules:
  0.0 188.4 jit_solution(6826585868889207346)
XLA Ops:
  0.6 0.8 broadcast_in_dim.18
  1.4 19.2 %all_to_all.30 = bf16[8,64,256]{2,1,0:T(8,128)(2,1)S(1)} all-to-all(bf16[8,64,256]{2,1,0:T(8,128)(2,1)S(1)} %broadcast_in_dim.18), channel_id=1, replica_groups=mesh['grid'=16,'z'=8,'core'=2] {'z'}, dimensions={0} | all-to-all | bytes 524288 | tf_op jit(solution)/shard_map/all_to_all | solution.py:119
  20.6 2.5 %collective-permute-start = (bf16[8,64,256]{2,1,0:T(8,128)(2,1)S(1)}, bf16[8,64,256]{2,1,0:T(8,128)(2,1)S(1)}, u32[]{:S(2)}, u32[]{:S(2)}) collective-permute-start(bf16[8,64,256]{2,1,0:T(8,128)(2,1)S(1)} %all_to_all.30), channel_id=1, source_target_pairs={{0,1},{1,0},{2,3},{3,2},{4,5},{5,4},{6,7},{7,6},{8,9},{9,8},{10,11... | collective-permute-start | bytes 786440 | tf_op jit(solution)/shard_map/ppermute | solution.py:120
  23.1 1.2 collective-permute-done
  25.2 6.0 %fusion = f32[16,4,1024]{2,0,1:T(8,128)S(1)} fusion(bf16[1024,4096]{1,0:T(8,128)(2,1)} %param.5, bf16[16,4,4096]{2,1,0:T(4,128)(2,1)S(1)} %dot_general.26), kind=kOutput, calls=%fused_computation | convolution fusion | flops 536870912 | bytes 9175040 | tf_op jit(solution)/shard_map/dot_general | solution.py:125
  31.5 14.7 %all_to_all.31 = f32[16,4,1024]{2,1,0:T(4,128)S(1)} all-to-all(f32[16,4,1024]{2,1,0:T(4,128)S(1)} %copy.43), channel_id=1, replica_groups=mesh['grid'=16,'z'=8,'core'=2] {'grid'}, dimensions={0} | all-to-all | bytes 524288 | tf_op jit(solution)/shard_map/all_to_all | solution.py:128
  46.2 0.8 broadcast_in_dim.19
  46.9 3.5 %all-to-all-start.2 = ((f32[16,4,1024]{2,1,0:T(4,128)}), f32[16,4,1024]{2,1,0:T(4,128)S(1)}, u32[]{:S(2)}, u32[]{:S(2)}) async-start(f32[16,4,1024]{2,1,0:T(4,128)} %broadcast_in_dim.19), calls=%async_computation.2 | async-start | bytes 524288 | tf_op jit(solution)/shard_map/all_to_all | solution.py:130
  51.9 6.1 %all-to-all-done.2 = f32[16,4,1024]{2,1,0:T(4,128)S(1)} async-done(((f32[16,4,1024]{2,1,0:T(4,128)}), f32[16,4,1024]{2,1,0:T(4,128)S(1)}, u32[]{:S(2)}, u32[]{:S(2)}) %all-to-all-start.2) | async-done | bytes 262176 | tf_op jit(solution)/shard_map/all_to_all | solution.py:130
  58.9 2.4 %fusion.10 = f32[8,64,64]{1,2,0:T(8,128)S(1)} fusion(f32[8,1024]{1,0:T(8,128)S(1)} %get-tuple-element.28, f32[8,64]{1,0:T(8,128)S(1)} %copy-done.2, f32[64,1024]{1,0:T(8,128)S(1)} %sub.133), kind=kOutput, calls=%fused_computation.11 | convolution fusion | flops 404226048 | bytes 428032 | tf_op jit(solution)/shard_map/rkd,rjd->rkj/dot_general | solution.py:103
  61.3 1.9 fusion.8
  63.8 2.8 %collective-permute-start.1 = (f32[264,128]{1,0:T(8,128)S(1)}, f32[264,128]{1,0:T(8,128)S(1)}, u32[]{:S(2)}, u32[]{:S(2)}) collective-permute-start(f32[264,128]{1,0:T(8,128)S(1)} %reshape.200), channel_id=1, source_target_pairs={{0,1},{1,0},{2,3},{3,2},{4,5},{5,4},{6,7},{7,6},{8,9},{9,8},{10,11... | collective-permute-start | bytes 405512 | tf_op jit(solution)/shard_map/ppermute | solution.py:94
  66.6 1.0 collective-permute-done.1
  67.6 1.1 broadcast_in_dim.22
  68.6 3.7 %all-to-all-start.3 = ((f32[8,264,128]{2,1,0:T(8,128)}), f32[8,264,128]{2,1,0:T(8,128)S(1)}, u32[]{:S(2)}, u32[]{:S(2)}) async-start(f32[8,264,128]{2,1,0:T(8,128)} %broadcast_in_dim.22), calls=%async_computation.3 | async-start | bytes 2162688 | tf_op jit(solution)/shard_map/all_to_all | solution.py:96
  72.4 27.5 %all-to-all-done.3 = f32[8,264,128]{2,1,0:T(8,128)S(1)} async-done(((f32[8,264,128]{2,1,0:T(8,128)}), f32[8,264,128]{2,1,0:T(8,128)S(1)}, u32[]{:S(2)}, u32[]{:S(2)}) %all-to-all-start.3) | async-done | bytes 1081376 | tf_op jit(solution)/shard_map/all_to_all | solution.py:96
  101.5 1.0 fusion.42.covs_ref
  102.5 7.4 %shard_map.92 = (f32[8,64,64]{2,1,0:T(8,128)}, f32[8,128]{1,0:T(8,128)}) custom-call(f32[8,64,64]{2,1,0:T(8,128)} %fusion.42.covs_ref), custom_call_target="tpu_custom_call" | custom-call | tf_op jit(solution)/shard_map/pallas_call | solution.py:63
  110.0 0.8 subtract_reduce_fusion.1
  110.8 3.0 %multiply_reduce_fusion.1 = f32[8,1024]{1,0:T(8,128)S(1)} fusion(f32[8,64,64]{2,1,0:T(8,128)} %get-tuple-element.10, f32[8,64]{1,0:T(8,128)S(1)} %get-tuple-element.26, f32[64,1024]{1,0:T(8,128)S(1)} %sub.133), kind=kOutput, calls=%fused_computation.20 | convolution fusion | flops 404217856 | bytes 428032 | tf_op jit(solution)/shard_map/rkj,rjd->rkd/dot_general | solution.py:88
  114.1 2.4 %fusion.4 = f32[8,64,64]{1,2,0:T(8,128)S(1)} fusion(f32[8,1024]{1,0:T(8,128)S(1)} %get-tuple-element.23, f32[8,64]{1,0:T(8,128)S(1)} %get-tuple-element.26, f32[64,1024]{1,0:T(8,128)S(1)} %sub.133), kind=kOutput, calls=%fused_computation.4 | convolution fusion | flops 404226048 | bytes 428032 | tf_op jit(solution)/shard_map/rkd,rjd->rkj/dot_general | solution.py:103
  116.5 1.9 fusion.2
  119.6 1.0 collective-permute-done.2
  120.7 32.5 %all_to_all.32 = f32[8,264,128]{2,1,0:T(8,128)S(1)} all-to-all(f32[8,264,128]{2,1,0:T(8,128)S(1)} %broadcast_in_dim.25), channel_id=1, replica_groups=mesh['grid'=16,'z'=8,'core'=2] {'z'}, dimensions={0} | all-to-all | bytes 2162688 | tf_op jit(solution)/shard_map/all_to_all | solution.py:96
  154.1 1.2 broadcast_divide_fusion
  156.1 1.0 fusion.38.covs_ref
  157.1 7.4 %shard_map.93 = (f32[8,64,64]{2,1,0:T(8,128)}, f32[8,128]{1,0:T(8,128)}) custom-call(f32[8,64,64]{2,1,0:T(8,128)} %fusion.38.covs_ref), custom_call_target="tpu_custom_call" | custom-call | tf_op jit(solution)/shard_map/pallas_call | solution.py:63
  164.5 3.0 %multiply_reduce_fusion = f32[8,1024]{1,0:T(8,128)S(1)} fusion(f32[8,64,64]{2,1,0:T(8,128)} %get-tuple-element.12, f32[8,64]{1,0:T(8,128)S(1)} %get-tuple-element.21, f32[64,1024]{1,0:T(8,128)S(1)} %sub.133), kind=kOutput, calls=%fused_computation.17 | convolution fusion | flops 404217856 | bytes 428032 | tf_op jit(solution)/shard_map/rkj,rjd->rkd/dot_general | solution.py:88
  167.4 0.8 subtract_reduce_fusion
  168.6 4.6 %fusion.55 = f32[8,4096]{1,0:T(8,128)S(1)} fusion(bf16[1024,4096]{1,0:T(8,128)(2,1)} %param.5, f32[8,1024]{1,0:T(8,128)S(1)} %get-tuple-element.18), kind=kOutput, calls=%fused_computation.71 | convolution fusion | flops 67117056 | bytes 8552448 | tf_op jit(solution)/shard_map/dot_general | solution.py:142
  173.3 14.2 %all_to_all.33 = f32[16,8,384]{2,1,0:T(8,128)S(1)} all-to-all(f32[16,8,384]{2,1,0:T(8,128)S(1)} %pad_maximum_fusion.2), channel_id=1, replica_groups=mesh['grid'=16,'z'=8,'core'=2] {'z','core'}, dimensions={0} | all-to-all | bytes 393216 | tf_op jit(solution)/shard_map/all_to_all | solution.py:146
  187.7 0.7 fusion.57
  (61 shorter events, 9.6 us)
Async XLA Ops:
  20.6 3.6 %collective-permute-start = (bf16[8,64,256]{2,1,0:T(8,128)(2,1)S(1)}, bf16[8,64,256]{2,1,0:T(8,128)(2,1)S(1)}, u32[]{:S(2)}, u32[]{:S(2)}) collective-permute-start(bf16[8,64,256]{2,1,0:T(8,128)(2,1)S(1)} %all_to_all.30), channel_id=1, source_target_pairs={{0,1},{1,0},{2,3},{3,2},{4,5},{5,4},{6,7},{7,6},{8,9},{9,8},{10,11... | collective-permute-start | bytes 786440 | tf_op jit(solution)/shard_map/ppermute | solution.py:120
  31.2 19.2 %copy-start.1 = (f32[8,64]{1,0:T(8,128)S(1)}, f32[8,64]{1,0:T(8,128)}, u32[]{:S(2)}) copy-start(f32[8,64]{1,0:T(8,128)} %param.8) | copy-start | bytes 6148
  31.3 19.4 %copy-start.4 = (f32[8]{0:T(128)S(1)}, f32[8]{0:T(128)}, u32[]{:S(2)}) copy-start(f32[8]{0:T(128)} %param.9) | copy-start | bytes 100
  31.3 26.8 %copy-start.2 = (f32[8,64]{1,0:T(8,128)S(1)}, f32[8,64]{1,0:T(8,128)}, u32[]{:S(2)}) copy-start(f32[8,64]{1,0:T(8,128)} %param.7) | copy-start | bytes 6148
  46.9 11.0 %all-to-all-start.2 = ((f32[16,4,1024]{2,1,0:T(4,128)}), f32[16,4,1024]{2,1,0:T(4,128)S(1)}, u32[]{:S(2)}, u32[]{:S(2)}) async-start(f32[16,4,1024]{2,1,0:T(4,128)} %broadcast_in_dim.19), calls=%async_computation.2 | async-start | bytes 524288 | tf_op jit(solution)/shard_map/all_to_all | solution.py:130
  63.8 3.8 %collective-permute-start.1 = (f32[264,128]{1,0:T(8,128)S(1)}, f32[264,128]{1,0:T(8,128)S(1)}, u32[]{:S(2)}, u32[]{:S(2)}) collective-permute-start(f32[264,128]{1,0:T(8,128)S(1)} %reshape.200), channel_id=1, source_target_pairs={{0,1},{1,0},{2,3},{3,2},{4,5},{5,4},{6,7},{7,6},{8,9},{9,8},{10,11... | collective-permute-start | bytes 405512 | tf_op jit(solution)/shard_map/ppermute | solution.py:94
  68.6 31.2 %all-to-all-start.3 = ((f32[8,264,128]{2,1,0:T(8,128)}), f32[8,264,128]{2,1,0:T(8,128)S(1)}, u32[]{:S(2)}, u32[]{:S(2)}) async-start(f32[8,264,128]{2,1,0:T(8,128)} %broadcast_in_dim.22), calls=%async_computation.3 | async-start | bytes 2162688 | tf_op jit(solution)/shard_map/all_to_all | solution.py:96
  119.0 1.6 collective-permute-start.2
  156.1 17.2 %copy-start.3 = (f32[8,64]{1,0:T(8,128)}, f32[8,64]{1,0:T(8,128)S(1)}, u32[]{:S(2)}) copy-start(f32[8,64]{1,0:T(8,128)S(1)} %get-tuple-element.21) | copy-start | bytes 6148
  168.6 4.6 %copy-start = (f32[8,1024]{1,0:T(8,128)}, f32[8,1024]{1,0:T(8,128)S(1)}, u32[]{:S(2)}) copy-start(f32[8,1024]{1,0:T(8,128)S(1)} %get-tuple-element.18) | copy-start | bytes 98308

commit v2 on v0

v2 whole, which is shorter than its diff:
```python
import functools

import jax
import jax.numpy as jnp
from jax import lax
from jax.experimental import pallas as pl
from jax.experimental.pallas import tpu as pltpu
from jax.sharding import Mesh, PartitionSpec as P

K = 64
R = 8
HALF = R // 2
F32 = jnp.float32
BF16 = jnp.bfloat16
PRECISE = lax.Precision.HIGHEST
REG = 0.01
SWAP = [(0, 1), (1, 0)]
ROWS = K + 8
VMEM = pl.BlockSpec(memory_space=pltpu.VMEM)


def call(kernel, outs, operands, **cost):
    return pl.pallas_call(
        kernel,
        out_shape=tuple(jax.ShapeDtypeStruct(s, d) for s, d in outs),
        in_specs=[VMEM] * len(operands),
        out_specs=tuple([VMEM] * len(outs)),
        compiler_params=pltpu.CompilerParams(vmem_limit_bytes=48 * 1024 * 1024),
    )(*operands)


def lanes_of(x, index):
    return jnp.take_along_axis(x, index, axis=1)


def tile_ids():
    lane = lax.broadcasted_iota(jnp.int32, (8, 128), 1)
    sub = lax.broadcasted_iota(jnp.int32, (8, 128), 0)
    half = (lane >= K).astype(jnp.int32) * K
    return sub, half, lane - half


def by_core(core, at_zero, at_one):
    return jnp.where(core == 0, at_zero, at_one)


def eliminate(pairs):
    sub, half, col = tile_ids()
    for k in range(K):
        g, s = divmod(k, 8)
        at = half + k
        here = col == k
        for groups in pairs:
            row = jnp.broadcast_to(groups[g][s:s + 1, :], (8, 128))
            scaled = jnp.where(here, 1.0, row) / lanes_of(row, at)
            for i in range(g, 8):
                if i == g and s == 7:
                    continue
                new = jnp.where(here, 0.0, groups[i]) - lanes_of(groups[i], at) * scaled
                groups[i] = jnp.where(sub > s, new, groups[i]) if i == g else new
    results = []
    for groups in pairs:
        outs = []
        logs = jnp.zeros((8, 128), F32)
        for i in range(8):
            row_id = sub + 8 * i
            diag = lanes_of(groups[i], half + row_id)
            unit = jnp.where(col < row_id, groups[i], jnp.where(col == row_id, 1.0, 0.0))
            outs.append(unit * lax.rsqrt(diag))
            logs = logs + jnp.log(diag)
        results.append((outs, 0.5 * jnp.sum(logs, axis=0, keepdims=True)))
    return results


def project_kernel(own_ref, other_ref, fields_ref, out_ref):
    core = lax.axis_index("core")
    parts = []
    for z in range(8):
        own, other = own_ref[z], other_ref[z]
        parts += [by_core(core, own, other), by_core(core, other, own)]
    patterns = jnp.concatenate(parts, axis=1)
    for c in range(4):
        part = lax.dot_general(
            patterns, fields_ref[256 * c:256 * c + 256, :], (((1,), (1,)), ((), ())),
            preferred_element_type=F32)
        at = 256 * (c % 2)
        for b in range(8):
            out_ref[2 * b + c // 2, :, at:at + 256] = part[8 * b:8 * b + 8, :]


def read_pcs(pcs_ref):
    return [jnp.concatenate([pcs_ref[2 * b], pcs_ref[2 * b + 1]], axis=1) for b in range(8)]


def centre(pcs, row, offset):
    sub, _, _ = tile_ids()
    row = jnp.broadcast_to(row, (8, 128))
    outs = []
    for b in range(8):
        column = lanes_of(row, sub + (8 * b + offset))
        outs.append(pcs[b] - jnp.concatenate([column] * (pcs[b].shape[1] // 128), axis=1))
    return outs


def softmax_of(logp):
    top = jnp.max(logp, axis=0, keepdims=True)
    expo = jnp.exp(logp - top)
    return expo / jnp.sum(expo, axis=0, keepdims=True)


def moments(core, centred_of, resp, keep_ref, send_ref):
    days = resp.shape[1]
    counts = jnp.broadcast_to(jnp.sum(resp, axis=1, keepdims=True), (R, K))
    row_id = lax.broadcasted_iota(jnp.int32, (K, K), 0)
    col_id = lax.broadcasted_iota(jnp.int32, (K, K), 1)
    seconds, firsts = [], []
    for r in range(R):
        centred = jnp.concatenate(centred_of(r), axis=0)
        weight = resp[r:r + 1, :]
        left = jnp.concatenate([centred * weight, jnp.broadcast_to(weight, (8, days))], axis=0)
        got = lax.dot_general(left, centred, (((1,), (1,)), ((), ())), precision=PRECISE,
                              preferred_element_type=F32)
        seconds.append(got[:K])
        firsts.append(got[K:K + 1])
    packs = []
    for h in range(2):
        squares, tails = [], []
        for p in range(2):
            a = HALF * h + 2 * p
            squares.append(jnp.where(row_id >= col_id, seconds[a], seconds[a + 1]))
            diag = jnp.sum(jnp.where(row_id == col_id, seconds[a + 1], 0.0), axis=0, keepdims=True)
            tails.append(jnp.concatenate(
                [diag, firsts[a], firsts[a + 1], counts[a:a + 1], counts[a + 1:a + 2],
                 jnp.zeros((3, K), F32)], axis=0))
        packs.append(jnp.concatenate(
            [jnp.concatenate(squares, axis=1), jnp.concatenate(tails, axis=1)], axis=0))
    keep_ref[...] = by_core(core, packs[0], packs[1])
    send_ref[...] = by_core(core, packs[1], packs[0])


def first_kernel(pcs_ref, params_ref, base_ref, keep_ref, send_ref):
    pcs = read_pcs(pcs_ref)
    sub, _, _ = tile_ids()
    logs = []
    for r in range(R):
        row = params_ref[r:r + 1, :]
        inverse = jnp.broadcast_to(1.0 / row, (8, 128))
        centred = centre(pcs, row, 0)
        total = None
        for b in range(8):
            column = lanes_of(inverse, sub + (8 * b + K))
            scale = jnp.concatenate([column] * 8, axis=1)
            term = centred[b] * centred[b] * scale
            total = term if total is None else total + term
        logs.append(jnp.sum(total, axis=0, keepdims=True))
    logp = base_ref[:, 0:1] - 0.5 * jnp.concatenate(logs, axis=0)
    resp = softmax_of(logp)
    moments(lax.axis_index("core"), lambda r: centre(pcs, params_ref[r:r + 1, :], 0), resp, keep_ref, send_ref)


def merge_kernel(parts_ref, shift_ref, block_ref, covs_ref):
    sub, half, col = tile_ids()
    total = parts_ref[0]
    for z in range(1, 8):
        total = total + parts_ref[z]
    packed = total[:K]
    flipped = packed.T
    flipped = jnp.concatenate([flipped[:K], flipped[K:]], axis=1)
    tail = total[K:]
    pairs = []
    infos = []
    for p in range(2):
        first, count, shift = tail[1 + p:2 + p], tail[3 + p:4 + p], shift_ref[p:p + 1, :]
        counted = jnp.maximum(count, 1.0)
        mean = (first + count * shift) / counted
        delta = mean - shift
        rest = first - count * delta
        first_b, delta_b = jnp.broadcast_to(first, (8, 128)), jnp.broadcast_to(delta, (8, 128))
        scale = 1.0 / counted
        groups = []
        for g in range(8):
            row_id = sub + 8 * g
            straight, turned = packed[8 * g:8 * g + 8], flipped[8 * g:8 * g + 8]
            if p == 0:
                second = jnp.where(row_id >= col, straight, turned)
            else:
                second = jnp.where(row_id < col, straight, jnp.where(row_id > col, turned, tail[0:1]))
            at = half + row_id
            second = second - lanes_of(first_b, at) * delta - lanes_of(delta_b, at) * rest
            cov = second * scale + jnp.where(row_id == col, REG, 0.0)
            covs_ref[K * p + 8 * g:K * p + 8 * g + 8, :] = cov
            groups.append(cov)
        pairs.append(groups)
        infos.append((mean, counted))
    (first_out, first_log), (second_out, second_log) = eliminate(pairs)
    for g in range(8):
        block_ref[8 * g:8 * g + 8, :] = first_out[g]
        block_ref[K + 8 * g:K + 8 * g + 8, :] = second_out[g]
    block_ref[2 * K:, :] = jnp.concatenate(
        [infos[0][0], infos[1][0], first_log, second_log, infos[0][1], infos[1][1],
         jnp.zeros((2, 128), F32)], axis=0)


def regime_of(r):
    h, q = divmod(r, HALF)
    return h, q % 2, K * (q // 2)


def expect(pcs, halves):
    infos = [block[2 * K:] for block in halves]

    def column(at):
        rows = []
        for r in range(R):
            h, p, offset = regime_of(r)
            rows.append(infos[h][at + p:at + p + 1, offset:offset + 1])
        return jnp.concatenate(rows, axis=0)

    counted = column(4)
    weights = counted / jnp.sum(counted, axis=0, keepdims=True)
    logs = []
    for r in range(R):
        h, p, offset = regime_of(r)
        inverse = halves[h][K * p:K * p + K, offset:offset + K]
        centred = jnp.concatenate(centre(pcs, infos[h][p:p + 1, :], offset), axis=0)
        shifted = lax.dot_general(inverse, centred, (((1,), (0,)), ((), ())), precision=PRECISE,
                                  preferred_element_type=F32)
        logs.append(jnp.sum(shifted * shifted, axis=0, keepdims=True))
    logp = jnp.log(weights) - column(2) - 0.5 * jnp.concatenate(logs, axis=0)
    return softmax_of(logp), weights


def halves_of(core, keep_ref, got_ref):
    keep, got = keep_ref[...], got_ref[...]
    return [by_core(core, keep, got), by_core(core, got, keep)]


def middle_kernel(pcs_ref, keep_ref, got_ref, out_keep_ref, out_send_ref):
    core = lax.axis_index("core")
    pcs = read_pcs(pcs_ref)
    halves = halves_of(core, keep_ref, got_ref)
    resp, _ = expect(pcs, halves)

    def centred_of(r):
        h, p, offset = regime_of(r)
        return centre(pcs, halves[h][2 * K + p:2 * K + p + 1, :], offset)

    moments(core, centred_of, resp, out_keep_ref, out_send_ref)


def last_kernel(pcs_ref, keep_ref, got_ref, fields_ref, member_ref, terms_ref, means_ref, weights_ref):
    core = lax.axis_index("core")
    pcs = read_pcs(pcs_ref)
    halves = halves_of(core, keep_ref, got_ref)
    member, weights = expect(pcs, halves)
    member_ref[...] = member
    weights_ref[...] = jnp.broadcast_to(weights, (R, 128))
    means = []
    for r in range(R):
        h, p, offset = regime_of(r)
        means.append(halves[h][2 * K + p:2 * K + p + 1, offset:offset + K])
    means_ref[...] = jnp.concatenate(means, axis=0)
    count = jnp.broadcast_to(jnp.sum(member, axis=1, keepdims=True), (R, 128))
    rounded = member.astype(BF16)
    for j in range(16):
        terms_ref[j, :, 0:256] = jnp.dot(rounded, fields_ref[:, 256 * j:256 * j + 256], preferred_element_type=F32)
        terms_ref[j, :, 256:384] = count


def spread(x, n):
    return jnp.broadcast_to(x[None], (n,) + x.shape)


def merge(keep, send, shift):
    half = keep + lax.ppermute(send, "core", SWAP)
    parts = lax.all_to_all(spread(half, 8), "z", 0, 0)
    return call(merge_kernel, [((2 * K + 8, 128), F32), ((2 * K, 128), F32)], [parts, shift])


def body(anomalies, eofs, means_init, variances, mixing):
    days = anomalies.shape[0]
    core = lax.axis_index("core")
    own = lax.all_to_all(spread(eofs, 8), "z", 0, 0)
    other = lax.ppermute(own, "core", SWAP)
    partial, = call(project_kernel, [((16, 8, days // 2), F32)], [own, other, anomalies])
    mine = jnp.sum(lax.all_to_all(partial, "grid", 0, 0), axis=0)
    pcs = lax.all_to_all(spread(mine, 16), "grid", 0, 0)

    params = jnp.concatenate([means_init, variances], axis=1)
    base = jnp.log(mixing / jnp.sum(mixing)) - 0.5 * jnp.sum(jnp.log(variances), axis=1)
    base = jnp.broadcast_to(base[:, None], (R, 128))
    sides = means_init.reshape(2, 2, 2, K).swapaxes(1, 2).reshape(2, 2, 2 * K)
    shift = jnp.where(core == 0, sides[0], sides[1])

    pack = [((ROWS, 128), F32)] * 2
    keep, send = call(first_kernel, pack, [pcs, params, base])
    block, _ = merge(keep, send, shift)
    got = lax.ppermute(block, "core", SWAP)
    keep, send = call(middle_kernel, pack, [pcs, block, got])
    block, covs = merge(keep, send, block[2 * K:2 * K + 2])
    got = lax.ppermute(block, "core", SWAP)
    got_covs = lax.ppermute(covs, "core", SWAP)
    member, terms, means, weights = call(
        last_kernel,
        [((R, days), F32), ((16, R, 384), F32), ((R, K), F32), ((R, 128), F32)],
        [pcs, block, got, anomalies])
    sums = jnp.sum(lax.all_to_all(terms, ("z", "core"), 0, 0), axis=0)
    composites = (sums[:, :256] / jnp.maximum(sums[:, 256:257], 1.0)).astype(BF16)

    both = jnp.where(core == 0, jnp.stack([covs, got_covs]), jnp.stack([got_covs, covs]))
    covs = both.reshape(2, 2, K, 2, K).transpose(0, 3, 1, 2, 4).reshape(R, K, K)
    return (means, covs, weights[:, 0], member, composites)


def solution(mesh):
    split = Mesh(mesh.devices.reshape(16, 8, 2), ("grid", "z", "core"))
    day = ("z", "core")
    in_specs = (P(day, "grid"), P(None, ("grid",) + day), P(), P(), P())
    out_specs = (P(), P(), P(), P(None, day), P(None, ("grid",) + day))
    return jax.shard_map(body, mesh=split, in_specs=in_specs, out_specs=out_specs, check_vma=False)
```

time: 668 us -> 141 us (0.21)
  other arithmetic: 271 us -> 2.43 us
  waiting for transfers between devices: 249 us -> 53 us
  blocking collectives: 97 us -> 19.2 us
  Pallas kernels: 0 us -> 31.7 us
  matrix products: 29.6 us -> 0 us
  starting transfers between devices: 0.57 us -> 28.1 us
  between operations: 14.1 us -> 0.81 us
    another operation x16 -> x0, other arithmetic: 259 us -> none  [the longest x10 141 us: log_density(): factor = jnp.linalg.cholesky(covs)]
    psum x3 -> x0, waiting for transfers between devices: 219 us -> none  [the longest x2 217 us: total_days(): return lax.psum(values, 'day')]
    psum x3 -> x0, blocking collectives: 74 us -> none  [the longest x2 50.5 us: total_days(): return lax.psum(values, 'day')]
    all_to_all x0 -> x5, waiting for transfers between devices: none -> 47.4 us  [the longest x2 25.8 us: merge(): parts = lax.all_to_all(spread(half, 8), 'z', 0, 0)]
    pallas_call x0 -> x6, Pallas kernels: none -> 31.7 us  [call(): pl.pallas_call(kernel, out_shape=tuple((jax.ShapeDtypeStruct(s, d) for s,...]
    reduce_scatter x1 -> x0, waiting for transfers between devices: 30 us -> none  [body(): sums = lax.psum_scatter(terms, 'day', scatter_dimension=1, tiled=True)]
    dot_general x9 -> x0, matrix products: 27.8 us -> none  [the longest x2 7.29 us: second_moments(): jnp.einsum('rkd,rjd->rkj', diff * resp[:, None, :], diff, precision=PRECISE)]
    all_gather x1 -> x0, blocking collectives: 23 us -> none  [body(): lax.all_gather(eofs, 'day', axis=1, tiled=True)]
  transfers between devices with their start and end apart: 4 -> 11, of which waited for: 4 -> 11; matrix products, arithmetic and copies ran while one was open for 14% -> 2% of each run, Pallas kernels for 0% -> 0%
where the time goes in v2:
time: 141 us; the launch traced here: 140 us
  waiting for transfers between devices  53 us (38%)
  Pallas kernels  31.7 us (22%)
  starting transfers between devices  28.1 us (20%)
  blocking collectives  19.2 us (14%)
  local copies, waits for them, and re-layouts  4.74 us (3%)
  other arithmetic  2.43 us (2%)
    pallas_call x6, Pallas kernels, call(): pl.pallas_call(kernel, out_shape=tuple((jax.ShapeDtypeStruct(s, d) for s,...  31.7 us
    all_to_all x2, waiting for transfers between devices, merge(): parts = lax.all_to_all(spread(half, 8), 'z', 0, 0)  25.8 us
    all_to_all x1, blocking collectives, body(): own = lax.all_to_all(spread(eofs, 8), 'z', 0, 0)  19.2 us
    all_to_all x1, waiting for transfers between devices, body(): mine = jnp.sum(lax.all_to_all(partial, 'grid', 0, 0), axis=0)  7.98 us
    all_to_all x1, waiting for transfers between devices, body(): sums = jnp.sum(lax.all_to_all(terms, ('z', 'core'), 0, 0), axis=0)  7.47 us
    all_to_all x2, starting transfers between devices, merge(): parts = lax.all_to_all(spread(half, 8), 'z', 0, 0)  6.84 us
    all_to_all x1, starting transfers between devices, body(): mine = jnp.sum(lax.all_to_all(partial, 'grid', 0, 0), axis=0)  6.75 us
    all_to_all x1, waiting for transfers between devices, body(): pcs = lax.all_to_all(spread(mine, 16), 'grid', 0, 0)  6.16 us
  transfers between devices with their start and end apart: 11, of which 11 were waited for; matrix products, arithmetic and copies ran while one was open for 2% of the time, Pallas kernels for 0%

profile of v2, /device:TPU:1, one launch (start us, length us, event | category | flops | bytes accessed | tf_op | source)
XLA Modules:
  0.0 139.9 jit_solution(14060766630162939460)
XLA Ops:
  0.7 0.8 broadcast_in_dim.10
  1.5 19.2 %all_to_all.30.own_ref = bf16[8,64,256]{2,1,0:T(8,128)(2,1)S(1)} all-to-all(bf16[8,64,256]{2,1,0:T(8,128)(2,1)S(1)} %broadcast_in_dim.10), channel_id=1, replica_groups=mesh['grid'=16,'z'=8,'core'=2] {'z'}, dimensions={0} | all-to-all | bytes 524288 | tf_op jit(solution)/shard_map/all_to_all | solution.py:283
  20.6 2.5 %collective-permute-start = (bf16[8,64,256]{2,1,0:T(8,128)(2,1)S(1)}, bf16[8,64,256]{2,1,0:T(8,128)(2,1)S(1)}, u32[]{:S(2)}, u32[]{:S(2)}) collective-permute-start(bf16[8,64,256]{2,1,0:T(8,128)(2,1)S(1)} %all_to_all.30.own_ref), channel_id=1, source_target_pairs={{0,1},{1,0},{2,3},{3,2},{4,5},{5,4},{6,7},{7,6},{8,9},{9,8},{10,11... | collective-permute-start | bytes 786440 | tf_op jit(solution)/shard_map/ppermute | solution.py:284
  23.1 1.2 collective-permute-done.other_ref
  24.3 6.7 %shard_map.92 = f32[16,8,512]{2,1,0:T(8,128)} custom-call(bf16[8,64,256]{2,1,0:T(8,128)(2,1)S(1)} %all_to_all.30.own_ref, bf16[8,64,256]{2,1,0:T(8,128)(2,1)S(1)} %collective-permute-done.other_ref, bf16[1024,4096]{1,0:T(8,128)(2,1)} %fields_ref.3), custom_call_target="tpu_custom_call" | custom-call | tf_op jit(solution)/shard_map/pallas_call | solution.py:23
  31.0 6.8 %all-to-all-start.1 = ((f32[16,8,512]{2,1,0:T(8,128)}), f32[16,8,512]{2,1,0:T(8,128)S(1)}, u32[]{:S(2)}, u32[]{:S(2)}) async-start(f32[16,8,512]{2,1,0:T(8,128)} %shard_map.92), calls=%async_computation.1 | async-start | bytes 524288 | tf_op jit(solution)/shard_map/all_to_all | solution.py:286
  37.9 8.0 %all-to-all-done.1 = f32[16,8,512]{2,1,0:T(8,128)S(1)} async-done(((f32[16,8,512]{2,1,0:T(8,128)}), f32[16,8,512]{2,1,0:T(8,128)S(1)}, u32[]{:S(2)}, u32[]{:S(2)}) %all-to-all-start.1) | async-done | bytes 262176 | tf_op jit(solution)/shard_map/all_to_all | solution.py:286
  45.9 0.7 broadcast_in_dim.11
  46.6 3.5 %all-to-all-start.2 = ((f32[16,8,512]{2,1,0:T(8,128)}), f32[16,8,512]{2,1,0:T(8,128)S(1)}, u32[]{:S(2)}, u32[]{:S(2)}) async-start(f32[16,8,512]{2,1,0:T(8,128)} %broadcast_in_dim.11), calls=%async_computation.2 | async-start | bytes 524288 | tf_op jit(solution)/shard_map/all_to_all | solution.py:287
  51.5 6.2 %all-to-all-done.2.pcs_ref = f32[16,8,512]{2,1,0:T(8,128)S(1)} async-done(((f32[16,8,512]{2,1,0:T(8,128)}), f32[16,8,512]{2,1,0:T(8,128)S(1)}, u32[]{:S(2)}, u32[]{:S(2)}) %all-to-all-start.2) | async-done | bytes 262176 | tf_op jit(solution)/shard_map/all_to_all | solution.py:287
  57.7 2.8 %shard_map.93 = (f32[72,128]{1,0:T(8,128)S(1)}, f32[72,128]{1,0:T(8,128)S(1)}) custom-call(f32[16,8,512]{2,1,0:T(8,128)S(1)} %all-to-all-done.2.pcs_ref, f32[8,128]{1,0:T(8,128)S(1)} %pad_maximum_fusion.params_ref, f32[8,128]{1,0:T(8,128)S(1)} %broadcast_in_dim.12.base_ref), custom_call_target="tpu_custom_call" | custom-call | tf_op jit(solution)/shard_map/pallas_call | solution.py:23
  60.5 2.8 %collective-permute-start.1 = (f32[72,128]{1,0:T(8,128)S(1)}, f32[72,128]{1,0:T(8,128)S(1)}, u32[]{:S(2)}, u32[]{:S(2)}) collective-permute-start(f32[72,128]{1,0:T(8,128)S(1)} %get-tuple-element.17), channel_id=1, source_target_pairs={{0,1},{1,0},{2,3},{3,2},{4,5},{5,4},{6,7},{7,6},{8,9},{9,8},{10,11... | collective-permute-start | bytes 110600 | tf_op jit(solution)/shard_map/ppermute | solution.py:275
  63.3 0.9 collective-permute-done.1
  64.1 0.7 broadcast_in_dim.13
  64.9 3.4 %all-to-all-start.3 = ((f32[8,72,128]{2,1,0:T(8,128)}), f32[8,72,128]{2,1,0:T(8,128)S(1)}, u32[]{:S(2)}, u32[]{:S(2)}) async-start(f32[8,72,128]{2,1,0:T(8,128)} %broadcast_in_dim.13), calls=%async_computation.3 | async-start | bytes 589824 | tf_op jit(solution)/shard_map/all_to_all | solution.py:276
  68.4 12.9 %all-to-all-done.3.parts_ref = f32[8,72,128]{2,1,0:T(8,128)S(1)} async-done(((f32[8,72,128]{2,1,0:T(8,128)}), f32[8,72,128]{2,1,0:T(8,128)S(1)}, u32[]{:S(2)}, u32[]{:S(2)}) %all-to-all-start.3) | async-done | bytes 294944 | tf_op jit(solution)/shard_map/all_to_all | solution.py:276
  81.3 5.6 %shard_map.94 = (f32[136,128]{1,0:T(8,128)S(1)}, f32[128,128]{1,0:T(8,128)}) custom-call(f32[8,72,128]{2,1,0:T(8,128)S(1)} %all-to-all-done.3.parts_ref, f32[2,128]{1,0:T(2,128)S(1)} %select_n.21.shift_ref), custom_call_target="tpu_custom_call" | custom-call | tf_op jit(solution)/shard_map/pallas_call | solution.py:23
  86.8 0.7 collective-permute-start.2
  87.6 0.9 collective-permute-done.2.got_ref
  88.5 4.0 %shard_map.95 = (f32[72,128]{1,0:T(8,128)S(1)}, f32[72,128]{1,0:T(8,128)S(1)}) custom-call(f32[16,8,512]{2,1,0:T(8,128)S(1)} %all-to-all-done.2.pcs_ref, f32[136,128]{1,0:T(8,128)S(1)} %get-tuple-element.18.keep_ref, f32[136,128]{1,0:T(8,128)S(1)} %collective-permute-done.2.got_ref), custom_call_target="tpu_custom_call" | custom-call | tf_op jit(solution)/shard_map/pallas_call | solution.py:23
  92.9 0.9 collective-permute-done.3
  93.8 0.7 broadcast_in_dim.14
  94.5 3.4 %all-to-all-start.4 = ((f32[8,72,128]{2,1,0:T(8,128)}), f32[8,72,128]{2,1,0:T(8,128)S(1)}, u32[]{:S(2)}, u32[]{:S(2)}) async-start(f32[8,72,128]{2,1,0:T(8,128)} %broadcast_in_dim.14), calls=%async_computation.4 | async-start | bytes 589824 | tf_op jit(solution)/shard_map/all_to_all | solution.py:276
  98.0 13.0 %all-to-all-done.4.parts_ref = f32[8,72,128]{2,1,0:T(8,128)S(1)} async-done(((f32[8,72,128]{2,1,0:T(8,128)}), f32[8,72,128]{2,1,0:T(8,128)S(1)}, u32[]{:S(2)}, u32[]{:S(2)}) %all-to-all-start.4) | async-done | bytes 294944 | tf_op jit(solution)/shard_map/all_to_all | solution.py:276
  110.9 5.6 %shard_map.96 = (f32[136,128]{1,0:T(8,128)S(1)}, f32[128,128]{1,0:T(8,128)S(1)}) custom-call(f32[8,72,128]{2,1,0:T(8,128)S(1)} %all-to-all-done.4.parts_ref, f32[2,128]{1,0:T(2,128)S(1)} %slice.22.shift_ref), custom_call_target="tpu_custom_call" | custom-call | tf_op jit(solution)/shard_map/pallas_call | solution.py:23
  117.1 0.9 collective-permute-done.4.got_ref
  118.0 7.1 %shard_map.97 = (f32[8,1024]{1,0:T(8,128)}, f32[16,8,384]{2,1,0:T(8,128)}, f32[8,64]{1,0:T(8,128)}, f32[8,128]{1,0:T(8,128)S(1)}) custom-call(f32[16,8,512]{2,1,0:T(8,128)S(1)} %all-to-all-done.2.pcs_ref, f32[136,128]{1,0:T(8,128)S(1)} %get-tuple-element.21.keep_ref, f32[136,128]{1,0:T(8,128)S(1)} %collective-permute-done.4.got_ref, ...), custom_call_target="tpu_custom_call" | custom-call | tf_op jit(solution)/shard_map/pallas_call | solution.py:23
  125.1 3.7 %all-to-all-start.5 = ((f32[16,8,384]{2,1,0:T(8,128)}), f32[16,8,384]{2,1,0:T(8,128)S(1)}, u32[]{:S(2)}, u32[]{:S(2)}) async-start(f32[16,8,384]{2,1,0:T(8,128)} %get-tuple-element.26), calls=%async_computation.5 | async-start | bytes 393216 | tf_op jit(solution)/shard_map/all_to_all | solution.py:307
  129.2 0.8 collective-permute-done.5
  130.3 0.7 copy.13
  131.7 7.5 %all-to-all-done.5 = f32[16,8,384]{2,1,0:T(8,128)S(1)} async-done(((f32[16,8,384]{2,1,0:T(8,128)}), f32[16,8,384]{2,1,0:T(8,128)S(1)}, u32[]{:S(2)}, u32[]{:S(2)}) %all-to-all-start.5) | async-done | bytes 196640 | tf_op jit(solution)/shard_map/all_to_all | solution.py:307
  139.3 0.7 fusion.1
  (27 shorter events, 4.1 us)
Async XLA Ops:
  0.6 37.1 %copy-start = (f32[8,64]{1,0:T(8,128)S(1)}, f32[8,64]{1,0:T(8,128)}, u32[]{:S(2)}) copy-start(f32[8,64]{1,0:T(8,128)} %param.8) | copy-start | bytes 6148
  0.6 49.5 %copy-start.1 = (f32[8,64]{1,0:T(8,128)S(1)}, f32[8,64]{1,0:T(8,128)}, u32[]{:S(2)}) copy-start(f32[8,64]{1,0:T(8,128)} %param.7) | copy-start | bytes 6148
  0.7 49.6 %copy-start.2 = (f32[8]{0:T(128)S(1)}, f32[8]{0:T(128)}, u32[]{:S(2)}) copy-start(f32[8]{0:T(128)} %param.9) | copy-start | bytes 100
  20.6 3.6 %collective-permute-start = (bf16[8,64,256]{2,1,0:T(8,128)(2,1)S(1)}, bf16[8,64,256]{2,1,0:T(8,128)(2,1)S(1)}, u32[]{:S(2)}, u32[]{:S(2)}) collective-permute-start(bf16[8,64,256]{2,1,0:T(8,128)(2,1)S(1)} %all_to_all.30.own_ref), channel_id=1, source_target_pairs={{0,1},{1,0},{2,3},{3,2},{4,5},{5,4},{6,7},{7,6},{8,9},{9,8},{10,11... | collective-permute-start | bytes 786440 | tf_op jit(solution)/shard_map/ppermute | solution.py:284
  31.0 14.9 %all-to-all-start.1 = ((f32[16,8,512]{2,1,0:T(8,128)}), f32[16,8,512]{2,1,0:T(8,128)S(1)}, u32[]{:S(2)}, u32[]{:S(2)}) async-start(f32[16,8,512]{2,1,0:T(8,128)} %shard_map.92), calls=%async_computation.1 | async-start | bytes 524288 | tf_op jit(solution)/shard_map/all_to_all | solution.py:286
  46.6 11.0 %all-to-all-start.2 = ((f32[16,8,512]{2,1,0:T(8,128)}), f32[16,8,512]{2,1,0:T(8,128)S(1)}, u32[]{:S(2)}, u32[]{:S(2)}) async-start(f32[16,8,512]{2,1,0:T(8,128)} %broadcast_in_dim.11), calls=%async_computation.2 | async-start | bytes 524288 | tf_op jit(solution)/shard_map/all_to_all | solution.py:287
  60.5 3.6 %collective-permute-start.1 = (f32[72,128]{1,0:T(8,128)S(1)}, f32[72,128]{1,0:T(8,128)S(1)}, u32[]{:S(2)}, u32[]{:S(2)}) collective-permute-start(f32[72,128]{1,0:T(8,128)S(1)} %get-tuple-element.17), channel_id=1, source_target_pairs={{0,1},{1,0},{2,3},{3,2},{4,5},{5,4},{6,7},{7,6},{8,9},{9,8},{10,11... | collective-permute-start | bytes 110600 | tf_op jit(solution)/shard_map/ppermute | solution.py:275
  64.9 16.4 %all-to-all-start.3 = ((f32[8,72,128]{2,1,0:T(8,128)}), f32[8,72,128]{2,1,0:T(8,128)S(1)}, u32[]{:S(2)}, u32[]{:S(2)}) async-start(f32[8,72,128]{2,1,0:T(8,128)} %broadcast_in_dim.13), calls=%async_computation.3 | async-start | bytes 589824 | tf_op jit(solution)/shard_map/all_to_all | solution.py:276
  86.8 1.6 %collective-permute-start.2 = (f32[136,128]{1,0:T(8,128)S(1)}, f32[136,128]{1,0:T(8,128)S(1)}, u32[]{:S(2)}, u32[]{:S(2)}) collective-permute-start(f32[136,128]{1,0:T(8,128)S(1)} %get-tuple-element.18.keep_ref), channel_id=1, source_target_pairs={{0,1},{1,0},{2,3},{3,2},{4,5},{5,4},{6,7},{7,6},{8,9},{9,8},{10,11... | collective-permute-start | bytes 208904 | tf_op jit(solution)/shard_map/ppermute | solution.py:298
  92.5 1.3 collective-permute-start.3
  94.5 16.4 %all-to-all-start.4 = ((f32[8,72,128]{2,1,0:T(8,128)}), f32[8,72,128]{2,1,0:T(8,128)S(1)}, u32[]{:S(2)}, u32[]{:S(2)}) async-start(f32[8,72,128]{2,1,0:T(8,128)} %broadcast_in_dim.14), calls=%async_computation.4 | async-start | bytes 589824 | tf_op jit(solution)/shard_map/all_to_all | solution.py:276
  116.5 1.5 %collective-permute-start.4 = (f32[136,128]{1,0:T(8,128)S(1)}, f32[136,128]{1,0:T(8,128)S(1)}, u32[]{:S(2)}, u32[]{:S(2)}) collective-permute-start(f32[136,128]{1,0:T(8,128)S(1)} %get-tuple-element.21.keep_ref), channel_id=1, source_target_pairs={{0,1},{1,0},{2,3},{3,2},{4,5},{5,4},{6,7},{7,6},{8,9},{9,8},{10,11... | collective-permute-start | bytes 208904 | tf_op jit(solution)/shard_map/ppermute | solution.py:301
  125.1 14.0 %all-to-all-start.5 = ((f32[16,8,384]{2,1,0:T(8,128)}), f32[16,8,384]{2,1,0:T(8,128)S(1)}, u32[]{:S(2)}, u32[]{:S(2)}) async-start(f32[16,8,384]{2,1,0:T(8,128)} %get-tuple-element.26), calls=%async_computation.5 | async-start | bytes 393216 | tf_op jit(solution)/shard_map/all_to_all | solution.py:307
  128.8 1.3 collective-permute-start.5

commit v3 on v2

--- a/solution.py
+++ b/solution.py
@@ -16,16 +16,20 @@
 REG = 0.01
 SWAP = [(0, 1), (1, 0)]
 ROWS = K + 8
+LIMIT = 48 * 1024 * 1024
+CHUNKS = 8
 VMEM = pl.BlockSpec(memory_space=pltpu.VMEM)
-
-
-def call(kernel, outs, operands, **cost):
+HBM = pl.BlockSpec(memory_space=pltpu.HBM)
+
+
+def call(kernel, outs, operands, scratch=(), stay=0):
     return pl.pallas_call(
         kernel,
         out_shape=tuple(jax.ShapeDtypeStruct(s, d) for s, d in outs),
-        in_specs=[VMEM] * len(operands),
+        in_specs=[VMEM] * (len(operands) - stay) + [HBM] * stay,
         out_specs=tuple([VMEM] * len(outs)),
-        compiler_params=pltpu.CompilerParams(vmem_limit_bytes=48 * 1024 * 1024),
+        scratch_shapes=scratch,
+        compiler_params=pltpu.CompilerParams(vmem_limit_bytes=LIMIT),
     )(*operands)
 
 
@@ -46,18 +50,27 @@
 
 def eliminate(pairs):
     sub, half, col = tile_ids()
-    for k in range(K):
+    for k in range(0, K, 2):
         g, s = divmod(k, 8)
-        at = half + k
-        here = col == k
+        at0, at1 = half + k, half + k + 1
+        here0, here1 = col == k, col == k + 1
+        here = here0 | here1
         for groups in pairs:
-            row = jnp.broadcast_to(groups[g][s:s + 1, :], (8, 128))
-            scaled = jnp.where(here, 1.0, row) / lanes_of(row, at)
+            row0 = jnp.broadcast_to(groups[g][s:s + 1, :], (8, 128))
+            row1 = jnp.broadcast_to(groups[g][s + 1:s + 2, :], (8, 128))
+            a, b, c = lanes_of(row0, at0), lanes_of(row0, at1), lanes_of(row1, at1)
+            scale = 1.0 / (a * c - b * b)
+            row0 = jnp.where(here, here0.astype(F32), row0) * scale
+            row1 = jnp.where(here, here1.astype(F32), row1) * scale
+            scaled0 = c * row0 - b * row1
+            scaled1 = a * row1 - b * row0
             for i in range(g, 8):
-                if i == g and s == 7:
+                if i == g and s == 6:
                     continue
-                new = jnp.where(here, 0.0, groups[i]) - lanes_of(groups[i], at) * scaled
-                groups[i] = jnp.where(sub > s, new, groups[i]) if i == g else new
+                f0, f1 = lanes_of(groups[i], at0), lanes_of(groups[i], at1)
+                new = jnp.where(here, 0.0, groups[i]) - f0 * scaled0 - f1 * scaled1
+                groups[i] = jnp.where(sub > s + 1, new, groups[i]) if i == g else new
+    odd = (sub & 1) == 1
     results = []
     for groups in pairs:
         outs = []
@@ -65,27 +78,43 @@
         for i in range(8):
             row_id = sub + 8 * i
             diag = lanes_of(groups[i], half + row_id)
-            unit = jnp.where(col < row_id, groups[i], jnp.where(col == row_id, 1.0, 0.0))
+            side = lanes_of(groups[i], half + (row_id ^ 1))
+            unit = jnp.where(col < row_id - (sub & 1), groups[i], (col == row_id).astype(F32))
+            ratio = side / pltpu.roll(diag, 1, 0)
+            unit = jnp.where(odd, unit - ratio * pltpu.roll(unit, 1, 0), unit)
+            diag = jnp.where(odd, diag - ratio * side, diag)
             outs.append(unit * lax.rsqrt(diag))
             logs = logs + jnp.log(diag)
         results.append((outs, 0.5 * jnp.sum(logs, axis=0, keepdims=True)))
     return results
 
 
-def project_kernel(own_ref, other_ref, fields_ref, out_ref):
+def copies_of(fields_ref, out_ref, sems):
+    rows = fields_ref.shape[0] // CHUNKS
+    return [
+        pltpu.make_async_copy(
+            fields_ref.at[pl.ds(rows * i, rows)], out_ref.at[pl.ds(rows * i, rows)], sems.at[i])
+        for i in range(CHUNKS)]
+
+
+def project_kernel(own_ref, other_ref, fields_ref, out_ref, held_ref, sems):
+    copies = copies_of(fields_ref, held_ref, sems)
+    for copy in copies:
+        copy.start()
     core = lax.axis_index("core")
     parts = []
     for z in range(8):
         own, other = own_ref[z], other_ref[z]
         parts += [by_core(core, own, other), by_core(core, other, own)]
     patterns = jnp.concatenate(parts, axis=1)
-    for c in range(4):
+    for c in range(CHUNKS):
+        copies[c].wait()
         part = lax.dot_general(
-            patterns, fields_ref[256 * c:256 * c + 256, :], (((1,), (1,)), ((), ())),
-            preferred_element_type=F32)
-        at = 256 * (c % 2)
+            held_ref[128 * c:128 * c + 128, :], patterns, (((1,), (1,)), ((), ())),
+            preferred_element_type=F32).T
+        at = 128 * (c % 4)
         for b in range(8):
-            out_ref[2 * b + c // 2, :, at:at + 256] = part[8 * b:8 * b + 8, :]
+            out_ref[2 * b + c // 4, :, at:at + 128] = part[8 * b:8 * b + 8, :]
 
 
 def read_pcs(pcs_ref):
@@ -248,7 +277,11 @@
     moments(core, centred_of, resp, out_keep_ref, out_send_ref)
 
 
-def last_kernel(pcs_ref, keep_ref, got_ref, fields_ref, member_ref, terms_ref, means_ref, weights_ref):
+def last_kernel(pcs_ref, keep_ref, got_ref, fields_ref, member_ref, terms_ref, means_ref, weights_ref,
+                held_ref, sems):
+    copies = copies_of(fields_ref, held_ref, sems)
+    for copy in copies:
+        copy.start()
     core = lax.axis_index("core")
     pcs = read_pcs(pcs_ref)
     halves = halves_of(core, keep_ref, got_ref)
@@ -262,8 +295,10 @@
     means_ref[...] = jnp.concatenate(means, axis=0)
     count = jnp.broadcast_to(jnp.sum(member, axis=1, keepdims=True), (R, 128))
     rounded = member.astype(BF16)
+    for copy in copies:
+        copy.wait()
     for j in range(16):
-        terms_ref[j, :, 0:256] = jnp.dot(rounded, fields_ref[:, 256 * j:256 * j + 256], preferred_element_type=F32)
+        terms_ref[j, :, 0:256] = jnp.dot(rounded, held_ref[:, 256 * j:256 * j + 256], preferred_element_type=F32)
         terms_ref[j, :, 256:384] = count
 
 
@@ -282,7 +317,9 @@
     core = lax.axis_index("core")
     own = lax.all_to_all(spread(eofs, 8), "z", 0, 0)
     other = lax.ppermute(own, "core", SWAP)
-    partial, = call(project_kernel, [((16, 8, days // 2), F32)], [own, other, anomalies])
+    held = [pltpu.VMEM(anomalies.shape, anomalies.dtype), pltpu.SemaphoreType.DMA((CHUNKS,))]
+    partial, = call(
+        project_kernel, [((16, 8, days // 2), F32)], [own, other, anomalies], scratch=held, stay=1)
     mine = jnp.sum(lax.all_to_all(partial, "grid", 0, 0), axis=0)
     pcs = lax.all_to_all(spread(mine, 16), "grid", 0, 0)
 
@@ -303,7 +340,8 @@
     member, terms, means, weights = call(
         last_kernel,
         [((R, days), F32), ((16, R, 384), F32), ((R, K), F32), ((R, 128), F32)],
-        [pcs, block, got, anomalies])
+        [pcs, block, got, anomalies],
+        scratch=held, stay=1)
     sums = jnp.sum(lax.all_to_all(terms, ("z", "core"), 0, 0), axis=0)
     composites = (sums[:, :256] / jnp.maximum(sums[:, 256:257], 1.0)).astype(BF16)
 

time: 141 us -> 136 us (0.965)
  Pallas kernels: 31.7 us -> 27.3 us
    pallas_call x6, Pallas kernels: 31.7 us -> 27.3 us  [call(): pl.pallas_call(kernel, out_shape=tuple((jax.ShapeDtypeStruct(s, d) for s,...]
where the time goes in v3:
time: 136 us
  waiting for transfers between devices  53 us (39%)
  starting transfers between devices  28.1 us (21%)
  Pallas kernels  27.3 us (20%)
  blocking collectives  19.2 us (14%)
  local copies, waits for them, and re-layouts  4.74 us (3%)
  other arithmetic  2.43 us (2%)
    pallas_call x6, Pallas kernels, call(): pl.pallas_call(kernel, out_shape=tuple((jax.ShapeDtypeStruct(s, d) for s,...  27.3 us
    all_to_all x2, waiting for transfers between devices, merge(): parts = lax.all_to_all(spread(half, 8), 'z', 0, 0)  25.8 us
    all_to_all x1, blocking collectives, body(): own = lax.all_to_all(spread(eofs, 8), 'z', 0, 0)  19.2 us
    all_to_all x1, waiting for transfers between devices, body(): mine = jnp.sum(lax.all_to_all(partial, 'grid', 0, 0), axis=0)  7.98 us
    all_to_all x1, waiting for transfers between devices, body(): sums = jnp.sum(lax.all_to_all(terms, ('z', 'core'), 0, 0), axis=0)  7.47 us
    all_to_all x2, starting transfers between devices, merge(): parts = lax.all_to_all(spread(half, 8), 'z', 0, 0)  6.84 us
    all_to_all x1, starting transfers between devices, body(): mine = jnp.sum(lax.all_to_all(partial, 'grid', 0, 0), axis=0)  6.77 us
    all_to_all x1, waiting for transfers between devices, body(): pcs = lax.all_to_all(spread(mine, 16), 'grid', 0, 0)  6.16 us
  transfers between devices with their start and end apart: 11, of which 11 were waited for; matrix products, arithmetic and copies ran while one was open for 2% of the time, Pallas kernels for 0%

profile of v3, /device:TPU:1, one launch (start us, length us, event | category | flops | bytes accessed | tf_op | source)
XLA Modules:
  0.0 135.5 jit_solution(4520115294691298563)
XLA Ops:
  0.7 0.8 broadcast_in_dim.10
  1.5 19.2 %all_to_all.30.own_ref = bf16[8,64,256]{2,1,0:T(8,128)(2,1)S(1)} all-to-all(bf16[8,64,256]{2,1,0:T(8,128)(2,1)S(1)} %broadcast_in_dim.10), channel_id=1, replica_groups=mesh['grid'=16,'z'=8,'core'=2] {'z'}, dimensions={0} | all-to-all | bytes 524288 | tf_op jit(solution)/shard_map/all_to_all | solution.py:318
  20.6 2.5 %collective-permute-start = (bf16[8,64,256]{2,1,0:T(8,128)(2,1)S(1)}, bf16[8,64,256]{2,1,0:T(8,128)(2,1)S(1)}, u32[]{:S(2)}, u32[]{:S(2)}) collective-permute-start(bf16[8,64,256]{2,1,0:T(8,128)(2,1)S(1)} %all_to_all.30.own_ref), channel_id=1, source_target_pairs={{0,1},{1,0},{2,3},{3,2},{4,5},{5,4},{6,7},{7,6},{8,9},{9,8},{10,11... | collective-permute-start | bytes 786440 | tf_op jit(solution)/shard_map/ppermute | solution.py:319
  23.1 1.2 collective-permute-done.other_ref
  24.3 7.8 %shard_map.92 = f32[16,8,512]{2,1,0:T(8,128)} custom-call(bf16[8,64,256]{2,1,0:T(8,128)(2,1)S(1)} %all_to_all.30.own_ref, bf16[8,64,256]{2,1,0:T(8,128)(2,1)S(1)} %collective-permute-done.other_ref, bf16[1024,4096]{1,0:T(8,128)(2,1)} %fields_ref.3), custom_call_target="tpu_custom_call" | custom-call | tf_op jit(solution)/shard_map/pallas_call | solution.py:26
  32.0 6.8 %all-to-all-start.1 = ((f32[16,8,512]{2,1,0:T(8,128)}), f32[16,8,512]{2,1,0:T(8,128)S(1)}, u32[]{:S(2)}, u32[]{:S(2)}) async-start(f32[16,8,512]{2,1,0:T(8,128)} %shard_map.92), calls=%async_computation.1 | async-start | bytes 524288 | tf_op jit(solution)/shard_map/all_to_all | solution.py:323
  38.9 8.0 %all-to-all-done.1 = f32[16,8,512]{2,1,0:T(8,128)S(1)} async-done(((f32[16,8,512]{2,1,0:T(8,128)}), f32[16,8,512]{2,1,0:T(8,128)S(1)}, u32[]{:S(2)}, u32[]{:S(2)}) %all-to-all-start.1) | async-done | bytes 262176 | tf_op jit(solution)/shard_map/all_to_all | solution.py:323
  46.9 0.7 broadcast_in_dim.11
  47.7 3.5 %all-to-all-start.2 = ((f32[16,8,512]{2,1,0:T(8,128)}), f32[16,8,512]{2,1,0:T(8,128)S(1)}, u32[]{:S(2)}, u32[]{:S(2)}) async-start(f32[16,8,512]{2,1,0:T(8,128)} %broadcast_in_dim.11), calls=%async_computation.2 | async-start | bytes 524288 | tf_op jit(solution)/shard_map/all_to_all | solution.py:324
  52.6 6.2 %all-to-all-done.2.pcs_ref = f32[16,8,512]{2,1,0:T(8,128)S(1)} async-done(((f32[16,8,512]{2,1,0:T(8,128)}), f32[16,8,512]{2,1,0:T(8,128)S(1)}, u32[]{:S(2)}, u32[]{:S(2)}) %all-to-all-start.2) | async-done | bytes 262176 | tf_op jit(solution)/shard_map/all_to_all | solution.py:324
  58.8 2.8 %shard_map.93 = (f32[72,128]{1,0:T(8,128)S(1)}, f32[72,128]{1,0:T(8,128)S(1)}) custom-call(f32[16,8,512]{2,1,0:T(8,128)S(1)} %all-to-all-done.2.pcs_ref, f32[8,128]{1,0:T(8,128)S(1)} %pad_maximum_fusion.params_ref, f32[8,128]{1,0:T(8,128)S(1)} %broadcast_in_dim.12.base_ref), custom_call_target="tpu_custom_call" | custom-call | tf_op jit(solution)/shard_map/pallas_call | solution.py:26
  61.5 2.8 %collective-permute-start.1 = (f32[72,128]{1,0:T(8,128)S(1)}, f32[72,128]{1,0:T(8,128)S(1)}, u32[]{:S(2)}, u32[]{:S(2)}) collective-permute-start(f32[72,128]{1,0:T(8,128)S(1)} %get-tuple-element.17), channel_id=1, source_target_pairs={{0,1},{1,0},{2,3},{3,2},{4,5},{5,4},{6,7},{7,6},{8,9},{9,8},{10,11... | collective-permute-start | bytes 110600 | tf_op jit(solution)/shard_map/ppermute | solution.py:310
  64.3 0.9 collective-permute-done.1
  65.2 0.7 broadcast_in_dim.13
  65.9 3.4 %all-to-all-start.3 = ((f32[8,72,128]{2,1,0:T(8,128)}), f32[8,72,128]{2,1,0:T(8,128)S(1)}, u32[]{:S(2)}, u32[]{:S(2)}) async-start(f32[8,72,128]{2,1,0:T(8,128)} %broadcast_in_dim.13), calls=%async_computation.3 | async-start | bytes 589824 | tf_op jit(solution)/shard_map/all_to_all | solution.py:311
  69.4 12.9 %all-to-all-done.3.parts_ref = f32[8,72,128]{2,1,0:T(8,128)S(1)} async-done(((f32[8,72,128]{2,1,0:T(8,128)}), f32[8,72,128]{2,1,0:T(8,128)S(1)}, u32[]{:S(2)}, u32[]{:S(2)}) %all-to-all-start.3) | async-done | bytes 294944 | tf_op jit(solution)/shard_map/all_to_all | solution.py:311
  82.3 3.4 %shard_map.94 = (f32[136,128]{1,0:T(8,128)S(1)}, f32[128,128]{1,0:T(8,128)}) custom-call(f32[8,72,128]{2,1,0:T(8,128)S(1)} %all-to-all-done.3.parts_ref, f32[2,128]{1,0:T(2,128)S(1)} %select_n.21.shift_ref), custom_call_target="tpu_custom_call" | custom-call | tf_op jit(solution)/shard_map/pallas_call | solution.py:26
  85.8 0.7 collective-permute-start.2
  86.5 0.9 collective-permute-done.2.got_ref
  87.4 4.0 %shard_map.95 = (f32[72,128]{1,0:T(8,128)S(1)}, f32[72,128]{1,0:T(8,128)S(1)}) custom-call(f32[16,8,512]{2,1,0:T(8,128)S(1)} %all-to-all-done.2.pcs_ref, f32[136,128]{1,0:T(8,128)S(1)} %get-tuple-element.18.keep_ref, f32[136,128]{1,0:T(8,128)S(1)} %collective-permute-done.2.got_ref), custom_call_target="tpu_custom_call" | custom-call | tf_op jit(solution)/shard_map/pallas_call | solution.py:26
  91.8 0.9 collective-permute-done.3
  92.7 0.7 broadcast_in_dim.14
  93.4 3.4 %all-to-all-start.4 = ((f32[8,72,128]{2,1,0:T(8,128)}), f32[8,72,128]{2,1,0:T(8,128)S(1)}, u32[]{:S(2)}, u32[]{:S(2)}) async-start(f32[8,72,128]{2,1,0:T(8,128)} %broadcast_in_dim.14), calls=%async_computation.4 | async-start | bytes 589824 | tf_op jit(solution)/shard_map/all_to_all | solution.py:311
  96.9 13.0 %all-to-all-done.4.parts_ref = f32[8,72,128]{2,1,0:T(8,128)S(1)} async-done(((f32[8,72,128]{2,1,0:T(8,128)}), f32[8,72,128]{2,1,0:T(8,128)S(1)}, u32[]{:S(2)}, u32[]{:S(2)}) %all-to-all-start.4) | async-done | bytes 294944 | tf_op jit(solution)/shard_map/all_to_all | solution.py:311
  109.8 3.4 %shard_map.96 = (f32[136,128]{1,0:T(8,128)S(1)}, f32[128,128]{1,0:T(8,128)S(1)}) custom-call(f32[8,72,128]{2,1,0:T(8,128)S(1)} %all-to-all-done.4.parts_ref, f32[2,128]{1,0:T(2,128)S(1)} %slice.22.shift_ref), custom_call_target="tpu_custom_call" | custom-call | tf_op jit(solution)/shard_map/pallas_call | solution.py:26
  113.9 0.9 collective-permute-done.4.got_ref
  114.8 5.9 %shard_map.97 = (f32[8,1024]{1,0:T(8,128)}, f32[16,8,384]{2,1,0:T(8,128)}, f32[8,64]{1,0:T(8,128)}, f32[8,128]{1,0:T(8,128)S(1)}) custom-call(f32[16,8,512]{2,1,0:T(8,128)S(1)} %all-to-all-done.2.pcs_ref, f32[136,128]{1,0:T(8,128)S(1)} %get-tuple-element.21.keep_ref, f32[136,128]{1,0:T(8,128)S(1)} %collective-permute-done.4.got_ref, ...), custom_call_target="tpu_custom_call" | custom-call | tf_op jit(solution)/shard_map/pallas_call | solution.py:26
  120.7 3.7 %all-to-all-start.5 = ((f32[16,8,384]{2,1,0:T(8,128)}), f32[16,8,384]{2,1,0:T(8,128)S(1)}, u32[]{:S(2)}, u32[]{:S(2)}) async-start(f32[16,8,384]{2,1,0:T(8,128)} %get-tuple-element.26), calls=%async_computation.5 | async-start | bytes 393216 | tf_op jit(solution)/shard_map/all_to_all | solution.py:345
  124.8 0.8 collective-permute-done.5
  125.9 0.7 copy.13
  127.2 7.5 %all-to-all-done.5 = f32[16,8,384]{2,1,0:T(8,128)S(1)} async-done(((f32[16,8,384]{2,1,0:T(8,128)}), f32[16,8,384]{2,1,0:T(8,128)S(1)}, u32[]{:S(2)}, u32[]{:S(2)}) %all-to-all-start.5) | async-done | bytes 196640 | tf_op jit(solution)/shard_map/all_to_all | solution.py:345
  134.8 0.7 fusion.1
  (27 shorter events, 4.1 us)
Async XLA Ops:
  0.6 38.2 %copy-start = (f32[8,64]{1,0:T(8,128)S(1)}, f32[8,64]{1,0:T(8,128)}, u32[]{:S(2)}) copy-start(f32[8,64]{1,0:T(8,128)} %param.8) | copy-start | bytes 6148
  0.6 50.6 %copy-start.1 = (f32[8,64]{1,0:T(8,128)S(1)}, f32[8,64]{1,0:T(8,128)}, u32[]{:S(2)}) copy-start(f32[8,64]{1,0:T(8,128)} %param.7) | copy-start | bytes 6148
  0.7 50.6 %copy-start.2 = (f32[8]{0:T(128)S(1)}, f32[8]{0:T(128)}, u32[]{:S(2)}) copy-start(f32[8]{0:T(128)} %param.9) | copy-start | bytes 100
  20.6 3.6 %collective-permute-start = (bf16[8,64,256]{2,1,0:T(8,128)(2,1)S(1)}, bf16[8,64,256]{2,1,0:T(8,128)(2,1)S(1)}, u32[]{:S(2)}, u32[]{:S(2)}) collective-permute-start(bf16[8,64,256]{2,1,0:T(8,128)(2,1)S(1)} %all_to_all.30.own_ref), channel_id=1, source_target_pairs={{0,1},{1,0},{2,3},{3,2},{4,5},{5,4},{6,7},{7,6},{8,9},{9,8},{10,11... | collective-permute-start | bytes 786440 | tf_op jit(solution)/shard_map/ppermute | solution.py:319
  32.0 14.9 %all-to-all-start.1 = ((f32[16,8,512]{2,1,0:T(8,128)}), f32[16,8,512]{2,1,0:T(8,128)S(1)}, u32[]{:S(2)}, u32[]{:S(2)}) async-start(f32[16,8,512]{2,1,0:T(8,128)} %shard_map.92), calls=%async_computation.1 | async-start | bytes 524288 | tf_op jit(solution)/shard_map/all_to_all | solution.py:323
  47.7 11.0 %all-to-all-start.2 = ((f32[16,8,512]{2,1,0:T(8,128)}), f32[16,8,512]{2,1,0:T(8,128)S(1)}, u32[]{:S(2)}, u32[]{:S(2)}) async-start(f32[16,8,512]{2,1,0:T(8,128)} %broadcast_in_dim.11), calls=%async_computation.2 | async-start | bytes 524288 | tf_op jit(solution)/shard_map/all_to_all | solution.py:324
  61.5 3.6 %collective-permute-start.1 = (f32[72,128]{1,0:T(8,128)S(1)}, f32[72,128]{1,0:T(8,128)S(1)}, u32[]{:S(2)}, u32[]{:S(2)}) collective-permute-start(f32[72,128]{1,0:T(8,128)S(1)} %get-tuple-element.17), channel_id=1, source_target_pairs={{0,1},{1,0},{2,3},{3,2},{4,5},{5,4},{6,7},{7,6},{8,9},{9,8},{10,11... | collective-permute-start | bytes 110600 | tf_op jit(solution)/shard_map/ppermute | solution.py:310
  65.9 16.4 %all-to-all-start.3 = ((f32[8,72,128]{2,1,0:T(8,128)}), f32[8,72,128]{2,1,0:T(8,128)S(1)}, u32[]{:S(2)}, u32[]{:S(2)}) async-start(f32[8,72,128]{2,1,0:T(8,128)} %broadcast_in_dim.13), calls=%async_computation.3 | async-start | bytes 589824 | tf_op jit(solution)/shard_map/all_to_all | solution.py:311
  85.8 1.6 %collective-permute-start.2 = (f32[136,128]{1,0:T(8,128)S(1)}, f32[136,128]{1,0:T(8,128)S(1)}, u32[]{:S(2)}, u32[]{:S(2)}) collective-permute-start(f32[136,128]{1,0:T(8,128)S(1)} %get-tuple-element.18.keep_ref), channel_id=1, source_target_pairs={{0,1},{1,0},{2,3},{3,2},{4,5},{5,4},{6,7},{7,6},{8,9},{9,8},{10,11... | collective-permute-start | bytes 208904 | tf_op jit(solution)/shard_map/ppermute | solution.py:335
  91.4 1.3 collective-permute-start.3
  93.4 16.4 %all-to-all-start.4 = ((f32[8,72,128]{2,1,0:T(8,128)}), f32[8,72,128]{2,1,0:T(8,128)S(1)}, u32[]{:S(2)}, u32[]{:S(2)}) async-start(f32[8,72,128]{2,1,0:T(8,128)} %broadcast_in_dim.14), calls=%async_computation.4 | async-start | bytes 589824 | tf_op jit(solution)/shard_map/all_to_all | solution.py:311
  113.3 1.5 %collective-permute-start.4 = (f32[136,128]{1,0:T(8,128)S(1)}, f32[136,128]{1,0:T(8,128)S(1)}, u32[]{:S(2)}, u32[]{:S(2)}) collective-permute-start(f32[136,128]{1,0:T(8,128)S(1)} %get-tuple-element.21.keep_ref), channel_id=1, source_target_pairs={{0,1},{1,0},{2,3},{3,2},{4,5},{5,4},{6,7},{7,6},{8,9},{9,8},{10,11... | collective-permute-start | bytes 208904 | tf_op jit(solution)/shard_map/ppermute | solution.py:338
  120.7 14.1 %all-to-all-start.5 = ((f32[16,8,384]{2,1,0:T(8,128)}), f32[16,8,384]{2,1,0:T(8,128)S(1)}, u32[]{:S(2)}, u32[]{:S(2)}) async-start(f32[16,8,384]{2,1,0:T(8,128)} %get-tuple-element.26), calls=%async_computation.5 | async-start | bytes 393216 | tf_op jit(solution)/shard_map/all_to_all | solution.py:345
  124.3 1.3 collective-permute-start.5

commit v4 on v3

--- a/solution.py
+++ b/solution.py
@@ -17,19 +17,19 @@
 SWAP = [(0, 1), (1, 0)]
 ROWS = K + 8
 LIMIT = 48 * 1024 * 1024
-CHUNKS = 8
+SMALL = 16 * 1024 * 1024
+COVER = pl.CostEstimate(flops=20 * 10 ** 10, transcendentals=0, bytes_accessed=0)
 VMEM = pl.BlockSpec(memory_space=pltpu.VMEM)
-HBM = pl.BlockSpec(memory_space=pltpu.HBM)
-
-
-def call(kernel, outs, operands, scratch=(), stay=0):
+
+
+def call(kernel, outs, operands, limit=LIMIT, cost=None):
     return pl.pallas_call(
         kernel,
         out_shape=tuple(jax.ShapeDtypeStruct(s, d) for s, d in outs),
-        in_specs=[VMEM] * (len(operands) - stay) + [HBM] * stay,
+        in_specs=[VMEM] * len(operands),
         out_specs=tuple([VMEM] * len(outs)),
-        scratch_shapes=scratch,
-        compiler_params=pltpu.CompilerParams(vmem_limit_bytes=LIMIT),
+        compiler_params=pltpu.CompilerParams(vmem_limit_bytes=limit),
+        cost_estimate=cost,
     )(*operands)
 
 
@@ -89,32 +89,25 @@
     return results
 
 
-def copies_of(fields_ref, out_ref, sems):
-    rows = fields_ref.shape[0] // CHUNKS
-    return [
-        pltpu.make_async_copy(
-            fields_ref.at[pl.ds(rows * i, rows)], out_ref.at[pl.ds(rows * i, rows)], sems.at[i])
-        for i in range(CHUNKS)]
-
-
-def project_kernel(own_ref, other_ref, fields_ref, out_ref, held_ref, sems):
-    copies = copies_of(fields_ref, held_ref, sems)
-    for copy in copies:
-        copy.start()
+def spread_kernel(patterns_ref, out_ref):
+    for z in range(8):
+        out_ref[z] = patterns_ref[...]
+
+
+def project_kernel(own_ref, other_ref, fields_ref, out_ref):
     core = lax.axis_index("core")
     parts = []
     for z in range(8):
         own, other = own_ref[z], other_ref[z]
         parts += [by_core(core, own, other), by_core(core, other, own)]
     patterns = jnp.concatenate(parts, axis=1)
-    for c in range(CHUNKS):
-        copies[c].wait()
-        part = lax.dot_general(
-            held_ref[128 * c:128 * c + 128, :], patterns, (((1,), (1,)), ((), ())),
-            preferred_element_type=F32).T
-        at = 128 * (c % 4)
-        for b in range(8):
-            out_ref[2 * b + c // 4, :, at:at + 128] = part[8 * b:8 * b + 8, :]
+    part = lax.dot_general(
+        fields_ref[...], patterns, (((1,), (1,)), ((), ())), preferred_element_type=F32)
+    days = part.shape[0] // 2
+    part = jnp.concatenate([part[:days], part[days:]], axis=1).T
+    for b in range(8):
+        out_ref[2 * b] = part[8 * b:8 * b + 8]
+        out_ref[2 * b + 1] = part[K + 8 * b:K + 8 * b + 8]
 
 
 def read_pcs(pcs_ref):
@@ -277,11 +270,7 @@
     moments(core, centred_of, resp, out_keep_ref, out_send_ref)
 
 
-def last_kernel(pcs_ref, keep_ref, got_ref, fields_ref, member_ref, terms_ref, means_ref, weights_ref,
-                held_ref, sems):
-    copies = copies_of(fields_ref, held_ref, sems)
-    for copy in copies:
-        copy.start()
+def last_kernel(pcs_ref, keep_ref, got_ref, fields_ref, member_ref, terms_ref, means_ref, weights_ref):
     core = lax.axis_index("core")
     pcs = read_pcs(pcs_ref)
     halves = halves_of(core, keep_ref, got_ref)
@@ -295,10 +284,8 @@
     means_ref[...] = jnp.concatenate(means, axis=0)
     count = jnp.broadcast_to(jnp.sum(member, axis=1, keepdims=True), (R, 128))
     rounded = member.astype(BF16)
-    for copy in copies:
-        copy.wait()
     for j in range(16):
-        terms_ref[j, :, 0:256] = jnp.dot(rounded, held_ref[:, 256 * j:256 * j + 256], preferred_element_type=F32)
+        terms_ref[j, :, 0:256] = jnp.dot(rounded, fields_ref[:, 256 * j:256 * j + 256], preferred_element_type=F32)
         terms_ref[j, :, 256:384] = count
 
 
@@ -309,17 +296,20 @@
 def merge(keep, send, shift):
     half = keep + lax.ppermute(send, "core", SWAP)
     parts = lax.all_to_all(spread(half, 8), "z", 0, 0)
-    return call(merge_kernel, [((2 * K + 8, 128), F32), ((2 * K, 128), F32)], [parts, shift])
+    return call(merge_kernel, [((2 * K + 8, 128), F32), ((2 * K, 128), F32)], [parts, shift],
+                limit=SMALL, cost=COVER)
 
 
 def body(anomalies, eofs, means_init, variances, mixing):
     days = anomalies.shape[0]
     core = lax.axis_index("core")
-    own = lax.all_to_all(spread(eofs, 8), "z", 0, 0)
+    eight, = call(
+        spread_kernel, [((8,) + eofs.shape, BF16)], [eofs], limit=SMALL,
+        cost=COVER)
+    own = lax.all_to_all(eight, "z", 0, 0)
     other = lax.ppermute(own, "core", SWAP)
-    held = [pltpu.VMEM(anomalies.shape, anomalies.dtype), pltpu.SemaphoreType.DMA((CHUNKS,))]
     partial, = call(
-        project_kernel, [((16, 8, days // 2), F32)], [own, other, anomalies], scratch=held, stay=1)
+        project_kernel, [((16, 8, days // 2), F32)], [own, other, anomalies], limit=SMALL)
     mine = jnp.sum(lax.all_to_all(partial, "grid", 0, 0), axis=0)
     pcs = lax.all_to_all(spread(mine, 16), "grid", 0, 0)
 
@@ -341,7 +331,7 @@
         last_kernel,
         [((R, days), F32), ((16, R, 384), F32), ((R, K), F32), ((R, 128), F32)],
         [pcs, block, got, anomalies],
-        scratch=held, stay=1)
+        limit=SMALL)
     sums = jnp.sum(lax.all_to_all(terms, ("z", "core"), 0, 0), axis=0)
     composites = (sums[:, :256] / jnp.maximum(sums[:, 256:257], 1.0)).astype(BF16)
 

time: 136 us -> 130 us (0.956)
  Pallas kernels: 27.3 us -> 20.6 us
    pallas_call x6 -> x7, Pallas kernels: 27.3 us -> 20.6 us  [call(): pl.pallas_call(kernel, out_shape=tuple((jax.ShapeDtypeStruct(s, d) for s,...]
    broadcast_in_dim x4 -> x3, local copies, waits for them, and re-layouts: 2.97 us -> 2.2 us  [spread(): return jnp.broadcast_to(x[None], (n,) + x.shape)]
  transfers between devices with their start and end apart: 11 -> 11, of which waited for: 11 -> 11; matrix products, arithmetic and copies ran while one was open for 2% -> 3% of each run, Pallas kernels for 0% -> 0%
where the time goes in v4:
time: 130 us; the launch traced here: 129 us
  waiting for transfers between devices  53 us (41%)
  starting transfers between devices  28 us (22%)
  Pallas kernels  20.6 us (16%)
  blocking collectives  19.4 us (15%)
  local copies, waits for them, and re-layouts  4.74 us (4%)
  other arithmetic  2.43 us (2%)
    all_to_all x2, waiting for transfers between devices, merge(): parts = lax.all_to_all(spread(half, 8), 'z', 0, 0)  25.8 us
    pallas_call x7, Pallas kernels, call(): pl.pallas_call(kernel, out_shape=tuple((jax.ShapeDtypeStruct(s, d) for s,...  20.6 us
    all_to_all x1, blocking collectives, body(): own = lax.all_to_all(eight, 'z', 0, 0)  19.4 us
    all_to_all x1, waiting for transfers between devices, body(): mine = jnp.sum(lax.all_to_all(partial, 'grid', 0, 0), axis=0)  7.99 us
    all_to_all x1, waiting for transfers between devices, body(): sums = jnp.sum(lax.all_to_all(terms, ('z', 'core'), 0, 0), axis=0)  7.47 us
    all_to_all x2, starting transfers between devices, merge(): parts = lax.all_to_all(spread(half, 8), 'z', 0, 0)  6.84 us
    all_to_all x1, starting transfers between devices, body(): mine = jnp.sum(lax.all_to_all(partial, 'grid', 0, 0), axis=0)  6.75 us
    all_to_all x1, waiting for transfers between devices, body(): pcs = lax.all_to_all(spread(mine, 16), 'grid', 0, 0)  6.16 us
  transfers between devices with their start and end apart: 11, of which 11 were waited for; matrix products, arithmetic and copies ran while one was open for 3% of the time, Pallas kernels for 0%

profile of v4, /device:TPU:1, one launch (start us, length us, event | category | flops | bytes accessed | tf_op | source)
XLA Modules:
  0.0 129.1 jit_solution(2311114182885579929)
XLA Ops:
  0.6 0.7 copy-done.2
  1.4 19.4 %all_to_all.30.own_ref = bf16[8,64,256]{2,1,0:T(8,128)(2,1)S(1)} all-to-all(bf16[8,64,256]{2,1,0:T(8,128)(2,1)S(1)} %shard_map.92), channel_id=1, replica_groups=mesh['grid'=16,'z'=8,'core'=2] {'z'}, dimensions={0} | all-to-all | bytes 524288 | tf_op jit(solution)/shard_map/all_to_all | solution.py:309
  20.9 2.5 %collective-permute-start = (bf16[8,64,256]{2,1,0:T(8,128)(2,1)S(1)}, bf16[8,64,256]{2,1,0:T(8,128)(2,1)S(1)}, u32[]{:S(2)}, u32[]{:S(2)}) collective-permute-start(bf16[8,64,256]{2,1,0:T(8,128)(2,1)S(1)} %all_to_all.30.own_ref), channel_id=1, source_target_pairs={{0,1},{1,0},{2,3},{3,2},{4,5},{5,4},{6,7},{7,6},{8,9},{9,8},{10,11... | collective-permute-start | bytes 786440 | tf_op jit(solution)/shard_map/ppermute | solution.py:310
  23.4 1.2 collective-permute-done.other_ref
  24.5 3.2 %shard_map.93 = f32[16,8,512]{2,1,0:T(8,128)} custom-call(bf16[8,64,256]{2,1,0:T(8,128)(2,1)S(1)} %all_to_all.30.own_ref, bf16[8,64,256]{2,1,0:T(8,128)(2,1)S(1)} %collective-permute-done.other_ref, bf16[1024,4096]{1,0:T(8,128)(2,1)S(1)} %copy-done), custom_call_target="tpu_custom_call" | custom-call | tf_op jit(solution)/shard_map/pallas_call | solution.py:26
  27.7 6.8 %all-to-all-start.1 = ((f32[16,8,512]{2,1,0:T(8,128)}), f32[16,8,512]{2,1,0:T(8,128)S(1)}, u32[]{:S(2)}, u32[]{:S(2)}) async-start(f32[16,8,512]{2,1,0:T(8,128)} %shard_map.93), calls=%async_computation.1 | async-start | bytes 524288 | tf_op jit(solution)/shard_map/all_to_all | solution.py:313
  34.6 8.0 %all-to-all-done.1 = f32[16,8,512]{2,1,0:T(8,128)S(1)} async-done(((f32[16,8,512]{2,1,0:T(8,128)}), f32[16,8,512]{2,1,0:T(8,128)S(1)}, u32[]{:S(2)}, u32[]{:S(2)}) %all-to-all-start.1) | async-done | bytes 262176 | tf_op jit(solution)/shard_map/all_to_all | solution.py:313
  42.6 0.7 broadcast_in_dim.8
  43.4 3.5 %all-to-all-start.2 = ((f32[16,8,512]{2,1,0:T(8,128)}), f32[16,8,512]{2,1,0:T(8,128)S(1)}, u32[]{:S(2)}, u32[]{:S(2)}) async-start(f32[16,8,512]{2,1,0:T(8,128)} %broadcast_in_dim.8), calls=%async_computation.2 | async-start | bytes 524288 | tf_op jit(solution)/shard_map/all_to_all | solution.py:314
  48.3 6.2 %all-to-all-done.2.pcs_ref = f32[16,8,512]{2,1,0:T(8,128)S(1)} async-done(((f32[16,8,512]{2,1,0:T(8,128)}), f32[16,8,512]{2,1,0:T(8,128)S(1)}, u32[]{:S(2)}, u32[]{:S(2)}) %all-to-all-start.2) | async-done | bytes 262176 | tf_op jit(solution)/shard_map/all_to_all | solution.py:314
  54.5 2.8 %shard_map.94 = (f32[72,128]{1,0:T(8,128)S(1)}, f32[72,128]{1,0:T(8,128)S(1)}) custom-call(f32[16,8,512]{2,1,0:T(8,128)S(1)} %all-to-all-done.2.pcs_ref, f32[8,128]{1,0:T(8,128)S(1)} %pad_maximum_fusion.params_ref, f32[8,128]{1,0:T(8,128)S(1)} %broadcast_in_dim.9.base_ref), custom_call_target="tpu_custom_call" | custom-call | tf_op jit(solution)/shard_map/pallas_call | solution.py:26
  57.2 2.8 %collective-permute-start.1 = (f32[72,128]{1,0:T(8,128)S(1)}, f32[72,128]{1,0:T(8,128)S(1)}, u32[]{:S(2)}, u32[]{:S(2)}) collective-permute-start(f32[72,128]{1,0:T(8,128)S(1)} %get-tuple-element.17), channel_id=1, source_target_pairs={{0,1},{1,0},{2,3},{3,2},{4,5},{5,4},{6,7},{7,6},{8,9},{9,8},{10,11... | collective-permute-start | bytes 110600 | tf_op jit(solution)/shard_map/ppermute | solution.py:297
  60.0 0.9 collective-permute-done.1
  60.9 0.7 broadcast_in_dim.10
  61.6 3.4 %all-to-all-start.3 = ((f32[8,72,128]{2,1,0:T(8,128)}), f32[8,72,128]{2,1,0:T(8,128)S(1)}, u32[]{:S(2)}, u32[]{:S(2)}) async-start(f32[8,72,128]{2,1,0:T(8,128)} %broadcast_in_dim.10), calls=%async_computation.3 | async-start | bytes 589824 | tf_op jit(solution)/shard_map/all_to_all | solution.py:298
  65.2 12.9 %all-to-all-done.3.parts_ref = f32[8,72,128]{2,1,0:T(8,128)S(1)} async-done(((f32[8,72,128]{2,1,0:T(8,128)}), f32[8,72,128]{2,1,0:T(8,128)S(1)}, u32[]{:S(2)}, u32[]{:S(2)}) %all-to-all-start.3) | async-done | bytes 294944 | tf_op jit(solution)/shard_map/all_to_all | solution.py:298
  78.0 3.4 %shard_map.95 = (f32[136,128]{1,0:T(8,128)S(1)}, f32[128,128]{1,0:T(8,128)}) custom-call(f32[8,72,128]{2,1,0:T(8,128)S(1)} %all-to-all-done.3.parts_ref, f32[2,128]{1,0:T(2,128)S(1)} %select_n.21.shift_ref), custom_call_target="tpu_custom_call" | custom-call | flops 199999995904 | tf_op jit(solution)/shard_map/pallas_call | solution.py:26
  81.5 0.7 collective-permute-start.2
  82.2 0.9 collective-permute-done.2.got_ref
  83.1 4.0 %shard_map.96 = (f32[72,128]{1,0:T(8,128)S(1)}, f32[72,128]{1,0:T(8,128)S(1)}) custom-call(f32[16,8,512]{2,1,0:T(8,128)S(1)} %all-to-all-done.2.pcs_ref, f32[136,128]{1,0:T(8,128)S(1)} %get-tuple-element.18.keep_ref, f32[136,128]{1,0:T(8,128)S(1)} %collective-permute-done.2.got_ref), custom_call_target="tpu_custom_call" | custom-call | tf_op jit(solution)/shard_map/pallas_call | solution.py:26
  87.6 0.9 collective-permute-done.3
  88.4 0.7 broadcast_in_dim.11
  89.2 3.4 %all-to-all-start.4 = ((f32[8,72,128]{2,1,0:T(8,128)}), f32[8,72,128]{2,1,0:T(8,128)S(1)}, u32[]{:S(2)}, u32[]{:S(2)}) async-start(f32[8,72,128]{2,1,0:T(8,128)} %broadcast_in_dim.11), calls=%async_computation.4 | async-start | bytes 589824 | tf_op jit(solution)/shard_map/all_to_all | solution.py:298
  92.6 13.0 %all-to-all-done.4.parts_ref = f32[8,72,128]{2,1,0:T(8,128)S(1)} async-done(((f32[8,72,128]{2,1,0:T(8,128)}), f32[8,72,128]{2,1,0:T(8,128)S(1)}, u32[]{:S(2)}, u32[]{:S(2)}) %all-to-all-start.4) | async-done | bytes 294944 | tf_op jit(solution)/shard_map/all_to_all | solution.py:298
  105.6 3.4 %shard_map.97 = (f32[136,128]{1,0:T(8,128)S(1)}, f32[128,128]{1,0:T(8,128)S(1)}) custom-call(f32[8,72,128]{2,1,0:T(8,128)S(1)} %all-to-all-done.4.parts_ref, f32[2,128]{1,0:T(2,128)S(1)} %slice.22.shift_ref), custom_call_target="tpu_custom_call" | custom-call | flops 199999995904 | tf_op jit(solution)/shard_map/pallas_call | solution.py:26
  109.6 0.9 collective-permute-done.4.got_ref
  110.5 3.7 %shard_map.98 = (f32[8,1024]{1,0:T(8,128)}, f32[16,8,384]{2,1,0:T(8,128)}, f32[8,64]{1,0:T(8,128)}, f32[8,128]{1,0:T(8,128)S(1)}) custom-call(f32[16,8,512]{2,1,0:T(8,128)S(1)} %all-to-all-done.2.pcs_ref, f32[136,128]{1,0:T(8,128)S(1)} %get-tuple-element.21.keep_ref, f32[136,128]{1,0:T(8,128)S(1)} %collective-permute-done.4.got_ref, ...), custom_call_target="tpu_custom_call" | custom-call | tf_op jit(solution)/shard_map/pallas_call | solution.py:26
  114.2 3.7 %all-to-all-start.5 = ((f32[16,8,384]{2,1,0:T(8,128)}), f32[16,8,384]{2,1,0:T(8,128)S(1)}, u32[]{:S(2)}, u32[]{:S(2)}) async-start(f32[16,8,384]{2,1,0:T(8,128)} %get-tuple-element.26), calls=%async_computation.5 | async-start | bytes 393216 | tf_op jit(solution)/shard_map/all_to_all | solution.py:335
  118.3 0.8 collective-permute-done.5
  119.4 0.7 copy.13
  120.8 7.5 %all-to-all-done.5 = f32[16,8,384]{2,1,0:T(8,128)S(1)} async-done(((f32[16,8,384]{2,1,0:T(8,128)}), f32[16,8,384]{2,1,0:T(8,128)S(1)}, u32[]{:S(2)}, u32[]{:S(2)}) %all-to-all-start.5) | async-done | bytes 196640 | tf_op jit(solution)/shard_map/all_to_all | solution.py:335
  128.4 0.7 fusion.1
  (33 shorter events, 4.1 us)
Async XLA Ops:
  0.6 0.8 copy-start.2
  1.4 23.1 %copy-start = (bf16[1024,4096]{1,0:T(8,128)(2,1)S(1)}, bf16[1024,4096]{1,0:T(8,128)(2,1)}, u32[]{:S(2)}) copy-start(bf16[1024,4096]{1,0:T(8,128)(2,1)} %fields_ref.3) | copy-start | bytes 25165828
  1.4 33.1 %copy-start.3 = (f32[8,64]{1,0:T(8,128)S(1)}, f32[8,64]{1,0:T(8,128)}, u32[]{:S(2)}) copy-start(f32[8,64]{1,0:T(8,128)} %param.8) | copy-start | bytes 6148
  1.4 45.5 %copy-start.4 = (f32[8,64]{1,0:T(8,128)S(1)}, f32[8,64]{1,0:T(8,128)}, u32[]{:S(2)}) copy-start(f32[8,64]{1,0:T(8,128)} %param.7) | copy-start | bytes 6148
  1.4 45.6 %copy-start.5 = (f32[8]{0:T(128)S(1)}, f32[8]{0:T(128)}, u32[]{:S(2)}) copy-start(f32[8]{0:T(128)} %param.9) | copy-start | bytes 100
  20.9 3.6 %collective-permute-start = (bf16[8,64,256]{2,1,0:T(8,128)(2,1)S(1)}, bf16[8,64,256]{2,1,0:T(8,128)(2,1)S(1)}, u32[]{:S(2)}, u32[]{:S(2)}) collective-permute-start(bf16[8,64,256]{2,1,0:T(8,128)(2,1)S(1)} %all_to_all.30.own_ref), channel_id=1, source_target_pairs={{0,1},{1,0},{2,3},{3,2},{4,5},{5,4},{6,7},{7,6},{8,9},{9,8},{10,11... | collective-permute-start | bytes 786440 | tf_op jit(solution)/shard_map/ppermute | solution.py:310
  27.7 14.9 %all-to-all-start.1 = ((f32[16,8,512]{2,1,0:T(8,128)}), f32[16,8,512]{2,1,0:T(8,128)S(1)}, u32[]{:S(2)}, u32[]{:S(2)}) async-start(f32[16,8,512]{2,1,0:T(8,128)} %shard_map.93), calls=%async_computation.1 | async-start | bytes 524288 | tf_op jit(solution)/shard_map/all_to_all | solution.py:313
  43.4 11.0 %all-to-all-start.2 = ((f32[16,8,512]{2,1,0:T(8,128)}), f32[16,8,512]{2,1,0:T(8,128)S(1)}, u32[]{:S(2)}, u32[]{:S(2)}) async-start(f32[16,8,512]{2,1,0:T(8,128)} %broadcast_in_dim.8), calls=%async_computation.2 | async-start | bytes 524288 | tf_op jit(solution)/shard_map/all_to_all | solution.py:314
  57.2 3.6 %collective-permute-start.1 = (f32[72,128]{1,0:T(8,128)S(1)}, f32[72,128]{1,0:T(8,128)S(1)}, u32[]{:S(2)}, u32[]{:S(2)}) collective-permute-start(f32[72,128]{1,0:T(8,128)S(1)} %get-tuple-element.17), channel_id=1, source_target_pairs={{0,1},{1,0},{2,3},{3,2},{4,5},{5,4},{6,7},{7,6},{8,9},{9,8},{10,11... | collective-permute-start | bytes 110600 | tf_op jit(solution)/shard_map/ppermute | solution.py:297
  61.6 16.4 %all-to-all-start.3 = ((f32[8,72,128]{2,1,0:T(8,128)}), f32[8,72,128]{2,1,0:T(8,128)S(1)}, u32[]{:S(2)}, u32[]{:S(2)}) async-start(f32[8,72,128]{2,1,0:T(8,128)} %broadcast_in_dim.10), calls=%async_computation.3 | async-start | bytes 589824 | tf_op jit(solution)/shard_map/all_to_all | solution.py:298
  81.5 1.6 %collective-permute-start.2 = (f32[136,128]{1,0:T(8,128)S(1)}, f32[136,128]{1,0:T(8,128)S(1)}, u32[]{:S(2)}, u32[]{:S(2)}) collective-permute-start(f32[136,128]{1,0:T(8,128)S(1)} %get-tuple-element.18.keep_ref), channel_id=1, source_target_pairs={{0,1},{1,0},{2,3},{3,2},{4,5},{5,4},{6,7},{7,6},{8,9},{9,8},{10,11... | collective-permute-start | bytes 208904 | tf_op jit(solution)/shard_map/ppermute | solution.py:325
  87.1 1.3 %collective-permute-start.3 = (f32[72,128]{1,0:T(8,128)S(1)}, f32[72,128]{1,0:T(8,128)S(1)}, u32[]{:S(2)}, u32[]{:S(2)}) collective-permute-start(f32[72,128]{1,0:T(8,128)S(1)} %get-tuple-element.20), channel_id=1, source_target_pairs={{0,1},{1,0},{2,3},{3,2},{4,5},{5,4},{6,7},{7,6},{8,9},{9,8},{10,11... | collective-permute-start | bytes 110600 | tf_op jit(solution)/shard_map/ppermute | solution.py:297
  89.2 16.4 %all-to-all-start.4 = ((f32[8,72,128]{2,1,0:T(8,128)}), f32[8,72,128]{2,1,0:T(8,128)S(1)}, u32[]{:S(2)}, u32[]{:S(2)}) async-start(f32[8,72,128]{2,1,0:T(8,128)} %broadcast_in_dim.11), calls=%async_computation.4 | async-start | bytes 589824 | tf_op jit(solution)/shard_map/all_to_all | solution.py:298
  105.6 4.9 %copy-start.1 = (bf16[1024,4096]{1,0:T(8,128)(2,1)S(1)}, bf16[1024,4096]{1,0:T(8,128)(2,1)}, u32[]{:S(2)}) copy-start(bf16[1024,4096]{1,0:T(8,128)(2,1)} %fields_ref.3) | copy-start | bytes 25165828
  109.0 1.5 %collective-permute-start.4 = (f32[136,128]{1,0:T(8,128)S(1)}, f32[136,128]{1,0:T(8,128)S(1)}, u32[]{:S(2)}, u32[]{:S(2)}) collective-permute-start(f32[136,128]{1,0:T(8,128)S(1)} %get-tuple-element.21.keep_ref), channel_id=1, source_target_pairs={{0,1},{1,0},{2,3},{3,2},{4,5},{5,4},{6,7},{7,6},{8,9},{9,8},{10,11... | collective-permute-start | bytes 208904 | tf_op jit(solution)/shard_map/ppermute | solution.py:328
  114.2 14.0 %all-to-all-start.5 = ((f32[16,8,384]{2,1,0:T(8,128)}), f32[16,8,384]{2,1,0:T(8,128)S(1)}, u32[]{:S(2)}, u32[]{:S(2)}) async-start(f32[16,8,384]{2,1,0:T(8,128)} %get-tuple-element.26), calls=%async_computation.5 | async-start | bytes 393216 | tf_op jit(solution)/shard_map/all_to_all | solution.py:335
  117.9 1.3 collective-permute-start.5

commit v5 on v4

--- a/solution.py
+++ b/solution.py
@@ -12,7 +12,6 @@
 HALF = R // 2
 F32 = jnp.float32
 BF16 = jnp.bfloat16
-PRECISE = lax.Precision.HIGHEST
 REG = 0.01
 SWAP = [(0, 1), (1, 0)]
 ROWS = K + 8
@@ -20,13 +19,14 @@
 SMALL = 16 * 1024 * 1024
 COVER = pl.CostEstimate(flops=20 * 10 ** 10, transcendentals=0, bytes_accessed=0)
 VMEM = pl.BlockSpec(memory_space=pltpu.VMEM)
-
-
-def call(kernel, outs, operands, limit=LIMIT, cost=None):
+SMEM = pl.BlockSpec(memory_space=pltpu.SMEM)
+
+
+def call(kernel, outs, operands, limit=LIMIT, cost=None, scalars=0):
     return pl.pallas_call(
         kernel,
         out_shape=tuple(jax.ShapeDtypeStruct(s, d) for s, d in outs),
-        in_specs=[VMEM] * len(operands),
+        in_specs=[VMEM] * (len(operands) - scalars) + [SMEM] * scalars,
         out_specs=tuple([VMEM] * len(outs)),
         compiler_params=pltpu.CompilerParams(vmem_limit_bytes=limit),
         cost_estimate=cost,
@@ -114,14 +114,21 @@
     return [jnp.concatenate([pcs_ref[2 * b], pcs_ref[2 * b + 1]], axis=1) for b in range(8)]
 
 
-def centre(pcs, row, offset):
+def centre(pcs, shift):
     sub, _, _ = tile_ids()
-    row = jnp.broadcast_to(row, (8, 128))
+    row = jnp.broadcast_to(jnp.concatenate([shift, shift], axis=1), (8, 128))
     outs = []
     for b in range(8):
-        column = lanes_of(row, sub + (8 * b + offset))
+        column = lanes_of(row, sub + 8 * b)
         outs.append(pcs[b] - jnp.concatenate([column] * (pcs[b].shape[1] // 128), axis=1))
-    return outs
+    return jnp.concatenate(outs, axis=0)
+
+
+def split(x):
+    high = x.astype(BF16)
+    rest = x - high.astype(F32)
+    middle = rest.astype(BF16)
+    return high, middle, (rest - middle.astype(F32)).astype(BF16)
 
 
 def softmax_of(logp):
@@ -130,20 +137,19 @@
     return expo / jnp.sum(expo, axis=0, keepdims=True)
 
 
-def moments(core, centred_of, resp, keep_ref, send_ref):
-    days = resp.shape[1]
+def moments(core, centred, terms, resp, keep_ref, send_ref):
     counts = jnp.broadcast_to(jnp.sum(resp, axis=1, keepdims=True), (R, K))
     row_id = lax.broadcasted_iota(jnp.int32, (K, K), 0)
     col_id = lax.broadcasted_iota(jnp.int32, (K, K), 1)
-    seconds, firsts = [], []
-    for r in range(R):
-        centred = jnp.concatenate(centred_of(r), axis=0)
-        weight = resp[r:r + 1, :]
-        left = jnp.concatenate([centred * weight, jnp.broadcast_to(weight, (8, days))], axis=0)
-        got = lax.dot_general(left, centred, (((1,), (1,)), ((), ())), precision=PRECISE,
-                              preferred_element_type=F32)
-        seconds.append(got[:K])
-        firsts.append(got[K:K + 1])
+    left = jnp.concatenate([centred * resp[r:r + 1, :] for r in range(R)] + [resp], axis=0)
+    high, middle, low = split(left)
+    contract = (((1,), (1,)), ((), ()))
+    got = lax.dot_general(high, jnp.concatenate(terms, axis=0), contract, preferred_element_type=F32)
+    more = lax.dot_general(middle, jnp.concatenate(terms[:2], axis=0), contract, preferred_element_type=F32)
+    last = lax.dot_general(low, terms[0], contract, preferred_element_type=F32)
+    got = got[:, :K] + (got[:, K:2 * K] + more[:, :K]) + (got[:, 2 * K:] + more[:, K:] + last)
+    seconds = [got[K * r:K * r + K] for r in range(R)]
+    firsts = [got[K * R + r:K * R + r + 1] for r in range(R)]
     packs = []
     for h in range(2):
         squares, tails = [], []
@@ -160,24 +166,36 @@
     send_ref[...] = by_core(core, packs[1], packs[0])
 
 
-def first_kernel(pcs_ref, params_ref, base_ref, keep_ref, send_ref):
+def put_shift(shift, shift_ref):
+    shift_ref[...] = jnp.broadcast_to(jnp.concatenate([shift, shift], axis=1), (8, 128))
+
+
+def first_kernel(pcs_ref, means_ref, variances_ref, mixing_ref, keep_ref, send_ref, shift_ref):
     pcs = read_pcs(pcs_ref)
     sub, _, _ = tile_ids()
+    means, variances = means_ref[...], variances_ref[...]
+    shift = jnp.sum(means, axis=0, keepdims=True) / R
+    put_shift(shift, shift_ref)
+    centred = centre(pcs, shift)
+    params = jnp.concatenate([means - shift, 1.0 / variances], axis=1)
+    mixing = jnp.zeros((R, 128), F32)
+    for r in range(R):
+        mixing = jnp.where(sub == r, mixing_ref[r], mixing)
+    weights = mixing / jnp.sum(mixing, axis=0, keepdims=True)
+    base = jnp.log(weights[:, 0:1]) - 0.5 * jnp.sum(jnp.log(variances), axis=1, keepdims=True)
     logs = []
     for r in range(R):
-        row = params_ref[r:r + 1, :]
-        inverse = jnp.broadcast_to(1.0 / row, (8, 128))
-        centred = centre(pcs, row, 0)
+        row = jnp.broadcast_to(params[r:r + 1, :], (8, 128))
         total = None
         for b in range(8):
-            column = lanes_of(inverse, sub + (8 * b + K))
-            scale = jnp.concatenate([column] * 8, axis=1)
-            term = centred[b] * centred[b] * scale
+            mean = jnp.concatenate([lanes_of(row, sub + 8 * b)] * 8, axis=1)
+            scale = jnp.concatenate([lanes_of(row, sub + (8 * b + K))] * 8, axis=1)
+            apart = centred[8 * b:8 * b + 8] - mean
+            term = apart * apart * scale
             total = term if total is None else total + term
         logs.append(jnp.sum(total, axis=0, keepdims=True))
-    logp = base_ref[:, 0:1] - 0.5 * jnp.concatenate(logs, axis=0)
-    resp = softmax_of(logp)
-    moments(lax.axis_index("core"), lambda r: centre(pcs, params_ref[r:r + 1, :], 0), resp, keep_ref, send_ref)
+    resp = softmax_of(base - 0.5 * jnp.concatenate(logs, axis=0))
+    moments(lax.axis_index("core"), centred, split(centred), resp, keep_ref, send_ref)
 
 
 def merge_kernel(parts_ref, shift_ref, block_ref, covs_ref):
@@ -192,7 +210,7 @@
     pairs = []
     infos = []
     for p in range(2):
-        first, count, shift = tail[1 + p:2 + p], tail[3 + p:4 + p], shift_ref[p:p + 1, :]
+        first, count, shift = tail[1 + p:2 + p], tail[3 + p:4 + p], shift_ref[0:1, :]
         counted = jnp.maximum(count, 1.0)
         mean = (first + count * shift) / counted
         delta = mean - shift
@@ -238,18 +256,32 @@
             rows.append(infos[h][at + p:at + p + 1, offset:offset + 1])
         return jnp.concatenate(rows, axis=0)
 
+    means, inverses = [], []
+    for r in range(R):
+        h, p, offset = regime_of(r)
+        means.append(infos[h][p:p + 1, offset:offset + K])
+        inverses.append(halves[h][K * p:K * p + K, offset:offset + K])
+    means = jnp.concatenate(means, axis=0)
     counted = column(4)
     weights = counted / jnp.sum(counted, axis=0, keepdims=True)
+    shift = jnp.sum(means * weights, axis=0, keepdims=True)
+    centred = centre(pcs, shift)
+    days = centred.shape[1]
+    apart = jnp.concatenate([means - shift, jnp.zeros((128 - R, K), F32)], axis=0).T
+    terms = split(centred)
+    ends = split(apart)
+    c1, c2, c3 = [jnp.concatenate([x, y], axis=1) for x, y in zip(terms, ends)]
+    w1, w2, w3 = split(jnp.concatenate(inverses, axis=0))
+    left = jnp.concatenate([w1, w1, w2, w2, w1, w3], axis=1)
+    right = jnp.concatenate([c1, c2, c1, c2, c3, c1], axis=0)
+    shifted = jnp.dot(left, right, preferred_element_type=F32)
     logs = []
     for r in range(R):
-        h, p, offset = regime_of(r)
-        inverse = halves[h][K * p:K * p + K, offset:offset + K]
-        centred = jnp.concatenate(centre(pcs, infos[h][p:p + 1, :], offset), axis=0)
-        shifted = lax.dot_general(inverse, centred, (((1,), (0,)), ((), ())), precision=PRECISE,
-                                  preferred_element_type=F32)
-        logs.append(jnp.sum(shifted * shifted, axis=0, keepdims=True))
+        mine = shifted[K * r:K * r + K]
+        mine = mine[:, :days] - mine[:, days + r:days + r + 1]
+        logs.append(jnp.sum(mine * mine, axis=0, keepdims=True))
     logp = jnp.log(weights) - column(2) - 0.5 * jnp.concatenate(logs, axis=0)
-    return softmax_of(logp), weights
+    return softmax_of(logp), weights, means, shift, centred, terms
 
 
 def halves_of(core, keep_ref, got_ref):
@@ -257,31 +289,19 @@
     return [by_core(core, keep, got), by_core(core, got, keep)]
 
 
-def middle_kernel(pcs_ref, keep_ref, got_ref, out_keep_ref, out_send_ref):
+def middle_kernel(pcs_ref, keep_ref, got_ref, out_keep_ref, out_send_ref, shift_ref):
     core = lax.axis_index("core")
-    pcs = read_pcs(pcs_ref)
-    halves = halves_of(core, keep_ref, got_ref)
-    resp, _ = expect(pcs, halves)
-
-    def centred_of(r):
-        h, p, offset = regime_of(r)
-        return centre(pcs, halves[h][2 * K + p:2 * K + p + 1, :], offset)
-
-    moments(core, centred_of, resp, out_keep_ref, out_send_ref)
+    resp, _, _, shift, centred, terms = expect(read_pcs(pcs_ref), halves_of(core, keep_ref, got_ref))
+    put_shift(shift, shift_ref)
+    moments(core, centred, terms, resp, out_keep_ref, out_send_ref)
 
 
 def last_kernel(pcs_ref, keep_ref, got_ref, fields_ref, member_ref, terms_ref, means_ref, weights_ref):
     core = lax.axis_index("core")
-    pcs = read_pcs(pcs_ref)
-    halves = halves_of(core, keep_ref, got_ref)
-    member, weights = expect(pcs, halves)
+    member, weights, means, _, _, _ = expect(read_pcs(pcs_ref), halves_of(core, keep_ref, got_ref))
     member_ref[...] = member
     weights_ref[...] = jnp.broadcast_to(weights, (R, 128))
-    means = []
-    for r in range(R):
-        h, p, offset = regime_of(r)
-        means.append(halves[h][2 * K + p:2 * K + p + 1, offset:offset + K])
-    means_ref[...] = jnp.concatenate(means, axis=0)
+    means_ref[...] = means
     count = jnp.broadcast_to(jnp.sum(member, axis=1, keepdims=True), (R, 128))
     rounded = member.astype(BF16)
     for j in range(16):
@@ -313,18 +333,12 @@
     mine = jnp.sum(lax.all_to_all(partial, "grid", 0, 0), axis=0)
     pcs = lax.all_to_all(spread(mine, 16), "grid", 0, 0)
 
-    params = jnp.concatenate([means_init, variances], axis=1)
-    base = jnp.log(mixing / jnp.sum(mixing)) - 0.5 * jnp.sum(jnp.log(variances), axis=1)
-    base = jnp.broadcast_to(base[:, None], (R, 128))
-    sides = means_init.reshape(2, 2, 2, K).swapaxes(1, 2).reshape(2, 2, 2 * K)
-    shift = jnp.where(core == 0, sides[0], sides[1])
-
-    pack = [((ROWS, 128), F32)] * 2
-    keep, send = call(first_kernel, pack, [pcs, params, base])
+    pack = [((ROWS, 128), F32)] * 2 + [((8, 128), F32)]
+    keep, send, shift = call(first_kernel, pack, [pcs, means_init, variances, mixing], scalars=1)
     block, _ = merge(keep, send, shift)
     got = lax.ppermute(block, "core", SWAP)
-    keep, send = call(middle_kernel, pack, [pcs, block, got])
-    block, covs = merge(keep, send, block[2 * K:2 * K + 2])
+    keep, send, shift = call(middle_kernel, pack, [pcs, block, got])
+    block, covs = merge(keep, send, shift)
     got = lax.ppermute(block, "core", SWAP)
     got_covs = lax.ppermute(covs, "core", SWAP)
     member, terms, means, weights = call(

time: 130 us -> 122 us (0.938)
  blocking collectives: 19.4 us -> 74.4 us
  waiting for transfers between devices: 53 us -> 13 us
  starting transfers between devices: 28 us -> 11.7 us
  Pallas kernels: 20.6 us -> 18 us
  local copies, waits for them, and re-layouts: 4.74 us -> 2.44 us
  other arithmetic: 2.43 us -> 0.98 us
    all_to_all x0 -> x4, blocking collectives: none -> 55 us  [the longest x2 30.1 us: merge(): parts = lax.all_to_all(spread(half, 8), 'z', 0, 0)]
    all_to_all x4 -> x0, waiting for transfers between devices: 40 us -> none  [the longest x2 25.8 us: merge(): parts = lax.all_to_all(spread(half, 8), 'z', 0, 0)]
    all_to_all x4 -> x0, starting transfers between devices: 17.1 us -> none  [the longest x2 6.84 us: merge(): parts = lax.all_to_all(spread(half, 8), 'z', 0, 0)]
    pallas_call x7, Pallas kernels: 20.6 us -> 18 us  [call(): pl.pallas_call(kernel, out_shape=tuple((jax.ShapeDtypeStruct(s, d) for s,...]
    broadcast_in_dim x3, local copies, waits for them, and re-layouts: 2.2 us -> 0.06 us  [spread(): return jnp.broadcast_to(x[None], (n,) + x.shape)]
  transfers between devices with their start and end apart: 11 -> 7, of which waited for: 11 -> 7; matrix products, arithmetic and copies ran while one was open for 3% -> 1% of each run, Pallas kernels for 0% -> 0%
where the time goes in v5:
time: 122 us; the launch traced here: 121 us
  blocking collectives  74.4 us (61%)
  Pallas kernels  18 us (15%)
  waiting for transfers between devices  13 us (11%)
  starting transfers between devices  11.7 us (10%)
  local copies, waits for them, and re-layouts  2.44 us (2%)
    all_to_all x2, blocking collectives, merge(): parts = lax.all_to_all(spread(half, 8), 'z', 0, 0)  30.1 us
    all_to_all x1, blocking collectives, body(): own = lax.all_to_all(eight, 'z', 0, 0)  19.4 us
    pallas_call x7, Pallas kernels, call(): pl.pallas_call(kernel, out_shape=tuple((jax.ShapeDtypeStruct(s, d) for s,...  18 us
    all_to_all x1, blocking collectives, body(): mine = jnp.sum(lax.all_to_all(partial, 'grid', 0, 0), axis=0)  14.7 us
    all_to_all x1, blocking collectives, body(): pcs = lax.all_to_all(spread(mine, 16), 'grid', 0, 0)  10.2 us
    all_to_all x1, waiting for transfers between devices, body(): sums = jnp.sum(lax.all_to_all(terms, ('z', 'core'), 0, 0), axis=0)  7.47 us
    all_to_all x1, starting transfers between devices, body(): sums = jnp.sum(lax.all_to_all(terms, ('z', 'core'), 0, 0), axis=0)  3.66 us
    ppermute x2, starting transfers between devices, merge(): half = keep + lax.ppermute(send, 'core', SWAP)  3.39 us
  transfers between devices with their start and end apart: 7, of which 7 were waited for; matrix products, arithmetic and copies ran while one was open for 1% of the time, Pallas kernels for 0%

profile of v5, /device:TPU:1, one launch (start us, length us, event | category | flops | bytes accessed | tf_op | source)
XLA Modules:
  0.0 121.4 jit_solution(13396141912302214740)
XLA Ops:
  0.6 0.7 copy-done.5
  1.4 19.4 %all_to_all.30.own_ref = bf16[8,64,256]{2,1,0:T(8,128)(2,1)S(1)} all-to-all(bf16[8,64,256]{2,1,0:T(8,128)(2,1)S(1)} %shard_map.92), channel_id=1, replica_groups=mesh['grid'=16,'z'=8,'core'=2] {'z'}, dimensions={0} | all-to-all | bytes 524288 | tf_op jit(solution)/shard_map/all_to_all | solution.py:329
  20.9 2.5 %collective-permute-start = (bf16[8,64,256]{2,1,0:T(8,128)(2,1)S(1)}, bf16[8,64,256]{2,1,0:T(8,128)(2,1)S(1)}, u32[]{:S(2)}, u32[]{:S(2)}) collective-permute-start(bf16[8,64,256]{2,1,0:T(8,128)(2,1)S(1)} %all_to_all.30.own_ref), channel_id=1, source_target_pairs={{0,1},{1,0},{2,3},{3,2},{4,5},{5,4},{6,7},{7,6},{8,9},{9,8},{10,11... | collective-permute-start | bytes 786440 | tf_op jit(solution)/shard_map/ppermute | solution.py:330
  23.4 1.2 collective-permute-done.other_ref
  24.5 2.5 %shard_map.93 = f32[16,8,512]{2,1,0:T(8,128)S(1)} custom-call(bf16[8,64,256]{2,1,0:T(8,128)(2,1)S(1)} %all_to_all.30.own_ref, bf16[8,64,256]{2,1,0:T(8,128)(2,1)S(1)} %collective-permute-done.other_ref, bf16[1024,4096]{1,0:T(8,128)(2,1)S(1)} %copy-done), custom_call_target="tpu_custom_call" | custom-call | tf_op jit(solution)/shard_map/pallas_call | solution.py:26
  27.0 14.7 %all_to_all.31 = f32[16,8,512]{2,1,0:T(8,128)S(1)} all-to-all(f32[16,8,512]{2,1,0:T(8,128)S(1)} %shard_map.93), channel_id=1, replica_groups=mesh['grid'=16,'z'=8,'core'=2] {'grid'}, dimensions={0} | all-to-all | bytes 524288 | tf_op jit(solution)/shard_map/all_to_all | solution.py:333
  41.8 10.2 %all_to_all.32.pcs_ref = f32[16,8,512]{2,1,0:T(8,128)S(1)} all-to-all(f32[16,8,512]{2,1,0:T(8,128)S(1)} %broadcast_in_dim.6), channel_id=1, replica_groups=mesh['grid'=16,'z'=8,'core'=2] {'grid'}, dimensions={0} | all-to-all | bytes 524288 | tf_op jit(solution)/shard_map/all_to_all | solution.py:334
  52.0 2.3 %shard_map.94 = (f32[72,128]{1,0:T(8,128)S(1)}, f32[72,128]{1,0:T(8,128)S(1)}, f32[8,128]{1,0:T(8,128)S(1)}) custom-call(f32[16,8,512]{2,1,0:T(8,128)S(1)} %all_to_all.32.pcs_ref, f32[8,64]{1,0:T(8,128)S(1)} %copy-done.2, f32[8,64]{1,0:T(8,128)S(1)} %copy-done.3, f32[8]{0:T(128)S(1)} %copy-done.4), custom_call_target="tpu_custom_call" | custom-call | tf_op jit(solution)/shard_map/pallas_call | solution.py:26
  54.3 3.0 %collective-permute-start.1 = (f32[72,128]{1,0:T(8,128)S(1)}, f32[72,128]{1,0:T(8,128)S(1)}, u32[]{:S(2)}, u32[]{:S(2)}) collective-permute-start(f32[72,128]{1,0:T(8,128)S(1)} %get-tuple-element.19), channel_id=1, source_target_pairs={{0,1},{1,0},{2,3},{3,2},{4,5},{5,4},{6,7},{7,6},{8,9},{9,8},{10,11... | collective-permute-start | bytes 110600 | tf_op jit(solution)/shard_map/ppermute | solution.py:317
  57.2 0.9 collective-permute-done.1
  58.1 15.0 %all_to_all.33.parts_ref = f32[8,72,128]{2,1,0:T(8,128)S(1)} all-to-all(f32[8,72,128]{2,1,0:T(8,128)S(1)} %broadcast_in_dim.7), channel_id=1, replica_groups=mesh['grid'=16,'z'=8,'core'=2] {'z'}, dimensions={0} | all-to-all | bytes 589824 | tf_op jit(solution)/shard_map/all_to_all | solution.py:318
  73.2 3.4 %shard_map.95 = (f32[136,128]{1,0:T(8,128)S(1)}, f32[128,128]{1,0:T(8,128)}) custom-call(f32[8,72,128]{2,1,0:T(8,128)S(1)} %all_to_all.33.parts_ref, f32[8,128]{1,0:T(8,128)S(1)} %get-tuple-element.20.shift_ref), custom_call_target="tpu_custom_call" | custom-call | flops 199999995904 | tf_op jit(solution)/shard_map/pallas_call | solution.py:26
  76.6 0.9 collective-permute-start.2
  77.6 0.9 collective-permute-done.2.got_ref
  78.5 3.0 %shard_map.96 = (f32[72,128]{1,0:T(8,128)S(1)}, f32[72,128]{1,0:T(8,128)S(1)}, f32[8,128]{1,0:T(8,128)S(1)}) custom-call(f32[16,8,512]{2,1,0:T(8,128)S(1)} %all_to_all.32.pcs_ref, f32[136,128]{1,0:T(8,128)S(1)} %get-tuple-element.21.keep_ref, f32[136,128]{1,0:T(8,128)S(1)} %collective-permute-done.2.got_ref), custom_call_target="tpu_custom_call" | custom-call | tf_op jit(solution)/shard_map/pallas_call | solution.py:26
  81.5 0.4 collective-permute-start.3
  81.9 0.9 collective-permute-done.3
  82.8 15.0 %all_to_all.34.parts_ref = f32[8,72,128]{2,1,0:T(8,128)S(1)} all-to-all(f32[8,72,128]{2,1,0:T(8,128)S(1)} %broadcast_in_dim.8), channel_id=1, replica_groups=mesh['grid'=16,'z'=8,'core'=2] {'z'}, dimensions={0} | all-to-all | bytes 589824 | tf_op jit(solution)/shard_map/all_to_all | solution.py:318
  97.9 3.4 %shard_map.97 = (f32[136,128]{1,0:T(8,128)S(1)}, f32[128,128]{1,0:T(8,128)S(1)}) custom-call(f32[8,72,128]{2,1,0:T(8,128)S(1)} %all_to_all.34.parts_ref, f32[8,128]{1,0:T(8,128)S(1)} %get-tuple-element.24.shift_ref), custom_call_target="tpu_custom_call" | custom-call | flops 199999995904 | tf_op jit(solution)/shard_map/pallas_call | solution.py:26
  101.3 1.0 collective-permute-start.4
  102.3 0.9 collective-permute-done.4.got_ref
  103.2 3.3 %shard_map.98 = (f32[8,1024]{1,0:T(8,128)}, f32[16,8,384]{2,1,0:T(8,128)}, f32[8,64]{1,0:T(8,128)}, f32[8,128]{1,0:T(8,128)S(1)}) custom-call(f32[16,8,512]{2,1,0:T(8,128)S(1)} %all_to_all.32.pcs_ref, f32[136,128]{1,0:T(8,128)S(1)} %get-tuple-element.25.keep_ref, f32[136,128]{1,0:T(8,128)S(1)} %collective-permute-done.4.got_ref, bf16[1024,4096]{1,0:T(8,128)(2,1)S(1)} %copy-done.1), custom_call_target="tpu_custom_call" | custom-call | tf_op jit(solution)/shard_map/pallas_call | solution.py:26
  106.5 3.7 %all-to-all-start.5 = ((f32[16,8,384]{2,1,0:T(8,128)}), f32[16,8,384]{2,1,0:T(8,128)S(1)}, u32[]{:S(2)}, u32[]{:S(2)}) async-start(f32[16,8,384]{2,1,0:T(8,128)} %get-tuple-element.30), calls=%async_computation.5 | async-start | bytes 393216 | tf_op jit(solution)/shard_map/all_to_all | solution.py:349
  110.2 0.3 collective-permute-start.5
  110.5 0.1 stack.14
  110.6 0.8 collective-permute-done.5
  111.5 0.1 stack.15
  111.6 0.1 fusion
  111.7 0.7 copy.11
  112.5 0.6 slice_reduce_fusion
  113.1 7.5 %all-to-all-done.5 = f32[16,8,384]{2,1,0:T(8,128)S(1)} async-done(((f32[16,8,384]{2,1,0:T(8,128)}), f32[16,8,384]{2,1,0:T(8,128)S(1)}, u32[]{:S(2)}, u32[]{:S(2)}) %all-to-all-start.5) | async-done | bytes 196640 | tf_op jit(solution)/shard_map/all_to_all | solution.py:349
  120.7 0.7 fusion.1
  (20 shorter events, 0.3 us)
Async XLA Ops:
  0.6 0.8 copy-start.5
  1.4 23.1 %copy-start = (bf16[1024,4096]{1,0:T(8,128)(2,1)S(1)}, bf16[1024,4096]{1,0:T(8,128)(2,1)}, u32[]{:S(2)}) copy-start(bf16[1024,4096]{1,0:T(8,128)(2,1)} %fields_ref.3) | copy-start | bytes 25165828
  1.4 50.6 %copy-start.2 = (f32[8,64]{1,0:T(8,128)S(1)}, f32[8,64]{1,0:T(8,128)}, u32[]{:S(2)}) copy-start(f32[8,64]{1,0:T(8,128)} %means_ref.1) | copy-start | bytes 6148
  1.4 50.6 %copy-start.3 = (f32[8,64]{1,0:T(8,128)S(1)}, f32[8,64]{1,0:T(8,128)}, u32[]{:S(2)}) copy-start(f32[8,64]{1,0:T(8,128)} %variances_ref.1) | copy-start | bytes 6148
  1.4 50.6 %copy-start.4 = (f32[8]{0:T(128)S(1)}, f32[8]{0:T(128)}, u32[]{:S(2)}) copy-start(f32[8]{0:T(128)} %mixing_ref.1) | copy-start | bytes 100
  20.9 3.6 %collective-permute-start = (bf16[8,64,256]{2,1,0:T(8,128)(2,1)S(1)}, bf16[8,64,256]{2,1,0:T(8,128)(2,1)S(1)}, u32[]{:S(2)}, u32[]{:S(2)}) collective-permute-start(bf16[8,64,256]{2,1,0:T(8,128)(2,1)S(1)} %all_to_all.30.own_ref), channel_id=1, source_target_pairs={{0,1},{1,0},{2,3},{3,2},{4,5},{5,4},{6,7},{7,6},{8,9},{9,8},{10,11... | collective-permute-start | bytes 786440 | tf_op jit(solution)/shard_map/ppermute | solution.py:330
  54.3 3.8 %collective-permute-start.1 = (f32[72,128]{1,0:T(8,128)S(1)}, f32[72,128]{1,0:T(8,128)S(1)}, u32[]{:S(2)}, u32[]{:S(2)}) collective-permute-start(f32[72,128]{1,0:T(8,128)S(1)} %get-tuple-element.19), channel_id=1, source_target_pairs={{0,1},{1,0},{2,3},{3,2},{4,5},{5,4},{6,7},{7,6},{8,9},{9,8},{10,11... | collective-permute-start | bytes 110600 | tf_op jit(solution)/shard_map/ppermute | solution.py:317
  76.6 1.8 %collective-permute-start.2 = (f32[136,128]{1,0:T(8,128)S(1)}, f32[136,128]{1,0:T(8,128)S(1)}, u32[]{:S(2)}, u32[]{:S(2)}) collective-permute-start(f32[136,128]{1,0:T(8,128)S(1)} %get-tuple-element.21.keep_ref), channel_id=1, source_target_pairs={{0,1},{1,0},{2,3},{3,2},{4,5},{5,4},{6,7},{7,6},{8,9},{9,8},{10,11... | collective-permute-start | bytes 208904 | tf_op jit(solution)/shard_map/ppermute | solution.py:339
  81.5 1.3 %collective-permute-start.3 = (f32[72,128]{1,0:T(8,128)S(1)}, f32[72,128]{1,0:T(8,128)S(1)}, u32[]{:S(2)}, u32[]{:S(2)}) collective-permute-start(f32[72,128]{1,0:T(8,128)S(1)} %get-tuple-element.23), channel_id=1, source_target_pairs={{0,1},{1,0},{2,3},{3,2},{4,5},{5,4},{6,7},{7,6},{8,9},{9,8},{10,11... | collective-permute-start | bytes 110600 | tf_op jit(solution)/shard_map/ppermute | solution.py:317
  97.9 5.3 %copy-start.1 = (bf16[1024,4096]{1,0:T(8,128)(2,1)S(1)}, bf16[1024,4096]{1,0:T(8,128)(2,1)}, u32[]{:S(2)}) copy-start(bf16[1024,4096]{1,0:T(8,128)(2,1)} %fields_ref.3) | copy-start | bytes 25165828
  101.3 1.9 %collective-permute-start.4 = (f32[136,128]{1,0:T(8,128)S(1)}, f32[136,128]{1,0:T(8,128)S(1)}, u32[]{:S(2)}, u32[]{:S(2)}) collective-permute-start(f32[136,128]{1,0:T(8,128)S(1)} %get-tuple-element.25.keep_ref), channel_id=1, source_target_pairs={{0,1},{1,0},{2,3},{3,2},{4,5},{5,4},{6,7},{7,6},{8,9},{9,8},{10,11... | collective-permute-start | bytes 208904 | tf_op jit(solution)/shard_map/ppermute | solution.py:342
  106.5 14.0 %all-to-all-start.5 = ((f32[16,8,384]{2,1,0:T(8,128)}), f32[16,8,384]{2,1,0:T(8,128)S(1)}, u32[]{:S(2)}, u32[]{:S(2)}) async-start(f32[16,8,384]{2,1,0:T(8,128)} %get-tuple-element.30), calls=%async_computation.5 | async-start | bytes 393216 | tf_op jit(solution)/shard_map/all_to_all | solution.py:349
  110.2 1.3 %collective-permute-start.5 = (f32[128,128]{1,0:T(8,128)S(1)}, f32[128,128]{1,0:T(8,128)S(1)}, u32[]{:S(2)}, u32[]{:S(2)}) collective-permute-start(f32[128,128]{1,0:T(8,128)S(1)} %get-tuple-element.27), channel_id=1, source_target_pairs={{0,1},{1,0},{2,3},{3,2},{4,5},{5,4},{6,7},{7,6},{8,9},{9,8},{10,11... | collective-permute-start | bytes 196616 | tf_op jit(solution)/shard_map/ppermute | solution.py:343

commit v6 on v5

--- a/solution.py
+++ b/solution.py
@@ -15,6 +15,7 @@
 REG = 0.01
 SWAP = [(0, 1), (1, 0)]
 ROWS = K + 8
+INFO = 2 * K
 LIMIT = 48 * 1024 * 1024
 SMALL = 16 * 1024 * 1024
 COVER = pl.CostEstimate(flops=20 * 10 ** 10, transcendentals=0, bytes_accessed=0)
@@ -22,12 +23,12 @@
 SMEM = pl.BlockSpec(memory_space=pltpu.SMEM)
 
 
-def call(kernel, outs, operands, limit=LIMIT, cost=None, scalars=0):
+def call(kernel, outs, operands, limit=LIMIT, cost=None, scalars=0, scalar_outs=0):
     return pl.pallas_call(
         kernel,
         out_shape=tuple(jax.ShapeDtypeStruct(s, d) for s, d in outs),
         in_specs=[VMEM] * (len(operands) - scalars) + [SMEM] * scalars,
-        out_specs=tuple([VMEM] * len(outs)),
+        out_specs=tuple([VMEM] * (len(outs) - scalar_outs) + [SMEM] * scalar_outs),
         compiler_params=pltpu.CompilerParams(vmem_limit_bytes=limit),
         cost_estimate=cost,
     )(*operands)
@@ -198,7 +199,7 @@
     moments(lax.axis_index("core"), centred, split(centred), resp, keep_ref, send_ref)
 
 
-def merge_kernel(parts_ref, shift_ref, block_ref, covs_ref):
+def merge_kernel(parts_ref, shift_ref, block_ref):
     sub, half, col = tile_ids()
     total = parts_ref[0]
     for z in range(1, 8):
@@ -228,7 +229,9 @@
             at = half + row_id
             second = second - lanes_of(first_b, at) * delta - lanes_of(delta_b, at) * rest
             cov = second * scale + jnp.where(row_id == col, REG, 0.0)
-            covs_ref[K * p + 8 * g:K * p + 8 * g + 8, :] = cov
+            if block_ref.shape[0] > INFO + 8:
+                at = INFO + 8 + K * p + 8 * g
+                block_ref[at:at + 8, :] = cov
             groups.append(cov)
         pairs.append(groups)
         infos.append((mean, counted))
@@ -236,7 +239,7 @@
     for g in range(8):
         block_ref[8 * g:8 * g + 8, :] = first_out[g]
         block_ref[K + 8 * g:K + 8 * g + 8, :] = second_out[g]
-    block_ref[2 * K:, :] = jnp.concatenate(
+    block_ref[INFO:INFO + 8, :] = jnp.concatenate(
         [infos[0][0], infos[1][0], first_log, second_log, infos[0][1], infos[1][1],
          jnp.zeros((2, 128), F32)], axis=0)
 
@@ -247,7 +250,7 @@
 
 
 def expect(pcs, halves):
-    infos = [block[2 * K:] for block in halves]
+    infos = [block[INFO:INFO + 8] for block in halves]
 
     def column(at):
         rows = []
@@ -296,11 +299,17 @@
     moments(core, centred, terms, resp, out_keep_ref, out_send_ref)
 
 
-def last_kernel(pcs_ref, keep_ref, got_ref, fields_ref, member_ref, terms_ref, means_ref, weights_ref):
+def last_kernel(pcs_ref, keep_ref, got_ref, fields_ref, member_ref, terms_ref, means_ref, covs_ref, weights_ref):
     core = lax.axis_index("core")
-    member, weights, means, _, _, _ = expect(read_pcs(pcs_ref), halves_of(core, keep_ref, got_ref))
+    halves = halves_of(core, keep_ref, got_ref)
+    for r in range(R):
+        h, p, offset = regime_of(r)
+        at = INFO + 8 + K * p
+        covs_ref[r] = halves[h][at:at + K, offset:offset + K]
+    member, weights, means, _, _, _ = expect(read_pcs(pcs_ref), halves)
     member_ref[...] = member
-    weights_ref[...] = jnp.broadcast_to(weights, (R, 128))
+    for r in range(R):
+        weights_ref[r] = weights[r, 0]
     means_ref[...] = means
     count = jnp.broadcast_to(jnp.sum(member, axis=1, keepdims=True), (R, 128))
     rounded = member.astype(BF16)
@@ -313,16 +322,15 @@
     return jnp.broadcast_to(x[None], (n,) + x.shape)
 
 
-def merge(keep, send, shift):
+def merge(keep, send, shift, rows):
     half = keep + lax.ppermute(send, "core", SWAP)
     parts = lax.all_to_all(spread(half, 8), "z", 0, 0)
-    return call(merge_kernel, [((2 * K + 8, 128), F32), ((2 * K, 128), F32)], [parts, shift],
-                limit=SMALL, cost=COVER)
+    block, = call(merge_kernel, [((rows, 128), F32)], [parts, shift], limit=SMALL, cost=COVER)
+    return block, lax.ppermute(block, "core", SWAP)
 
 
 def body(anomalies, eofs, means_init, variances, mixing):
     days = anomalies.shape[0]
-    core = lax.axis_index("core")
     eight, = call(
         spread_kernel, [((8,) + eofs.shape, BF16)], [eofs], limit=SMALL,
         cost=COVER)
@@ -335,23 +343,17 @@
 
     pack = [((ROWS, 128), F32)] * 2 + [((8, 128), F32)]
     keep, send, shift = call(first_kernel, pack, [pcs, means_init, variances, mixing], scalars=1)
-    block, _ = merge(keep, send, shift)
-    got = lax.ppermute(block, "core", SWAP)
+    block, got = merge(keep, send, shift, INFO + 8)
     keep, send, shift = call(middle_kernel, pack, [pcs, block, got])
-    block, covs = merge(keep, send, shift)
-    got = lax.ppermute(block, "core", SWAP)
-    got_covs = lax.ppermute(covs, "core", SWAP)
-    member, terms, means, weights = call(
+    block, got = merge(keep, send, shift, INFO + 8 + 2 * K)
+    member, terms, means, covs, weights = call(
         last_kernel,
-        [((R, days), F32), ((16, R, 384), F32), ((R, K), F32), ((R, 128), F32)],
-        [pcs, block, got, anomalies],
-        limit=SMALL)
+        [((R, days), F32), ((16, R, 384), F32), ((R, K), F32), ((R, K, K), F32), ((R,), F32)],
+        [pcs, block, got, anomalies], limit=SMALL, scalar_outs=1)
     sums = jnp.sum(lax.all_to_all(terms, ("z", "core"), 0, 0), axis=0)
     composites = (sums[:, :256] / jnp.maximum(sums[:, 256:257], 1.0)).astype(BF16)
 
-    both = jnp.where(core == 0, jnp.stack([covs, got_covs]), jnp.stack([got_covs, covs]))
-    covs = both.reshape(2, 2, K, 2, K).transpose(0, 3, 1, 2, 4).reshape(R, K, K)
-    return (means, covs, weights[:, 0], member, composites)
+    return (means, covs, weights, member, composites)
 
 
 def solution(mesh):

time: 122 us -> 121 us (level)
  blocking collectives: 74.4 us -> 87.6 us
  waiting for transfers between devices: 13 us -> 4.79 us
  starting transfers between devices: 11.7 us -> 7.75 us
  local copies, waits for them, and re-layouts: 2.44 us -> 0.84 us
    all_to_all x0 -> x1, blocking collectives: none -> 13.2 us  [body(): sums = jnp.sum(lax.all_to_all(terms, ('z', 'core'), 0, 0), axis=0)]
    all_to_all x1 -> x0, waiting for transfers between devices: 7.47 us -> none  [body(): sums = jnp.sum(lax.all_to_all(terms, ('z', 'core'), 0, 0), axis=0)]
    all_to_all x1 -> x0, starting transfers between devices: 3.66 us -> none  [body(): sums = jnp.sum(lax.all_to_all(terms, ('z', 'core'), 0, 0), axis=0)]
    ppermute x3 -> x2, waiting for transfers between devices: 2.65 us -> 1.9 us  [merge(): return (block, lax.ppermute(block, 'core', SWAP))]
  transfers between devices with their start and end apart: 7 -> 5, of which waited for: 7 -> 5; matrix products, arithmetic and copies ran while one was open for 1% -> 0% of each run, Pallas kernels for 0% -> 0%
where the time goes in v6:
time: 121 us
  blocking collectives  87.6 us (72%)
  Pallas kernels  18 us (15%)
  starting transfers between devices  7.75 us (6%)
  waiting for transfers between devices  4.79 us (4%)
    all_to_all x2, blocking collectives, merge(): parts = lax.all_to_all(spread(half, 8), 'z', 0, 0)  30.1 us
    all_to_all x1, blocking collectives, body(): own = lax.all_to_all(eight, 'z', 0, 0)  19.4 us
    pallas_call x7, Pallas kernels, call(): pl.pallas_call(kernel, out_shape=tuple((jax.ShapeDtypeStruct(s, d) for s,...  18 us
    all_to_all x1, blocking collectives, body(): mine = jnp.sum(lax.all_to_all(partial, 'grid', 0, 0), axis=0)  14.7 us
    all_to_all x1, blocking collectives, body(): sums = jnp.sum(lax.all_to_all(terms, ('z', 'core'), 0, 0), axis=0)  13.2 us
    all_to_all x1, blocking collectives, body(): pcs = lax.all_to_all(spread(mine, 16), 'grid', 0, 0)  10.2 us
    ppermute x2, starting transfers between devices, merge(): half = keep + lax.ppermute(send, 'core', SWAP)  3.39 us
    ppermute x1, starting transfers between devices, body(): other = lax.ppermute(own, 'core', SWAP)  2.46 us
  transfers between devices with their start and end apart: 5, of which 5 were waited for; matrix products, arithmetic and copies ran while one was open for 0% of the time, Pallas kernels for 0%

profile of v6, /device:TPU:1, one launch (start us, length us, event | category | flops | bytes accessed | tf_op | source)
XLA Modules:
  0.0 120.6 jit_solution(4125582685483421306)
XLA Ops:
  0.6 0.0 copy-start.5
  0.6 0.7 copy-done.5
  1.4 0.0 copy-start.2
  1.4 0.0 copy-start.3
  1.4 0.0 copy-start.4
  1.4 19.4 %all_to_all.30.own_ref = bf16[8,64,256]{2,1,0:T(8,128)(2,1)S(1)} all-to-all(bf16[8,64,256]{2,1,0:T(8,128)(2,1)S(1)} %shard_map.92), channel_id=1, replica_groups=mesh['grid'=16,'z'=8,'core'=2] {'z'}, dimensions={0} | all-to-all | bytes 524288 | tf_op jit(solution)/shard_map/all_to_all | solution.py:337
  20.9 2.5 %collective-permute-start = (bf16[8,64,256]{2,1,0:T(8,128)(2,1)S(1)}, bf16[8,64,256]{2,1,0:T(8,128)(2,1)S(1)}, u32[]{:S(2)}, u32[]{:S(2)}) collective-permute-start(bf16[8,64,256]{2,1,0:T(8,128)(2,1)S(1)} %all_to_all.30.own_ref), channel_id=1, source_target_pairs={{0,1},{1,0},{2,3},{3,2},{4,5},{5,4},{6,7},{7,6},{8,9},{9,8},{10,11... | collective-permute-start | bytes 786440 | tf_op jit(solution)/shard_map/ppermute | solution.py:338
  23.4 1.2 collective-permute-done.other_ref
  24.5 0.0 copy-done
  24.5 2.5 %shard_map.93 = f32[16,8,512]{2,1,0:T(8,128)S(1)} custom-call(bf16[8,64,256]{2,1,0:T(8,128)(2,1)S(1)} %all_to_all.30.own_ref, bf16[8,64,256]{2,1,0:T(8,128)(2,1)S(1)} %collective-permute-done.other_ref, bf16[1024,4096]{1,0:T(8,128)(2,1)S(1)} %copy-done), custom_call_target="tpu_custom_call" | custom-call | tf_op jit(solution)/shard_map/pallas_call | solution.py:27
  27.0 14.7 %all_to_all.31 = f32[16,8,512]{2,1,0:T(8,128)S(1)} all-to-all(f32[16,8,512]{2,1,0:T(8,128)S(1)} %shard_map.93), channel_id=1, replica_groups=mesh['grid'=16,'z'=8,'core'=2] {'grid'}, dimensions={0} | all-to-all | bytes 524288 | tf_op jit(solution)/shard_map/all_to_all | solution.py:341
  41.8 10.2 %all_to_all.32.pcs_ref = f32[16,8,512]{2,1,0:T(8,128)S(1)} all-to-all(f32[16,8,512]{2,1,0:T(8,128)S(1)} %broadcast_in_dim.6), channel_id=1, replica_groups=mesh['grid'=16,'z'=8,'core'=2] {'grid'}, dimensions={0} | all-to-all | bytes 524288 | tf_op jit(solution)/shard_map/all_to_all | solution.py:342
  52.0 0.0 copy-done.2
  52.0 0.0 copy-done.4
  52.0 2.3 %shard_map.94 = (f32[72,128]{1,0:T(8,128)S(1)}, f32[72,128]{1,0:T(8,128)S(1)}, f32[8,128]{1,0:T(8,128)S(1)}) custom-call(f32[16,8,512]{2,1,0:T(8,128)S(1)} %all_to_all.32.pcs_ref, f32[8,64]{1,0:T(8,128)S(1)} %copy-done.2, f32[8,64]{1,0:T(8,128)S(1)} %copy-done.3, f32[8]{0:T(128)S(1)} %copy-done.4), custom_call_target="tpu_custom_call" | custom-call | tf_op jit(solution)/shard_map/pallas_call | solution.py:27
  54.3 3.0 %collective-permute-start.1 = (f32[72,128]{1,0:T(8,128)S(1)}, f32[72,128]{1,0:T(8,128)S(1)}, u32[]{:S(2)}, u32[]{:S(2)}) collective-permute-start(f32[72,128]{1,0:T(8,128)S(1)} %get-tuple-element.17), channel_id=1, source_target_pairs={{0,1},{1,0},{2,3},{3,2},{4,5},{5,4},{6,7},{7,6},{8,9},{9,8},{10,11... | collective-permute-start | bytes 110600 | tf_op jit(solution)/shard_map/ppermute | solution.py:326
  57.2 0.9 collective-permute-done.1
  58.1 15.0 %all_to_all.33.parts_ref = f32[8,72,128]{2,1,0:T(8,128)S(1)} all-to-all(f32[8,72,128]{2,1,0:T(8,128)S(1)} %broadcast_in_dim.7), channel_id=1, replica_groups=mesh['grid'=16,'z'=8,'core'=2] {'z'}, dimensions={0} | all-to-all | bytes 589824 | tf_op jit(solution)/shard_map/all_to_all | solution.py:327
  73.2 3.4 %shard_map.95.keep_ref = f32[136,128]{1,0:T(8,128)S(1)} custom-call(f32[8,72,128]{2,1,0:T(8,128)S(1)} %all_to_all.33.parts_ref, f32[8,128]{1,0:T(8,128)S(1)} %get-tuple-element.18.shift_ref), custom_call_target="tpu_custom_call" | custom-call | flops 199999995904 | tf_op jit(solution)/shard_map/pallas_call | solution.py:27
  76.6 0.9 collective-permute-start.2
  77.6 0.9 collective-permute-done.2.got_ref
  78.5 3.0 %shard_map.96 = (f32[72,128]{1,0:T(8,128)S(1)}, f32[72,128]{1,0:T(8,128)S(1)}, f32[8,128]{1,0:T(8,128)S(1)}) custom-call(f32[16,8,512]{2,1,0:T(8,128)S(1)} %all_to_all.32.pcs_ref, f32[136,128]{1,0:T(8,128)S(1)} %shard_map.95.keep_ref, f32[136,128]{1,0:T(8,128)S(1)} %collective-permute-done.2.got_ref), custom_call_target="tpu_custom_call" | custom-call | tf_op jit(solution)/shard_map/pallas_call | solution.py:27
  81.5 0.4 collective-permute-start.3
  81.9 0.9 collective-permute-done.3
  82.8 15.0 %all_to_all.34.parts_ref = f32[8,72,128]{2,1,0:T(8,128)S(1)} all-to-all(f32[8,72,128]{2,1,0:T(8,128)S(1)} %broadcast_in_dim.8), channel_id=1, replica_groups=mesh['grid'=16,'z'=8,'core'=2] {'z'}, dimensions={0} | all-to-all | bytes 589824 | tf_op jit(solution)/shard_map/all_to_all | solution.py:327
  97.9 3.4 %shard_map.97.keep_ref = f32[264,128]{1,0:T(8,128)S(1)} custom-call(f32[8,72,128]{2,1,0:T(8,128)S(1)} %all_to_all.34.parts_ref, f32[8,128]{1,0:T(8,128)S(1)} %get-tuple-element.21.shift_ref), custom_call_target="tpu_custom_call" | custom-call | flops 199999995904 | tf_op jit(solution)/shard_map/pallas_call | solution.py:27
  101.3 1.0 collective-permute-start.4
  102.3 1.0 collective-permute-done.4.got_ref
  103.3 3.3 %shard_map.98 = (f32[8,1024]{1,0:T(8,128)}, f32[16,8,384]{2,1,0:T(8,128)S(1)}, f32[8,64]{1,0:T(8,128)}, f32[8,64,64]{2,1,0:T(8,128)}, f32[8]{0:T(128)}) custom-call(f32[16,8,512]{2,1,0:T(8,128)S(1)} %all_to_all.32.pcs_ref, f32[264,128]{1,0:T(8,128)S(1)} %shard_map.97.keep_ref, f32[264,128]{1,0:T(8,128)S(1)} %collective-permute-done.4.got_ref, ...), custom_call_target="tpu_custom_call" | custom-call | tf_op jit(solution)/shard_map/pallas_call | solution.py:27
  106.6 13.2 %all_to_all.35 = f32[16,8,384]{2,1,0:T(8,128)S(1)} all-to-all(f32[16,8,384]{2,1,0:T(8,128)S(1)} %get-tuple-element.26), channel_id=1, replica_groups=mesh['grid'=16,'z'=8,'core'=2] {'z','core'}, dimensions={0} | all-to-all | bytes 393216 | tf_op jit(solution)/shard_map/all_to_all | solution.py:353
  119.8 0.1 fusion.1
  119.9 0.7 fusion
  (12 shorter events, 0.1 us)
Async XLA Ops:
  0.6 0.8 copy-start.5
  1.4 23.1 %copy-start = (bf16[1024,4096]{1,0:T(8,128)(2,1)S(1)}, bf16[1024,4096]{1,0:T(8,128)(2,1)}, u32[]{:S(2)}) copy-start(bf16[1024,4096]{1,0:T(8,128)(2,1)} %fields_ref.3) | copy-start | bytes 25165828
  1.4 50.6 %copy-start.2 = (f32[8,64]{1,0:T(8,128)S(1)}, f32[8,64]{1,0:T(8,128)}, u32[]{:S(2)}) copy-start(f32[8,64]{1,0:T(8,128)} %means_ref.1) | copy-start | bytes 6148
  1.4 50.6 %copy-start.3 = (f32[8,64]{1,0:T(8,128)S(1)}, f32[8,64]{1,0:T(8,128)}, u32[]{:S(2)}) copy-start(f32[8,64]{1,0:T(8,128)} %variances_ref.1) | copy-start | bytes 6148
  1.4 50.6 %copy-start.4 = (f32[8]{0:T(128)S(1)}, f32[8]{0:T(128)}, u32[]{:S(2)}) copy-start(f32[8]{0:T(128)} %mixing_ref.1) | copy-start | bytes 100
  20.9 3.6 %collective-permute-start = (bf16[8,64,256]{2,1,0:T(8,128)(2,1)S(1)}, bf16[8,64,256]{2,1,0:T(8,128)(2,1)S(1)}, u32[]{:S(2)}, u32[]{:S(2)}) collective-permute-start(bf16[8,64,256]{2,1,0:T(8,128)(2,1)S(1)} %all_to_all.30.own_ref), channel_id=1, source_target_pairs={{0,1},{1,0},{2,3},{3,2},{4,5},{5,4},{6,7},{7,6},{8,9},{9,8},{10,11... | collective-permute-start | bytes 786440 | tf_op jit(solution)/shard_map/ppermute | solution.py:338
  54.3 3.8 %collective-permute-start.1 = (f32[72,128]{1,0:T(8,128)S(1)}, f32[72,128]{1,0:T(8,128)S(1)}, u32[]{:S(2)}, u32[]{:S(2)}) collective-permute-start(f32[72,128]{1,0:T(8,128)S(1)} %get-tuple-element.17), channel_id=1, source_target_pairs={{0,1},{1,0},{2,3},{3,2},{4,5},{5,4},{6,7},{7,6},{8,9},{9,8},{10,11... | collective-permute-start | bytes 110600 | tf_op jit(solution)/shard_map/ppermute | solution.py:326
  76.6 1.8 %collective-permute-start.2 = (f32[136,128]{1,0:T(8,128)S(1)}, f32[136,128]{1,0:T(8,128)S(1)}, u32[]{:S(2)}, u32[]{:S(2)}) collective-permute-start(f32[136,128]{1,0:T(8,128)S(1)} %shard_map.95.keep_ref), channel_id=1, source_target_pairs={{0,1},{1,0},{2,3},{3,2},{4,5},{5,4},{6,7},{7,6},{8,9},{9,8},{10,11... | collective-permute-start | bytes 208904 | tf_op jit(solution)/shard_map/ppermute | solution.py:329
  81.5 1.3 %collective-permute-start.3 = (f32[72,128]{1,0:T(8,128)S(1)}, f32[72,128]{1,0:T(8,128)S(1)}, u32[]{:S(2)}, u32[]{:S(2)}) collective-permute-start(f32[72,128]{1,0:T(8,128)S(1)} %get-tuple-element.20), channel_id=1, source_target_pairs={{0,1},{1,0},{2,3},{3,2},{4,5},{5,4},{6,7},{7,6},{8,9},{9,8},{10,11... | collective-permute-start | bytes 110600 | tf_op jit(solution)/shard_map/ppermute | solution.py:326
  97.9 5.4 %copy-start.1 = (bf16[1024,4096]{1,0:T(8,128)(2,1)S(1)}, bf16[1024,4096]{1,0:T(8,128)(2,1)}, u32[]{:S(2)}) copy-start(bf16[1024,4096]{1,0:T(8,128)(2,1)} %fields_ref.3) | copy-start | bytes 25165828
  101.3 1.9 %collective-permute-start.4 = (f32[264,128]{1,0:T(8,128)S(1)}, f32[264,128]{1,0:T(8,128)S(1)}, u32[]{:S(2)}, u32[]{:S(2)}) collective-permute-start(f32[264,128]{1,0:T(8,128)S(1)} %shard_map.97.keep_ref), channel_id=1, source_target_pairs={{0,1},{1,0},{2,3},{3,2},{4,5},{5,4},{6,7},{7,6},{8,9},{9,8},{10,11... | collective-permute-start | bytes 405512 | tf_op jit(solution)/shard_map/ppermute | solution.py:329

commit v7 on v6

--- a/solution.py
+++ b/solution.py
@@ -21,14 +21,16 @@
 COVER = pl.CostEstimate(flops=20 * 10 ** 10, transcendentals=0, bytes_accessed=0)
 VMEM = pl.BlockSpec(memory_space=pltpu.VMEM)
 SMEM = pl.BlockSpec(memory_space=pltpu.SMEM)
-
-
-def call(kernel, outs, operands, limit=LIMIT, cost=None, scalars=0, scalar_outs=0):
+HBM = pl.BlockSpec(memory_space=pltpu.HBM)
+
+
+def call(kernel, outs, operands, limit=LIMIT, cost=None, scalars=0, places=None, scratch=()):
     return pl.pallas_call(
         kernel,
         out_shape=tuple(jax.ShapeDtypeStruct(s, d) for s, d in outs),
         in_specs=[VMEM] * (len(operands) - scalars) + [SMEM] * scalars,
-        out_specs=tuple([VMEM] * (len(outs) - scalar_outs) + [SMEM] * scalar_outs),
+        out_specs=tuple(places or [VMEM] * len(outs)),
+        scratch_shapes=scratch,
         compiler_params=pltpu.CompilerParams(vmem_limit_bytes=limit),
         cost_estimate=cost,
     )(*operands)
@@ -51,26 +53,47 @@
 
 def eliminate(pairs):
     sub, half, col = tile_ids()
-    for k in range(0, K, 2):
+    for k in range(0, K, 4):
         g, s = divmod(k, 8)
-        at0, at1 = half + k, half + k + 1
-        here0, here1 = col == k, col == k + 1
-        here = here0 | here1
+        at = [half + (k + q) for q in range(4)]
+        here = [col == k + q for q in range(4)]
+        one = [h.astype(F32) for h in here]
+        low, high = here[0] | here[1], here[2] | here[3]
         for groups in pairs:
-            row0 = jnp.broadcast_to(groups[g][s:s + 1, :], (8, 128))
-            row1 = jnp.broadcast_to(groups[g][s + 1:s + 2, :], (8, 128))
-            a, b, c = lanes_of(row0, at0), lanes_of(row0, at1), lanes_of(row1, at1)
+            rows = [jnp.broadcast_to(groups[g][s + q:s + q + 1, :], (8, 128)) for q in range(4)]
+            a, b, c = lanes_of(rows[0], at[0]), lanes_of(rows[0], at[1]), lanes_of(rows[1], at[1])
+            p02, p03 = lanes_of(rows[0], at[2]), lanes_of(rows[0], at[3])
+            p12, p13 = lanes_of(rows[1], at[2]), lanes_of(rows[1], at[3])
+            p22, p23, p33 = lanes_of(rows[2], at[2]), lanes_of(rows[2], at[3]), lanes_of(rows[3], at[3])
             scale = 1.0 / (a * c - b * b)
-            row0 = jnp.where(here, here0.astype(F32), row0) * scale
-            row1 = jnp.where(here, here1.astype(F32), row1) * scale
-            scaled0 = c * row0 - b * row1
-            scaled1 = a * row1 - b * row0
+            row0 = jnp.where(low, one[0], rows[0])
+            row1 = jnp.where(low, one[1], rows[1])
+            turned0 = c * row0 - b * row1
+            turned1 = a * row1 - b * row0
+            g02, g12 = (c * p02 - b * p12) * scale, (a * p12 - b * p02) * scale
+            g03, g13 = (c * p03 - b * p13) * scale, (a * p13 - b * p03) * scale
+            s22 = p22 - (p02 * g02 + p12 * g12)
+            s23 = p23 - (p02 * g03 + p12 * g13)
+            s33 = p33 - (p03 * g03 + p13 * g13)
+            row2 = jnp.where(low, 0.0, rows[2]) - (p02 * turned0 + p12 * turned1) * scale
+            row3 = jnp.where(low, 0.0, rows[3]) - (p03 * turned0 + p13 * turned1) * scale
+            again = 1.0 / (s22 * s33 - s23 * s23)
+            row2 = jnp.where(high, one[2], row2)
+            row3 = jnp.where(high, one[3], row3)
+            turned2 = s33 * row2 - s23 * row3
+            turned3 = s22 * row3 - s23 * row2
             for i in range(g, 8):
-                if i == g and s == 6:
+                f0, f1, f2, f3 = [lanes_of(groups[i], x) for x in at]
+                new = jnp.where(low, 0.0, groups[i]) - (f0 * turned0 + f1 * turned1) * scale
+                if i == g:
+                    new = jnp.where(sub > s + 1, new, groups[i])
+                groups[i] = new
+                if i == g and s == 4:
                     continue
-                f0, f1 = lanes_of(groups[i], at0), lanes_of(groups[i], at1)
-                new = jnp.where(here, 0.0, groups[i]) - f0 * scaled0 - f1 * scaled1
-                groups[i] = jnp.where(sub > s + 1, new, groups[i]) if i == g else new
+                f2 = f2 - (f0 * g02 + f1 * g12)
+                f3 = f3 - (f0 * g03 + f1 * g13)
+                new = jnp.where(high, 0.0, new) - (f2 * turned2 + f3 * turned3) * again
+                groups[i] = jnp.where(sub > s + 3, new, groups[i]) if i == g else new
     odd = (sub & 1) == 1
     results = []
     for groups in pairs:
@@ -143,12 +166,11 @@
     row_id = lax.broadcasted_iota(jnp.int32, (K, K), 0)
     col_id = lax.broadcasted_iota(jnp.int32, (K, K), 1)
     left = jnp.concatenate([centred * resp[r:r + 1, :] for r in range(R)] + [resp], axis=0)
-    high, middle, low = split(left)
+    high, middle, _ = split(left)
     contract = (((1,), (1,)), ((), ()))
     got = lax.dot_general(high, jnp.concatenate(terms, axis=0), contract, preferred_element_type=F32)
     more = lax.dot_general(middle, jnp.concatenate(terms[:2], axis=0), contract, preferred_element_type=F32)
-    last = lax.dot_general(low, terms[0], contract, preferred_element_type=F32)
-    got = got[:, :K] + (got[:, K:2 * K] + more[:, :K]) + (got[:, 2 * K:] + more[:, K:] + last)
+    got = got[:, :K] + (got[:, K:2 * K] + more[:, :K]) + (got[:, 2 * K:] + more[:, K:])
     seconds = [got[K * r:K * r + K] for r in range(R)]
     firsts = [got[K * R + r:K * R + r + 1] for r in range(R)]
     packs = []
@@ -299,23 +321,33 @@
     moments(core, centred, terms, resp, out_keep_ref, out_send_ref)
 
 
-def last_kernel(pcs_ref, keep_ref, got_ref, fields_ref, member_ref, terms_ref, means_ref, covs_ref, weights_ref):
+def last_kernel(pcs_ref, keep_ref, got_ref, fields_ref, terms_ref, member_hbm, means_hbm, covs_hbm, weights_ref,
+                member_ref, means_ref, covs_ref, sems):
+    copies = [
+        pltpu.make_async_copy(source, target, sems.at[i])
+        for i, (source, target) in enumerate(
+            ((covs_ref, covs_hbm), (member_ref, member_hbm), (means_ref, means_hbm)))]
     core = lax.axis_index("core")
     halves = halves_of(core, keep_ref, got_ref)
     for r in range(R):
         h, p, offset = regime_of(r)
         at = INFO + 8 + K * p
         covs_ref[r] = halves[h][at:at + K, offset:offset + K]
+    copies[0].start()
     member, weights, means, _, _, _ = expect(read_pcs(pcs_ref), halves)
     member_ref[...] = member
+    copies[1].start()
+    means_ref[...] = means
+    copies[2].start()
     for r in range(R):
         weights_ref[r] = weights[r, 0]
-    means_ref[...] = means
     count = jnp.broadcast_to(jnp.sum(member, axis=1, keepdims=True), (R, 128))
     rounded = member.astype(BF16)
     for j in range(16):
         terms_ref[j, :, 0:256] = jnp.dot(rounded, fields_ref[:, 256 * j:256 * j + 256], preferred_element_type=F32)
         terms_ref[j, :, 256:384] = count
+    for copy in copies:
+        copy.wait()
 
 
 def spread(x, n):
@@ -346,10 +378,11 @@
     block, got = merge(keep, send, shift, INFO + 8)
     keep, send, shift = call(middle_kernel, pack, [pcs, block, got])
     block, got = merge(keep, send, shift, INFO + 8 + 2 * K)
-    member, terms, means, covs, weights = call(
-        last_kernel,
-        [((R, days), F32), ((16, R, 384), F32), ((R, K), F32), ((R, K, K), F32), ((R,), F32)],
-        [pcs, block, got, anomalies], limit=SMALL, scalar_outs=1)
+    results = [((R, days), F32), ((R, K), F32), ((R, K, K), F32)]
+    terms, member, means, covs, weights = call(
+        last_kernel, [((16, R, 384), F32)] + results + [((R,), F32)],
+        [pcs, block, got, anomalies], limit=SMALL, places=[VMEM, HBM, HBM, HBM, SMEM],
+        scratch=[pltpu.VMEM(*one) for one in results] + [pltpu.SemaphoreType.DMA((3,))])
     sums = jnp.sum(lax.all_to_all(terms, ("z", "core"), 0, 0), axis=0)
     composites = (sums[:, :256] / jnp.maximum(sums[:, 256:257], 1.0)).astype(BF16)
 

time: 121 us -> 119 us (0.983)
  Pallas kernels: 18 us -> 16.5 us
    pallas_call x7, Pallas kernels: 18 us -> 16.5 us  [call(): pl.pallas_call(kernel, out_shape=tuple((jax.ShapeDtypeStruct(s, d) for s,...]
where the time goes in v7:
time: 119 us
  blocking collectives  87.6 us (74%)
  Pallas kernels  16.5 us (14%)
  starting transfers between devices  7.75 us (7%)
  waiting for transfers between devices  4.79 us (4%)
    all_to_all x2, blocking collectives, merge(): parts = lax.all_to_all(spread(half, 8), 'z', 0, 0)  30.1 us
    all_to_all x1, blocking collectives, body(): own = lax.all_to_all(eight, 'z', 0, 0)  19.4 us
    pallas_call x7, Pallas kernels, call(): pl.pallas_call(kernel, out_shape=tuple((jax.ShapeDtypeStruct(s, d) for s,...  16.5 us
    all_to_all x1, blocking collectives, body(): mine = jnp.sum(lax.all_to_all(partial, 'grid', 0, 0), axis=0)  14.7 us
    all_to_all x1, blocking collectives, body(): sums = jnp.sum(lax.all_to_all(terms, ('z', 'core'), 0, 0), axis=0)  13.2 us
    all_to_all x1, blocking collectives, body(): pcs = lax.all_to_all(spread(mine, 16), 'grid', 0, 0)  10.2 us
    ppermute x2, starting transfers between devices, merge(): half = keep + lax.ppermute(send, 'core', SWAP)  3.39 us
    ppermute x1, starting transfers between devices, body(): other = lax.ppermute(own, 'core', SWAP)  2.46 us
  transfers between devices with their start and end apart: 5, of which 5 were waited for; matrix products, arithmetic and copies ran while one was open for 0% of the time, Pallas kernels for 0%

profile of v7, /device:TPU:1, one launch (start us, length us, event | category | flops | bytes accessed | tf_op | source)
XLA Modules:
  0.0 119.1 jit_solution(2722687565233248108)
XLA Ops:
  0.6 0.0 copy-start.5
  0.6 0.7 copy-done.5
  1.4 0.0 copy-start.2
  1.4 0.0 copy-start.3
  1.4 0.0 copy-start.4
  1.4 19.4 %all_to_all.30.own_ref = bf16[8,64,256]{2,1,0:T(8,128)(2,1)S(1)} all-to-all(bf16[8,64,256]{2,1,0:T(8,128)(2,1)S(1)} %shard_map.92), channel_id=1, replica_groups=mesh['grid'=16,'z'=8,'core'=2] {'z'}, dimensions={0} | all-to-all | bytes 524288 | tf_op jit(solution)/shard_map/all_to_all | solution.py:369
  20.9 2.5 %collective-permute-start = (bf16[8,64,256]{2,1,0:T(8,128)(2,1)S(1)}, bf16[8,64,256]{2,1,0:T(8,128)(2,1)S(1)}, u32[]{:S(2)}, u32[]{:S(2)}) collective-permute-start(bf16[8,64,256]{2,1,0:T(8,128)(2,1)S(1)} %all_to_all.30.own_ref), channel_id=1, source_target_pairs={{0,1},{1,0},{2,3},{3,2},{4,5},{5,4},{6,7},{7,6},{8,9},{9,8},{10,11... | collective-permute-start | bytes 786440 | tf_op jit(solution)/shard_map/ppermute | solution.py:370
  23.4 1.2 collective-permute-done.other_ref
  24.5 0.0 copy-done
  24.5 2.5 %shard_map.93 = f32[16,8,512]{2,1,0:T(8,128)S(1)} custom-call(bf16[8,64,256]{2,1,0:T(8,128)(2,1)S(1)} %all_to_all.30.own_ref, bf16[8,64,256]{2,1,0:T(8,128)(2,1)S(1)} %collective-permute-done.other_ref, bf16[1024,4096]{1,0:T(8,128)(2,1)S(1)} %copy-done), custom_call_target="tpu_custom_call" | custom-call | tf_op jit(solution)/shard_map/pallas_call | solution.py:28
  27.0 14.7 %all_to_all.31 = f32[16,8,512]{2,1,0:T(8,128)S(1)} all-to-all(f32[16,8,512]{2,1,0:T(8,128)S(1)} %shard_map.93), channel_id=1, replica_groups=mesh['grid'=16,'z'=8,'core'=2] {'grid'}, dimensions={0} | all-to-all | bytes 524288 | tf_op jit(solution)/shard_map/all_to_all | solution.py:373
  41.8 10.2 %all_to_all.32.pcs_ref = f32[16,8,512]{2,1,0:T(8,128)S(1)} all-to-all(f32[16,8,512]{2,1,0:T(8,128)S(1)} %broadcast_in_dim.6), channel_id=1, replica_groups=mesh['grid'=16,'z'=8,'core'=2] {'grid'}, dimensions={0} | all-to-all | bytes 524288 | tf_op jit(solution)/shard_map/all_to_all | solution.py:374
  52.0 0.0 copy-done.2
  52.0 0.0 copy-done.4
  52.0 2.1 %shard_map.94 = (f32[72,128]{1,0:T(8,128)S(1)}, f32[72,128]{1,0:T(8,128)S(1)}, f32[8,128]{1,0:T(8,128)S(1)}) custom-call(f32[16,8,512]{2,1,0:T(8,128)S(1)} %all_to_all.32.pcs_ref, f32[8,64]{1,0:T(8,128)S(1)} %copy-done.2, f32[8,64]{1,0:T(8,128)S(1)} %copy-done.3, f32[8]{0:T(128)S(1)} %copy-done.4), custom_call_target="tpu_custom_call" | custom-call | tf_op jit(solution)/shard_map/pallas_call | solution.py:28
  54.1 3.0 %collective-permute-start.1 = (f32[72,128]{1,0:T(8,128)S(1)}, f32[72,128]{1,0:T(8,128)S(1)}, u32[]{:S(2)}, u32[]{:S(2)}) collective-permute-start(f32[72,128]{1,0:T(8,128)S(1)} %get-tuple-element.17), channel_id=1, source_target_pairs={{0,1},{1,0},{2,3},{3,2},{4,5},{5,4},{6,7},{7,6},{8,9},{9,8},{10,11... | collective-permute-start | bytes 110600 | tf_op jit(solution)/shard_map/ppermute | solution.py:358
  57.1 0.9 collective-permute-done.1
  58.0 15.0 %all_to_all.33.parts_ref = f32[8,72,128]{2,1,0:T(8,128)S(1)} all-to-all(f32[8,72,128]{2,1,0:T(8,128)S(1)} %broadcast_in_dim.7), channel_id=1, replica_groups=mesh['grid'=16,'z'=8,'core'=2] {'z'}, dimensions={0} | all-to-all | bytes 589824 | tf_op jit(solution)/shard_map/all_to_all | solution.py:359
  73.0 2.8 %shard_map.95.keep_ref = f32[136,128]{1,0:T(8,128)S(1)} custom-call(f32[8,72,128]{2,1,0:T(8,128)S(1)} %all_to_all.33.parts_ref, f32[8,128]{1,0:T(8,128)S(1)} %get-tuple-element.18.shift_ref), custom_call_target="tpu_custom_call" | custom-call | flops 199999995904 | tf_op jit(solution)/shard_map/pallas_call | solution.py:28
  75.9 0.9 collective-permute-start.2
  76.8 0.9 collective-permute-done.2.got_ref
  77.7 2.4 %shard_map.96 = (f32[72,128]{1,0:T(8,128)S(1)}, f32[72,128]{1,0:T(8,128)S(1)}, f32[8,128]{1,0:T(8,128)S(1)}) custom-call(f32[16,8,512]{2,1,0:T(8,128)S(1)} %all_to_all.32.pcs_ref, f32[136,128]{1,0:T(8,128)S(1)} %shard_map.95.keep_ref, f32[136,128]{1,0:T(8,128)S(1)} %collective-permute-done.2.got_ref), custom_call_target="tpu_custom_call" | custom-call | tf_op jit(solution)/shard_map/pallas_call | solution.py:28
  80.1 0.4 collective-permute-start.3
  80.5 0.9 collective-permute-done.3
  81.4 15.0 %all_to_all.34.parts_ref = f32[8,72,128]{2,1,0:T(8,128)S(1)} all-to-all(f32[8,72,128]{2,1,0:T(8,128)S(1)} %broadcast_in_dim.8), channel_id=1, replica_groups=mesh['grid'=16,'z'=8,'core'=2] {'z'}, dimensions={0} | all-to-all | bytes 589824 | tf_op jit(solution)/shard_map/all_to_all | solution.py:359
  96.5 2.8 %shard_map.97.keep_ref = f32[264,128]{1,0:T(8,128)S(1)} custom-call(f32[8,72,128]{2,1,0:T(8,128)S(1)} %all_to_all.34.parts_ref, f32[8,128]{1,0:T(8,128)S(1)} %get-tuple-element.21.shift_ref), custom_call_target="tpu_custom_call" | custom-call | flops 199999995904 | tf_op jit(solution)/shard_map/pallas_call | solution.py:28
  99.3 1.0 collective-permute-start.4
  100.3 1.0 collective-permute-done.4.got_ref
  101.3 3.8 %shard_map.98 = (f32[16,8,384]{2,1,0:T(8,128)S(1)}, f32[8,1024]{1,0:T(8,128)}, f32[8,64]{1,0:T(8,128)}, f32[8,64,64]{2,1,0:T(8,128)}, f32[8]{0:T(128)}) custom-call(f32[16,8,512]{2,1,0:T(8,128)S(1)} %all_to_all.32.pcs_ref, f32[264,128]{1,0:T(8,128)S(1)} %shard_map.97.keep_ref, f32[264,128]{1,0:T(8,128)S(1)} %collective-permute-done.4.got_ref, ...), custom_call_target="tpu_custom_call" | custom-call | tf_op jit(solution)/shard_map/pallas_call | solution.py:28
  105.1 13.2 %all_to_all.35 = f32[16,8,384]{2,1,0:T(8,128)S(1)} all-to-all(f32[16,8,384]{2,1,0:T(8,128)S(1)} %get-tuple-element.26), channel_id=1, replica_groups=mesh['grid'=16,'z'=8,'core'=2] {'z','core'}, dimensions={0} | all-to-all | bytes 393216 | tf_op jit(solution)/shard_map/all_to_all | solution.py:386
  118.3 0.1 fusion.1
  118.4 0.7 fusion
  (12 shorter events, 0.1 us)
Async XLA Ops:
  0.6 0.8 copy-start.5
  1.4 23.1 %copy-start = (bf16[1024,4096]{1,0:T(8,128)(2,1)S(1)}, bf16[1024,4096]{1,0:T(8,128)(2,1)}, u32[]{:S(2)}) copy-start(bf16[1024,4096]{1,0:T(8,128)(2,1)} %fields_ref.3) | copy-start | bytes 25165828
  1.4 50.6 %copy-start.2 = (f32[8,64]{1,0:T(8,128)S(1)}, f32[8,64]{1,0:T(8,128)}, u32[]{:S(2)}) copy-start(f32[8,64]{1,0:T(8,128)} %means_ref.1) | copy-start | bytes 6148
  1.4 50.6 %copy-start.3 = (f32[8,64]{1,0:T(8,128)S(1)}, f32[8,64]{1,0:T(8,128)}, u32[]{:S(2)}) copy-start(f32[8,64]{1,0:T(8,128)} %variances_ref.1) | copy-start | bytes 6148
  1.4 50.6 %copy-start.4 = (f32[8]{0:T(128)S(1)}, f32[8]{0:T(128)}, u32[]{:S(2)}) copy-start(f32[8]{0:T(128)} %mixing_ref.1) | copy-start | bytes 100
  20.9 3.6 %collective-permute-start = (bf16[8,64,256]{2,1,0:T(8,128)(2,1)S(1)}, bf16[8,64,256]{2,1,0:T(8,128)(2,1)S(1)}, u32[]{:S(2)}, u32[]{:S(2)}) collective-permute-start(bf16[8,64,256]{2,1,0:T(8,128)(2,1)S(1)} %all_to_all.30.own_ref), channel_id=1, source_target_pairs={{0,1},{1,0},{2,3},{3,2},{4,5},{5,4},{6,7},{7,6},{8,9},{9,8},{10,11... | collective-permute-start | bytes 786440 | tf_op jit(solution)/shard_map/ppermute | solution.py:370
  54.1 3.8 %collective-permute-start.1 = (f32[72,128]{1,0:T(8,128)S(1)}, f32[72,128]{1,0:T(8,128)S(1)}, u32[]{:S(2)}, u32[]{:S(2)}) collective-permute-start(f32[72,128]{1,0:T(8,128)S(1)} %get-tuple-element.17), channel_id=1, source_target_pairs={{0,1},{1,0},{2,3},{3,2},{4,5},{5,4},{6,7},{7,6},{8,9},{9,8},{10,11... | collective-permute-start | bytes 110600 | tf_op jit(solution)/shard_map/ppermute | solution.py:358
  75.9 1.8 %collective-permute-start.2 = (f32[136,128]{1,0:T(8,128)S(1)}, f32[136,128]{1,0:T(8,128)S(1)}, u32[]{:S(2)}, u32[]{:S(2)}) collective-permute-start(f32[136,128]{1,0:T(8,128)S(1)} %shard_map.95.keep_ref), channel_id=1, source_target_pairs={{0,1},{1,0},{2,3},{3,2},{4,5},{5,4},{6,7},{7,6},{8,9},{9,8},{10,11... | collective-permute-start | bytes 208904 | tf_op jit(solution)/shard_map/ppermute | solution.py:361
  80.1 1.3 %collective-permute-start.3 = (f32[72,128]{1,0:T(8,128)S(1)}, f32[72,128]{1,0:T(8,128)S(1)}, u32[]{:S(2)}, u32[]{:S(2)}) collective-permute-start(f32[72,128]{1,0:T(8,128)S(1)} %get-tuple-element.20), channel_id=1, source_target_pairs={{0,1},{1,0},{2,3},{3,2},{4,5},{5,4},{6,7},{7,6},{8,9},{9,8},{10,11... | collective-permute-start | bytes 110600 | tf_op jit(solution)/shard_map/ppermute | solution.py:358
  96.5 4.8 %copy-start.1 = (bf16[1024,4096]{1,0:T(8,128)(2,1)S(1)}, bf16[1024,4096]{1,0:T(8,128)(2,1)}, u32[]{:S(2)}) copy-start(bf16[1024,4096]{1,0:T(8,128)(2,1)} %fields_ref.3) | copy-start | bytes 25165828
  99.3 1.9 %collective-permute-start.4 = (f32[264,128]{1,0:T(8,128)S(1)}, f32[264,128]{1,0:T(8,128)S(1)}, u32[]{:S(2)}, u32[]{:S(2)}) collective-permute-start(f32[264,128]{1,0:T(8,128)S(1)} %shard_map.97.keep_ref), channel_id=1, source_target_pairs={{0,1},{1,0},{2,3},{3,2},{4,5},{5,4},{6,7},{7,6},{8,9},{9,8},{10,11... | collective-permute-start | bytes 405512 | tf_op jit(solution)/shard_map/ppermute | solution.py:361

commit v8 on v7

--- a/solution.py
+++ b/solution.py
@@ -21,16 +21,14 @@
 COVER = pl.CostEstimate(flops=20 * 10 ** 10, transcendentals=0, bytes_accessed=0)
 VMEM = pl.BlockSpec(memory_space=pltpu.VMEM)
 SMEM = pl.BlockSpec(memory_space=pltpu.SMEM)
-HBM = pl.BlockSpec(memory_space=pltpu.HBM)
-
-
-def call(kernel, outs, operands, limit=LIMIT, cost=None, scalars=0, places=None, scratch=()):
+
+
+def call(kernel, outs, operands, limit=LIMIT, cost=None, scalars=0, scalar_outs=0):
     return pl.pallas_call(
         kernel,
         out_shape=tuple(jax.ShapeDtypeStruct(s, d) for s, d in outs),
         in_specs=[VMEM] * (len(operands) - scalars) + [SMEM] * scalars,
-        out_specs=tuple(places or [VMEM] * len(outs)),
-        scratch_shapes=scratch,
+        out_specs=tuple([VMEM] * (len(outs) - scalar_outs) + [SMEM] * scalar_outs),
         compiler_params=pltpu.CompilerParams(vmem_limit_bytes=limit),
         cost_estimate=cost,
     )(*operands)
@@ -321,33 +319,23 @@
     moments(core, centred, terms, resp, out_keep_ref, out_send_ref)
 
 
-def last_kernel(pcs_ref, keep_ref, got_ref, fields_ref, terms_ref, member_hbm, means_hbm, covs_hbm, weights_ref,
-                member_ref, means_ref, covs_ref, sems):
-    copies = [
-        pltpu.make_async_copy(source, target, sems.at[i])
-        for i, (source, target) in enumerate(
-            ((covs_ref, covs_hbm), (member_ref, member_hbm), (means_ref, means_hbm)))]
+def last_kernel(pcs_ref, keep_ref, got_ref, fields_ref, member_ref, terms_ref, means_ref, covs_ref, weights_ref):
     core = lax.axis_index("core")
     halves = halves_of(core, keep_ref, got_ref)
     for r in range(R):
         h, p, offset = regime_of(r)
         at = INFO + 8 + K * p
         covs_ref[r] = halves[h][at:at + K, offset:offset + K]
-    copies[0].start()
     member, weights, means, _, _, _ = expect(read_pcs(pcs_ref), halves)
     member_ref[...] = member
-    copies[1].start()
+    for r in range(R):
+        weights_ref[r] = weights[r, 0]
     means_ref[...] = means
-    copies[2].start()
-    for r in range(R):
-        weights_ref[r] = weights[r, 0]
     count = jnp.broadcast_to(jnp.sum(member, axis=1, keepdims=True), (R, 128))
     rounded = member.astype(BF16)
     for j in range(16):
         terms_ref[j, :, 0:256] = jnp.dot(rounded, fields_ref[:, 256 * j:256 * j + 256], preferred_element_type=F32)
         terms_ref[j, :, 256:384] = count
-    for copy in copies:
-        copy.wait()
 
 
 def spread(x, n):
@@ -378,11 +366,10 @@
     block, got = merge(keep, send, shift, INFO + 8)
     keep, send, shift = call(middle_kernel, pack, [pcs, block, got])
     block, got = merge(keep, send, shift, INFO + 8 + 2 * K)
-    results = [((R, days), F32), ((R, K), F32), ((R, K, K), F32)]
-    terms, member, means, covs, weights = call(
-        last_kernel, [((16, R, 384), F32)] + results + [((R,), F32)],
-        [pcs, block, got, anomalies], limit=SMALL, places=[VMEM, HBM, HBM, HBM, SMEM],
-        scratch=[pltpu.VMEM(*one) for one in results] + [pltpu.SemaphoreType.DMA((3,))])
+    member, terms, means, covs, weights = call(
+        last_kernel,
+        [((R, days), F32), ((16, R, 384), F32), ((R, K), F32), ((R, K, K), F32), ((R,), F32)],
+        [pcs, block, got, anomalies], limit=SMALL, scalar_outs=1)
     sums = jnp.sum(lax.all_to_all(terms, ("z", "core"), 0, 0), axis=0)
     composites = (sums[:, :256] / jnp.maximum(sums[:, 256:257], 1.0)).astype(BF16)
 

time: 119 us -> 119 us (level)
  no operation moved by 1% of the time
where the time goes in v8:
time: 119 us
  blocking collectives  87.6 us (74%)
  Pallas kernels  16 us (13%)
  starting transfers between devices  7.75 us (7%)
  waiting for transfers between devices  4.79 us (4%)
    all_to_all x2, blocking collectives, merge(): parts = lax.all_to_all(spread(half, 8), 'z', 0, 0)  30.1 us
    all_to_all x1, blocking collectives, body(): own = lax.all_to_all(eight, 'z', 0, 0)  19.4 us
    pallas_call x7, Pallas kernels, call(): pl.pallas_call(kernel, out_shape=tuple((jax.ShapeDtypeStruct(s, d) for s,...  16 us
    all_to_all x1, blocking collectives, body(): mine = jnp.sum(lax.all_to_all(partial, 'grid', 0, 0), axis=0)  14.7 us
    all_to_all x1, blocking collectives, body(): sums = jnp.sum(lax.all_to_all(terms, ('z', 'core'), 0, 0), axis=0)  13.2 us
    all_to_all x1, blocking collectives, body(): pcs = lax.all_to_all(spread(mine, 16), 'grid', 0, 0)  10.2 us
    ppermute x2, starting transfers between devices, merge(): half = keep + lax.ppermute(send, 'core', SWAP)  3.39 us
    ppermute x1, starting transfers between devices, body(): other = lax.ppermute(own, 'core', SWAP)  2.46 us
  transfers between devices with their start and end apart: 5, of which 5 were waited for; matrix products, arithmetic and copies ran while one was open for 0% of the time, Pallas kernels for 0%

profile of v8, /device:TPU:1, one launch (start us, length us, event | category | flops | bytes accessed | tf_op | source)
XLA Modules:
  0.0 118.5 jit_solution(10270157497270886219)
XLA Ops:
  0.6 0.0 copy-start.5
  0.6 0.7 copy-done.5
  1.4 0.0 copy-start.2
  1.4 0.0 copy-start.3
  1.4 0.0 copy-start.4
  1.4 19.4 %all_to_all.30.own_ref = bf16[8,64,256]{2,1,0:T(8,128)(2,1)S(1)} all-to-all(bf16[8,64,256]{2,1,0:T(8,128)(2,1)S(1)} %shard_map.92), channel_id=1, replica_groups=mesh['grid'=16,'z'=8,'core'=2] {'z'}, dimensions={0} | all-to-all | bytes 524288 | tf_op jit(solution)/shard_map/all_to_all | solution.py:357
  20.9 2.5 %collective-permute-start = (bf16[8,64,256]{2,1,0:T(8,128)(2,1)S(1)}, bf16[8,64,256]{2,1,0:T(8,128)(2,1)S(1)}, u32[]{:S(2)}, u32[]{:S(2)}) collective-permute-start(bf16[8,64,256]{2,1,0:T(8,128)(2,1)S(1)} %all_to_all.30.own_ref), channel_id=1, source_target_pairs={{0,1},{1,0},{2,3},{3,2},{4,5},{5,4},{6,7},{7,6},{8,9},{9,8},{10,11... | collective-permute-start | bytes 786440 | tf_op jit(solution)/shard_map/ppermute | solution.py:358
  23.4 1.2 collective-permute-done.other_ref
  24.5 0.0 copy-done
  24.5 2.5 %shard_map.93 = f32[16,8,512]{2,1,0:T(8,128)S(1)} custom-call(bf16[8,64,256]{2,1,0:T(8,128)(2,1)S(1)} %all_to_all.30.own_ref, bf16[8,64,256]{2,1,0:T(8,128)(2,1)S(1)} %collective-permute-done.other_ref, bf16[1024,4096]{1,0:T(8,128)(2,1)S(1)} %copy-done), custom_call_target="tpu_custom_call" | custom-call | tf_op jit(solution)/shard_map/pallas_call | solution.py:27
  27.0 14.7 %all_to_all.31 = f32[16,8,512]{2,1,0:T(8,128)S(1)} all-to-all(f32[16,8,512]{2,1,0:T(8,128)S(1)} %shard_map.93), channel_id=1, replica_groups=mesh['grid'=16,'z'=8,'core'=2] {'grid'}, dimensions={0} | all-to-all | bytes 524288 | tf_op jit(solution)/shard_map/all_to_all | solution.py:361
  41.8 10.2 %all_to_all.32.pcs_ref = f32[16,8,512]{2,1,0:T(8,128)S(1)} all-to-all(f32[16,8,512]{2,1,0:T(8,128)S(1)} %broadcast_in_dim.6), channel_id=1, replica_groups=mesh['grid'=16,'z'=8,'core'=2] {'grid'}, dimensions={0} | all-to-all | bytes 524288 | tf_op jit(solution)/shard_map/all_to_all | solution.py:362
  52.0 0.0 copy-done.2
  52.0 0.0 copy-done.4
  52.0 2.1 %shard_map.94 = (f32[72,128]{1,0:T(8,128)S(1)}, f32[72,128]{1,0:T(8,128)S(1)}, f32[8,128]{1,0:T(8,128)S(1)}) custom-call(f32[16,8,512]{2,1,0:T(8,128)S(1)} %all_to_all.32.pcs_ref, f32[8,64]{1,0:T(8,128)S(1)} %copy-done.2, f32[8,64]{1,0:T(8,128)S(1)} %copy-done.3, f32[8]{0:T(128)S(1)} %copy-done.4), custom_call_target="tpu_custom_call" | custom-call | tf_op jit(solution)/shard_map/pallas_call | solution.py:27
  54.1 3.0 %collective-permute-start.1 = (f32[72,128]{1,0:T(8,128)S(1)}, f32[72,128]{1,0:T(8,128)S(1)}, u32[]{:S(2)}, u32[]{:S(2)}) collective-permute-start(f32[72,128]{1,0:T(8,128)S(1)} %get-tuple-element.17), channel_id=1, source_target_pairs={{0,1},{1,0},{2,3},{3,2},{4,5},{5,4},{6,7},{7,6},{8,9},{9,8},{10,11... | collective-permute-start | bytes 110600 | tf_op jit(solution)/shard_map/ppermute | solution.py:346
  57.1 0.9 collective-permute-done.1
  58.0 15.0 %all_to_all.33.parts_ref = f32[8,72,128]{2,1,0:T(8,128)S(1)} all-to-all(f32[8,72,128]{2,1,0:T(8,128)S(1)} %broadcast_in_dim.7), channel_id=1, replica_groups=mesh['grid'=16,'z'=8,'core'=2] {'z'}, dimensions={0} | all-to-all | bytes 589824 | tf_op jit(solution)/shard_map/all_to_all | solution.py:347
  73.0 2.8 %shard_map.95.keep_ref = f32[136,128]{1,0:T(8,128)S(1)} custom-call(f32[8,72,128]{2,1,0:T(8,128)S(1)} %all_to_all.33.parts_ref, f32[8,128]{1,0:T(8,128)S(1)} %get-tuple-element.18.shift_ref), custom_call_target="tpu_custom_call" | custom-call | flops 199999995904 | tf_op jit(solution)/shard_map/pallas_call | solution.py:27
  75.9 0.9 collective-permute-start.2
  76.8 0.9 collective-permute-done.2.got_ref
  77.7 2.4 %shard_map.96 = (f32[72,128]{1,0:T(8,128)S(1)}, f32[72,128]{1,0:T(8,128)S(1)}, f32[8,128]{1,0:T(8,128)S(1)}) custom-call(f32[16,8,512]{2,1,0:T(8,128)S(1)} %all_to_all.32.pcs_ref, f32[136,128]{1,0:T(8,128)S(1)} %shard_map.95.keep_ref, f32[136,128]{1,0:T(8,128)S(1)} %collective-permute-done.2.got_ref), custom_call_target="tpu_custom_call" | custom-call | tf_op jit(solution)/shard_map/pallas_call | solution.py:27
  80.1 0.4 collective-permute-start.3
  80.5 0.9 collective-permute-done.3
  81.4 15.0 %all_to_all.34.parts_ref = f32[8,72,128]{2,1,0:T(8,128)S(1)} all-to-all(f32[8,72,128]{2,1,0:T(8,128)S(1)} %broadcast_in_dim.8), channel_id=1, replica_groups=mesh['grid'=16,'z'=8,'core'=2] {'z'}, dimensions={0} | all-to-all | bytes 589824 | tf_op jit(solution)/shard_map/all_to_all | solution.py:347
  96.5 2.8 %shard_map.97.keep_ref = f32[264,128]{1,0:T(8,128)S(1)} custom-call(f32[8,72,128]{2,1,0:T(8,128)S(1)} %all_to_all.34.parts_ref, f32[8,128]{1,0:T(8,128)S(1)} %get-tuple-element.21.shift_ref), custom_call_target="tpu_custom_call" | custom-call | flops 199999995904 | tf_op jit(solution)/shard_map/pallas_call | solution.py:27
  99.3 1.0 collective-permute-start.4
  100.3 1.0 collective-permute-done.4.got_ref
  101.3 3.3 %shard_map.98 = (f32[8,1024]{1,0:T(8,128)}, f32[16,8,384]{2,1,0:T(8,128)S(1)}, f32[8,64]{1,0:T(8,128)}, f32[8,64,64]{2,1,0:T(8,128)}, f32[8]{0:T(128)}) custom-call(f32[16,8,512]{2,1,0:T(8,128)S(1)} %all_to_all.32.pcs_ref, f32[264,128]{1,0:T(8,128)S(1)} %shard_map.97.keep_ref, f32[264,128]{1,0:T(8,128)S(1)} %collective-permute-done.4.got_ref, ...), custom_call_target="tpu_custom_call" | custom-call | tf_op jit(solution)/shard_map/pallas_call | solution.py:27
  104.6 13.2 %all_to_all.35 = f32[16,8,384]{2,1,0:T(8,128)S(1)} all-to-all(f32[16,8,384]{2,1,0:T(8,128)S(1)} %get-tuple-element.26), channel_id=1, replica_groups=mesh['grid'=16,'z'=8,'core'=2] {'z','core'}, dimensions={0} | all-to-all | bytes 393216 | tf_op jit(solution)/shard_map/all_to_all | solution.py:373
  117.8 0.1 fusion.1
  117.9 0.7 fusion
  (12 shorter events, 0.1 us)
Async XLA Ops:
  0.6 0.8 copy-start.5
  1.4 23.1 %copy-start = (bf16[1024,4096]{1,0:T(8,128)(2,1)S(1)}, bf16[1024,4096]{1,0:T(8,128)(2,1)}, u32[]{:S(2)}) copy-start(bf16[1024,4096]{1,0:T(8,128)(2,1)} %fields_ref.3) | copy-start | bytes 25165828
  1.4 50.6 %copy-start.2 = (f32[8,64]{1,0:T(8,128)S(1)}, f32[8,64]{1,0:T(8,128)}, u32[]{:S(2)}) copy-start(f32[8,64]{1,0:T(8,128)} %means_ref.1) | copy-start | bytes 6148
  1.4 50.6 %copy-start.3 = (f32[8,64]{1,0:T(8,128)S(1)}, f32[8,64]{1,0:T(8,128)}, u32[]{:S(2)}) copy-start(f32[8,64]{1,0:T(8,128)} %variances_ref.1) | copy-start | bytes 6148
  1.4 50.6 %copy-start.4 = (f32[8]{0:T(128)S(1)}, f32[8]{0:T(128)}, u32[]{:S(2)}) copy-start(f32[8]{0:T(128)} %mixing_ref.1) | copy-start | bytes 100
  20.9 3.6 %collective-permute-start = (bf16[8,64,256]{2,1,0:T(8,128)(2,1)S(1)}, bf16[8,64,256]{2,1,0:T(8,128)(2,1)S(1)}, u32[]{:S(2)}, u32[]{:S(2)}) collective-permute-start(bf16[8,64,256]{2,1,0:T(8,128)(2,1)S(1)} %all_to_all.30.own_ref), channel_id=1, source_target_pairs={{0,1},{1,0},{2,3},{3,2},{4,5},{5,4},{6,7},{7,6},{8,9},{9,8},{10,11... | collective-permute-start | bytes 786440 | tf_op jit(solution)/shard_map/ppermute | solution.py:358
  54.1 3.8 %collective-permute-start.1 = (f32[72,128]{1,0:T(8,128)S(1)}, f32[72,128]{1,0:T(8,128)S(1)}, u32[]{:S(2)}, u32[]{:S(2)}) collective-permute-start(f32[72,128]{1,0:T(8,128)S(1)} %get-tuple-element.17), channel_id=1, source_target_pairs={{0,1},{1,0},{2,3},{3,2},{4,5},{5,4},{6,7},{7,6},{8,9},{9,8},{10,11... | collective-permute-start | bytes 110600 | tf_op jit(solution)/shard_map/ppermute | solution.py:346
  75.9 1.8 %collective-permute-start.2 = (f32[136,128]{1,0:T(8,128)S(1)}, f32[136,128]{1,0:T(8,128)S(1)}, u32[]{:S(2)}, u32[]{:S(2)}) collective-permute-start(f32[136,128]{1,0:T(8,128)S(1)} %shard_map.95.keep_ref), channel_id=1, source_target_pairs={{0,1},{1,0},{2,3},{3,2},{4,5},{5,4},{6,7},{7,6},{8,9},{9,8},{10,11... | collective-permute-start | bytes 208904 | tf_op jit(solution)/shard_map/ppermute | solution.py:349
  80.1 1.3 %collective-permute-start.3 = (f32[72,128]{1,0:T(8,128)S(1)}, f32[72,128]{1,0:T(8,128)S(1)}, u32[]{:S(2)}, u32[]{:S(2)}) collective-permute-start(f32[72,128]{1,0:T(8,128)S(1)} %get-tuple-element.20), channel_id=1, source_target_pairs={{0,1},{1,0},{2,3},{3,2},{4,5},{5,4},{6,7},{7,6},{8,9},{9,8},{10,11... | collective-permute-start | bytes 110600 | tf_op jit(solution)/shard_map/ppermute | solution.py:346
  96.5 4.8 %copy-start.1 = (bf16[1024,4096]{1,0:T(8,128)(2,1)S(1)}, bf16[1024,4096]{1,0:T(8,128)(2,1)}, u32[]{:S(2)}) copy-start(bf16[1024,4096]{1,0:T(8,128)(2,1)} %fields_ref.3) | copy-start | bytes 25165828
  99.3 1.9 %collective-permute-start.4 = (f32[264,128]{1,0:T(8,128)S(1)}, f32[264,128]{1,0:T(8,128)S(1)}, u32[]{:S(2)}, u32[]{:S(2)}) collective-permute-start(f32[264,128]{1,0:T(8,128)S(1)} %shard_map.97.keep_ref), channel_id=1, source_target_pairs={{0,1},{1,0},{2,3},{3,2},{4,5},{5,4},{6,7},{7,6},{8,9},{9,8},{10,11... | collective-permute-start | bytes 405512 | tf_op jit(solution)/shard_map/ppermute | solution.py:349

commit v9 on v8

--- a/solution.py
+++ b/solution.py
@@ -319,7 +319,7 @@
     moments(core, centred, terms, resp, out_keep_ref, out_send_ref)
 
 
-def last_kernel(pcs_ref, keep_ref, got_ref, fields_ref, member_ref, terms_ref, means_ref, covs_ref, weights_ref):
+def last_kernel(pcs_ref, keep_ref, got_ref, fields_ref, member_ref, stay_ref, send_ref, means_ref, covs_ref, weights_ref):
     core = lax.axis_index("core")
     halves = halves_of(core, keep_ref, got_ref)
     for r in range(R):
@@ -333,9 +333,12 @@
     means_ref[...] = means
     count = jnp.broadcast_to(jnp.sum(member, axis=1, keepdims=True), (R, 128))
     rounded = member.astype(BF16)
-    for j in range(16):
-        terms_ref[j, :, 0:256] = jnp.dot(rounded, fields_ref[:, 256 * j:256 * j + 256], preferred_element_type=F32)
-        terms_ref[j, :, 256:384] = count
+    for z in range(8):
+        both = jnp.dot(rounded, fields_ref[:, 512 * z:512 * z + 512], preferred_element_type=F32)
+        stay_ref[z, :, 0:256] = by_core(core, both[:, :256], both[:, 256:])
+        send_ref[z, :, 0:256] = by_core(core, both[:, 256:], both[:, :256])
+        stay_ref[z, :, 256:384] = count
+        send_ref[z, :, 256:384] = count
 
 
 def spread(x, n):
@@ -366,11 +369,11 @@
     block, got = merge(keep, send, shift, INFO + 8)
     keep, send, shift = call(middle_kernel, pack, [pcs, block, got])
     block, got = merge(keep, send, shift, INFO + 8 + 2 * K)
-    member, terms, means, covs, weights = call(
+    member, stay, send, means, covs, weights = call(
         last_kernel,
-        [((R, days), F32), ((16, R, 384), F32), ((R, K), F32), ((R, K, K), F32), ((R,), F32)],
+        [((R, days), F32), ((8, R, 384), F32), ((8, R, 384), F32), ((R, K), F32), ((R, K, K), F32), ((R,), F32)],
         [pcs, block, got, anomalies], limit=SMALL, scalar_outs=1)
-    sums = jnp.sum(lax.all_to_all(terms, ("z", "core"), 0, 0), axis=0)
+    sums = jnp.sum(lax.all_to_all(stay + lax.ppermute(send, "core", SWAP), "z", 0, 0), axis=0)
     composites = (sums[:, :256] / jnp.maximum(sums[:, 256:257], 1.0)).astype(BF16)
 
     return (means, covs, weights, member, composites)

time: 119 us -> 117 us (0.983)
  blocking collectives: 87.6 us -> 84.4 us
    all_to_all x1, blocking collectives: 13.2 us -> 10 us  [body(): lax.all_to_all(stay + lax.ppermute(send, 'core', SWAP), 'z', 0, 0)]
  transfers between devices with their start and end apart: 5 -> 6, of which waited for: 5 -> 6; matrix products, arithmetic and copies ran while one was open for 0% -> 0% of each run, Pallas kernels for 0% -> 0%
where the time goes in v9:
time: 117 us
  blocking collectives  84.4 us (72%)
  Pallas kernels  16 us (14%)
  starting transfers between devices  8.2 us (7%)
  waiting for transfers between devices  5.74 us (5%)
    all_to_all x2, blocking collectives, merge(): parts = lax.all_to_all(spread(half, 8), 'z', 0, 0)  30.1 us
    all_to_all x1, blocking collectives, body(): own = lax.all_to_all(eight, 'z', 0, 0)  19.4 us
    pallas_call x7, Pallas kernels, call(): pl.pallas_call(kernel, out_shape=tuple((jax.ShapeDtypeStruct(s, d) for s,...  16 us
    all_to_all x1, blocking collectives, body(): mine = jnp.sum(lax.all_to_all(partial, 'grid', 0, 0), axis=0)  14.7 us
    all_to_all x1, blocking collectives, body(): pcs = lax.all_to_all(spread(mine, 16), 'grid', 0, 0)  10.2 us
    all_to_all x1, blocking collectives, body(): lax.all_to_all(stay + lax.ppermute(send, 'core', SWAP), 'z', 0, 0)  10 us
    ppermute x2, starting transfers between devices, merge(): half = keep + lax.ppermute(send, 'core', SWAP)  3.39 us
    ppermute x1, starting transfers between devices, body(): other = lax.ppermute(own, 'core', SWAP)  2.46 us
  transfers between devices with their start and end apart: 6, of which 6 were waited for; matrix products, arithmetic and copies ran while one was open for 0% of the time, Pallas kernels for 0%

profile of v9, /device:TPU:1, one launch (start us, length us, event | category | flops | bytes accessed | tf_op | source)
XLA Modules:
  0.0 116.8 jit_solution(15083012841940877144)
XLA Ops:
  0.6 0.0 copy-start.5
  0.6 0.7 copy-done.5
  1.4 0.0 copy-start.2
  1.4 0.0 copy-start.3
  1.4 0.0 copy-start.4
  1.4 19.4 %all_to_all.30.own_ref = bf16[8,64,256]{2,1,0:T(8,128)(2,1)S(1)} all-to-all(bf16[8,64,256]{2,1,0:T(8,128)(2,1)S(1)} %shard_map.92), channel_id=1, replica_groups=mesh['grid'=16,'z'=8,'core'=2] {'z'}, dimensions={0} | all-to-all | bytes 524288 | tf_op jit(solution)/shard_map/all_to_all | solution.py:360
  20.9 2.5 %collective-permute-start = (bf16[8,64,256]{2,1,0:T(8,128)(2,1)S(1)}, bf16[8,64,256]{2,1,0:T(8,128)(2,1)S(1)}, u32[]{:S(2)}, u32[]{:S(2)}) collective-permute-start(bf16[8,64,256]{2,1,0:T(8,128)(2,1)S(1)} %all_to_all.30.own_ref), channel_id=1, source_target_pairs={{0,1},{1,0},{2,3},{3,2},{4,5},{5,4},{6,7},{7,6},{8,9},{9,8},{10,11... | collective-permute-start | bytes 786440 | tf_op jit(solution)/shard_map/ppermute | solution.py:361
  23.4 1.2 collective-permute-done.other_ref
  24.5 0.0 copy-done
  24.5 2.5 %shard_map.93 = f32[16,8,512]{2,1,0:T(8,128)S(1)} custom-call(bf16[8,64,256]{2,1,0:T(8,128)(2,1)S(1)} %all_to_all.30.own_ref, bf16[8,64,256]{2,1,0:T(8,128)(2,1)S(1)} %collective-permute-done.other_ref, bf16[1024,4096]{1,0:T(8,128)(2,1)S(1)} %copy-done), custom_call_target="tpu_custom_call" | custom-call | tf_op jit(solution)/shard_map/pallas_call | solution.py:27
  27.0 14.7 %all_to_all.31 = f32[16,8,512]{2,1,0:T(8,128)S(1)} all-to-all(f32[16,8,512]{2,1,0:T(8,128)S(1)} %shard_map.93), channel_id=1, replica_groups=mesh['grid'=16,'z'=8,'core'=2] {'grid'}, dimensions={0} | all-to-all | bytes 524288 | tf_op jit(solution)/shard_map/all_to_all | solution.py:364
  41.8 10.2 %all_to_all.32.pcs_ref = f32[16,8,512]{2,1,0:T(8,128)S(1)} all-to-all(f32[16,8,512]{2,1,0:T(8,128)S(1)} %broadcast_in_dim.6), channel_id=1, replica_groups=mesh['grid'=16,'z'=8,'core'=2] {'grid'}, dimensions={0} | all-to-all | bytes 524288 | tf_op jit(solution)/shard_map/all_to_all | solution.py:365
  52.0 2.1 %shard_map.94 = (f32[72,128]{1,0:T(8,128)S(1)}, f32[72,128]{1,0:T(8,128)S(1)}, f32[8,128]{1,0:T(8,128)S(1)}) custom-call(f32[16,8,512]{2,1,0:T(8,128)S(1)} %all_to_all.32.pcs_ref, f32[8,64]{1,0:T(8,128)S(1)} %copy-done.2, f32[8,64]{1,0:T(8,128)S(1)} %copy-done.3, f32[8]{0:T(128)S(1)} %copy-done.4), custom_call_target="tpu_custom_call" | custom-call | tf_op jit(solution)/shard_map/pallas_call | solution.py:27
  54.1 3.0 %collective-permute-start.1 = (f32[72,128]{1,0:T(8,128)S(1)}, f32[72,128]{1,0:T(8,128)S(1)}, u32[]{:S(2)}, u32[]{:S(2)}) collective-permute-start(f32[72,128]{1,0:T(8,128)S(1)} %get-tuple-element.18), channel_id=1, source_target_pairs={{0,1},{1,0},{2,3},{3,2},{4,5},{5,4},{6,7},{7,6},{8,9},{9,8},{10,11... | collective-permute-start | bytes 110600 | tf_op jit(solution)/shard_map/ppermute | solution.py:349
  57.1 0.9 collective-permute-done.1
  58.0 15.0 %all_to_all.33.parts_ref = f32[8,72,128]{2,1,0:T(8,128)S(1)} all-to-all(f32[8,72,128]{2,1,0:T(8,128)S(1)} %broadcast_in_dim.7), channel_id=1, replica_groups=mesh['grid'=16,'z'=8,'core'=2] {'z'}, dimensions={0} | all-to-all | bytes 589824 | tf_op jit(solution)/shard_map/all_to_all | solution.py:350
  73.0 2.8 %shard_map.95.keep_ref = f32[136,128]{1,0:T(8,128)S(1)} custom-call(f32[8,72,128]{2,1,0:T(8,128)S(1)} %all_to_all.33.parts_ref, f32[8,128]{1,0:T(8,128)S(1)} %get-tuple-element.19.shift_ref), custom_call_target="tpu_custom_call" | custom-call | flops 199999995904 | tf_op jit(solution)/shard_map/pallas_call | solution.py:27
  75.9 0.9 collective-permute-start.2
  76.8 0.9 collective-permute-done.2.got_ref
  77.7 2.4 %shard_map.96 = (f32[72,128]{1,0:T(8,128)S(1)}, f32[72,128]{1,0:T(8,128)S(1)}, f32[8,128]{1,0:T(8,128)S(1)}) custom-call(f32[16,8,512]{2,1,0:T(8,128)S(1)} %all_to_all.32.pcs_ref, f32[136,128]{1,0:T(8,128)S(1)} %shard_map.95.keep_ref, f32[136,128]{1,0:T(8,128)S(1)} %collective-permute-done.2.got_ref), custom_call_target="tpu_custom_call" | custom-call | tf_op jit(solution)/shard_map/pallas_call | solution.py:27
  80.1 0.4 collective-permute-start.3
  80.5 0.9 collective-permute-done.3
  81.4 15.0 %all_to_all.34.parts_ref = f32[8,72,128]{2,1,0:T(8,128)S(1)} all-to-all(f32[8,72,128]{2,1,0:T(8,128)S(1)} %broadcast_in_dim.8), channel_id=1, replica_groups=mesh['grid'=16,'z'=8,'core'=2] {'z'}, dimensions={0} | all-to-all | bytes 589824 | tf_op jit(solution)/shard_map/all_to_all | solution.py:350
  96.5 2.8 %shard_map.97.keep_ref = f32[264,128]{1,0:T(8,128)S(1)} custom-call(f32[8,72,128]{2,1,0:T(8,128)S(1)} %all_to_all.34.parts_ref, f32[8,128]{1,0:T(8,128)S(1)} %get-tuple-element.22.shift_ref), custom_call_target="tpu_custom_call" | custom-call | flops 199999995904 | tf_op jit(solution)/shard_map/pallas_call | solution.py:27
  99.3 1.0 collective-permute-start.4
  100.3 1.0 collective-permute-done.4.got_ref
  101.3 3.3 %shard_map.98 = (f32[8,1024]{1,0:T(8,128)}, f32[8,8,384]{2,1,0:T(8,128)S(1)}, f32[8,8,384]{2,1,0:T(8,128)S(1)}, f32[8,64]{1,0:T(8,128)}, f32[8,64,64]{2,1,0:T(8,128)}, /*index=5*/f32[8]{0:T(128)}) custom-call(f32[16,8,512]{2,1,0:T(8,128)S(1)} %all_to_all.32.pcs_ref, f32[264,128]{1,0:T(8,128)S(1)} %shard_map.97.keep_ref, ...), custom_call_target="tpu_custom_call" | custom-call | tf_op jit(solution)/shard_map/pallas_call | solution.py:27
  104.6 0.4 collective-permute-start.5
  105.0 0.9 collective-permute-done.5
  106.0 10.0 %all_to_all.35 = f32[8,8,384]{2,1,0:T(8,128)S(1)} all-to-all(f32[8,8,384]{2,1,0:T(8,128)S(1)} %add.11), channel_id=1, replica_groups=mesh['grid'=16,'z'=8,'core'=2] {'z'}, dimensions={0} | all-to-all | bytes 196608 | tf_op jit(solution)/shard_map/all_to_all | solution.py:376
  116.0 0.1 fusion.1
  116.1 0.7 fusion
  (15 shorter events, 0.1 us)
Async XLA Ops:
  0.6 0.8 copy-start.5
  1.4 23.1 %copy-start = (bf16[1024,4096]{1,0:T(8,128)(2,1)S(1)}, bf16[1024,4096]{1,0:T(8,128)(2,1)}, u32[]{:S(2)}) copy-start(bf16[1024,4096]{1,0:T(8,128)(2,1)} %fields_ref.3) | copy-start | bytes 25165828
  1.4 50.6 %copy-start.2 = (f32[8,64]{1,0:T(8,128)S(1)}, f32[8,64]{1,0:T(8,128)}, u32[]{:S(2)}) copy-start(f32[8,64]{1,0:T(8,128)} %means_ref.1) | copy-start | bytes 6148
  1.4 50.6 %copy-start.3 = (f32[8,64]{1,0:T(8,128)S(1)}, f32[8,64]{1,0:T(8,128)}, u32[]{:S(2)}) copy-start(f32[8,64]{1,0:T(8,128)} %variances_ref.1) | copy-start | bytes 6148
  1.4 50.6 %copy-start.4 = (f32[8]{0:T(128)S(1)}, f32[8]{0:T(128)}, u32[]{:S(2)}) copy-start(f32[8]{0:T(128)} %mixing_ref.1) | copy-start | bytes 100
  20.9 3.6 %collective-permute-start = (bf16[8,64,256]{2,1,0:T(8,128)(2,1)S(1)}, bf16[8,64,256]{2,1,0:T(8,128)(2,1)S(1)}, u32[]{:S(2)}, u32[]{:S(2)}) collective-permute-start(bf16[8,64,256]{2,1,0:T(8,128)(2,1)S(1)} %all_to_all.30.own_ref), channel_id=1, source_target_pairs={{0,1},{1,0},{2,3},{3,2},{4,5},{5,4},{6,7},{7,6},{8,9},{9,8},{10,11... | collective-permute-start | bytes 786440 | tf_op jit(solution)/shard_map/ppermute | solution.py:361
  54.1 3.8 %collective-permute-start.1 = (f32[72,128]{1,0:T(8,128)S(1)}, f32[72,128]{1,0:T(8,128)S(1)}, u32[]{:S(2)}, u32[]{:S(2)}) collective-permute-start(f32[72,128]{1,0:T(8,128)S(1)} %get-tuple-element.18), channel_id=1, source_target_pairs={{0,1},{1,0},{2,3},{3,2},{4,5},{5,4},{6,7},{7,6},{8,9},{9,8},{10,11... | collective-permute-start | bytes 110600 | tf_op jit(solution)/shard_map/ppermute | solution.py:349
  75.9 1.8 %collective-permute-start.2 = (f32[136,128]{1,0:T(8,128)S(1)}, f32[136,128]{1,0:T(8,128)S(1)}, u32[]{:S(2)}, u32[]{:S(2)}) collective-permute-start(f32[136,128]{1,0:T(8,128)S(1)} %shard_map.95.keep_ref), channel_id=1, source_target_pairs={{0,1},{1,0},{2,3},{3,2},{4,5},{5,4},{6,7},{7,6},{8,9},{9,8},{10,11... | collective-permute-start | bytes 208904 | tf_op jit(solution)/shard_map/ppermute | solution.py:352
  80.1 1.3 %collective-permute-start.3 = (f32[72,128]{1,0:T(8,128)S(1)}, f32[72,128]{1,0:T(8,128)S(1)}, u32[]{:S(2)}, u32[]{:S(2)}) collective-permute-start(f32[72,128]{1,0:T(8,128)S(1)} %get-tuple-element.21), channel_id=1, source_target_pairs={{0,1},{1,0},{2,3},{3,2},{4,5},{5,4},{6,7},{7,6},{8,9},{9,8},{10,11... | collective-permute-start | bytes 110600 | tf_op jit(solution)/shard_map/ppermute | solution.py:349
  96.5 4.8 %copy-start.1 = (bf16[1024,4096]{1,0:T(8,128)(2,1)S(1)}, bf16[1024,4096]{1,0:T(8,128)(2,1)}, u32[]{:S(2)}) copy-start(bf16[1024,4096]{1,0:T(8,128)(2,1)} %fields_ref.3) | copy-start | bytes 25165828
  99.3 1.9 %collective-permute-start.4 = (f32[264,128]{1,0:T(8,128)S(1)}, f32[264,128]{1,0:T(8,128)S(1)}, u32[]{:S(2)}, u32[]{:S(2)}) collective-permute-start(f32[264,128]{1,0:T(8,128)S(1)} %shard_map.97.keep_ref), channel_id=1, source_target_pairs={{0,1},{1,0},{2,3},{3,2},{4,5},{5,4},{6,7},{7,6},{8,9},{9,8},{10,11... | collective-permute-start | bytes 405512 | tf_op jit(solution)/shard_map/ppermute | solution.py:352
  104.6 1.4 %collective-permute-start.5 = (f32[8,8,384]{2,1,0:T(8,128)S(1)}, f32[8,8,384]{2,1,0:T(8,128)S(1)}, u32[]{:S(2)}, u32[]{:S(2)}) collective-permute-start(f32[8,8,384]{2,1,0:T(8,128)S(1)} %get-tuple-element.28), channel_id=1, source_target_pairs={{0,1},{1,0},{2,3},{3,2},{4,5},{5,4},{6,7},{7,6},{8,9},{9,8},{10,11... | collective-permute-start | bytes 294920 | tf_op jit(solution)/shard_map/ppermute | solution.py:376
